TPU v7x, 512 devices: a whole 4x4x16 slice. The times are simulated.
512 devices in a mesh: expert: 8 (over x_lo, y), shard: 64 (over x_hi, z, core).
Axes of the slice: x: 4 (x_hi: 2, x_lo: 2; x = x_hi * 2 + x_lo), y: 4, z: 16, core: 2. Of those that a mesh axis runs over, the one named last changes fastest.
Arguments:
- fast_weights: bfloat16 [8, 64, 1, 64, 14336], P('expert', 'shard'), may hold values from -0.25 to 0.25
- slow_weights: float32 [8, 1, 64, 14336], P('expert', None, None, 'shard'), may hold values from -0.09375 to 0.09375
- step_counts: int32 [8, 64], P('expert', 'shard'), may hold values from 1 to 16
- token_counts: int32 [8, 64], P('expert', 'shard'), may hold values from 100 to 897
Outputs:
- new_slow: float32 [8, 1, 64, 14336], P('expert', None, None, 'shard')
- reset_fast: bfloat16 [8, 1, 64, 14336], P('expert')
All inputs are finite; a program needn't handle non-finite values.
Results may differ from a plain program's by a relative error of at most 0.001.
Values may be sent and summed in bfloat16 or wider, within the bound.
No kernel may reach another device: no remote copies, remote signals or barrier semaphores. Data moves between devices by JAX's collectives and lax.ppermute only.
A program may use at most 64 MiB of HBM per device.

v0:
```python
import jax
import jax.numpy as jnp
from jax import lax
from jax.sharding import Mesh
from jax.sharding import PartitionSpec as P

SHARD = ("shard_0", "shard_1", "shard_2")


outer_rate = 0.7


def copy_for_each(shard, axis):
    copies = jnp.broadcast_to(shard, (lax.axis_size(axis), *shard.shape))
    return lax.all_to_all(copies, axis, split_axis=0, concat_axis=0, tiled=True)


def over_copies(shard, axis):
    return copy_for_each(shard, axis).sum(axis=0)


def in_one(arrays, axis):
    ends = [0]
    for a in arrays:
        ends.append(ends[-1] + a.size)
    total = over_copies(jnp.concatenate([a.ravel() for a in arrays]), axis)
    return tuple((total[b:e].reshape(a.shape) for a, b, e in zip(arrays, ends, ends[1:])))


def own_block(pieces, axes, turns):
    shape = [lax.axis_size(a) for a in axes]
    pieces = pieces.reshape(*shape, *pieces.shape[1:])
    pieces = pieces.transpose(*turns, *range(len(axes), pieces.ndim))
    pieces = pieces.reshape(-1, *pieces.shape[len(axes) :])
    for k in turns:
        pieces = lax.psum_scatter(pieces, axes[k], scatter_dimension=0, tiled=True)
    return pieces[0]


def cut_along(shard, dim, size):
    shape = shard.shape
    pieces = shard.reshape(*shape[:dim], size, shape[dim] // size, *shape[dim + 1 :])
    return jnp.moveaxis(pieces, dim, 0)


def scatter_axes(shard, axes, turns, dim):
    size = lax.axis_size(axes)
    return own_block(cut_along(shard, dim, size), axes, turns)


def laid_out(pieces, dim):
    pieces = jnp.moveaxis(pieces, 0, dim)
    shape = pieces.shape
    return pieces.reshape(*shape[:dim], shape[dim] * shape[dim + 1], *shape[dim + 2 :])


def stacked_from(shard, axes, turns):
    pieces = shard[None]
    for k in turns:
        pieces = lax.all_gather(pieces, axes[k], axis=0, tiled=True)
    held = [lax.axis_size(axes[k]) for k in reversed(turns)]
    pieces = pieces.reshape(*held, *shard.shape)
    turned = sorted(range(len(turns)), key=lambda place: turns[len(turns) - 1 - place])
    return pieces.transpose(*turned, *range(len(turns), pieces.ndim)).reshape(-1, *shard.shape)


def gather_axes(shard, axes, turns, dim):
    return laid_out(stacked_from(shard, axes, turns), dim)


def shards(fast_weights, slow_weights, step_counts, token_counts):
    tokens = token_counts.astype(jnp.float32)[0, 0]
    steps = step_counts.astype(jnp.float32)[0, 0]
    share = tokens / steps
    work = tokens * steps
    groups = lax.axis_size("expert")
    tok_e, work_e, qsum = in_one((tokens, work, share), SHARD)
    total = over_copies(tok_e, "expert")
    rate = outer_rate * groups * work_e / (tok_e * total)
    weighted = share * fast_weights[0, 0].astype(jnp.float32)
    slow_part = slow_weights[0]
    mixed = scatter_axes(weighted, SHARD, (2, 1, 0), 2)
    new_slow = slow_part + rate * (mixed - qsum * slow_part)
    reset = gather_axes(new_slow.astype(jnp.bfloat16), SHARD, (0, 1, 2), 2)
    return (new_slow[None], reset[None])


def solution(mesh):
    torus = Mesh(
        mesh.devices.reshape(mesh.shape["expert"], 2, 16, 2),
        ("expert", "shard_0", "shard_1", "shard_2"),
    )
    placed = (
        P("expert", SHARD, None, None, None),
        P("expert", None, None, SHARD),
        P("expert", SHARD),
        P("expert", SHARD),
    )
    return jax.shard_map(
        shards,
        mesh=torus,
        in_specs=placed,
        out_specs=(P("expert", None, None, SHARD), P("expert", None, None, None)),
        check_vma=False,
    )
```

profile of v0, /device:TPU:1, one launch (start us, length us, event | category | flops | bytes accessed | tf_op | source)
XLA Modules:
  0.0 242.1 jit_solution(16552391406660231986)
XLA Ops:
  7.2 0.0 reduce-scatter.4.cloned.1.call-start
  8.5 3.6 %convert_multiply_fusion = f32[1,1,1,64,14336]{4,3,2,1,0:T(8,128)} fusion(bf16[1,1,1,64,14336]{4,3,2,1,0:T(8,128)(2,1)} %param.4, f32[]{:T(128)} %bitcast.6), kind=kLoop, calls=%fused_computation | loop fusion | flops 1835008 | bytes 5505028 | tf_op jit(solution)/shard_map/mul | solution.py:80
  12.1 5.7 %mul.52 = f32[1,64,64,224]{3,2,1,0:T(8,128)} reshape(f32[1,1,1,64,14336]{4,3,2,1,0:T(8,128)} %convert_multiply_fusion) | data formatting | bytes 7340032 | tf_op jit(solution)/shard_map/mul | solution.py:80
  17.8 4.6 %copy.61 = f32[64,1,64,224]{3,2,0,1:T(8,128)S(1)} copy(f32[64,1,64,224]{3,0,2,1:T(8,128)} %bitcast.41) | data formatting | bytes 7340032 | tf_op jit(solution)/shard_map/transpose | solution.py:43
  22.5 2.2 copy.62
  24.7 0.0 copy-start
  24.7 0.0 reduce-scatter.4.cloned.1.call-update
  24.7 0.0 reduce-scatter.6.cloned.1.call-start
  24.8 29.3 %reduce-scatter.4.cloned.1.call-done = f32[32,1,64,224]{3,2,0,1:T(8,128)} async-done(((f32[64,1,64,224]{3,2,0,1:T(8,128)}), f32[32,1,64,224]{3,2,0,1:T(8,128)}) %reduce-scatter.4.cloned.1.call-update) | async-done | bytes 1835024 | tf_op jit(solution)/shard_map/reduce_scatter | solution.py:36
  54.0 0.0 reduce-scatter.6.cloned.1.call-update
  54.1 0.0 reduce-scatter.8.cloned.1.call-start
  54.1 66.1 %reduce-scatter.6.cloned.1.call-done = f32[2,1,64,224]{3,2,0,1:T(8,128)} async-done(((f32[32,1,64,224]{3,2,0,1:T(8,128)}), f32[2,1,64,224]{3,2,0,1:T(8,128)}) %reduce-scatter.6.cloned.1.call-update) | async-done | bytes 114704 | tf_op jit(solution)/shard_map/reduce_scatter | solution.py:36
  120.1 0.0 reduce-scatter.8.cloned.1.call-update
  120.2 0.1 pad_maximum_fusion
  120.3 37.2 %all_to_all.12 = f32[64,1,3]{2,1,0:T(1,128)S(1)} all-to-all(f32[64,1,3]{2,1,0:T(1,128)S(1)} %broadcast_in_dim.8), channel_id=1, replica_groups=mesh['expert'=8,'shard_0'=2,'shard_1'=16,'shard_2'=2] {'shard_0','shard_..., dimensions={0} | all-to-all | bytes 1536 | tf_op jit(solution)/shard_map/all_to_all | solution.py:15
  157.5 0.1 reduce_sum.18
  157.5 0.6 fusion.3
  158.2 1.2 broadcast_in_dim.9
  159.4 4.1 %all-to-all-start.1 = ((f32[8,1,1]{2,1,0:T(1,128)}), f32[8,1,1]{2,1,0:T(1,128)S(1)}, u32[]{:S(2)}, u32[]{:S(2)}) async-start(f32[8,1,1]{2,1,0:T(1,128)} %broadcast_in_dim.9), calls=%async_computation.1 | async-start | bytes 8192 | tf_op jit(solution)/shard_map/all_to_all | solution.py:15
  163.5 0.0 all-gather.2.cloned.1.call-start
  164.2 4.3 %all-to-all-done.1 = f32[8,1,1]{2,1,0:T(1,128)S(1)} async-done(((f32[8,1,1]{2,1,0:T(1,128)}), f32[8,1,1]{2,1,0:T(1,128)S(1)}, u32[]{:S(2)}, u32[]{:S(2)}) %all-to-all-start.1) | async-done | bytes 64 | tf_op jit(solution)/shard_map/all_to_all | solution.py:15
  168.4 0.6 reduce_sum.19
  170.4 0.0 reduce-scatter.8.cloned.1.call-done
  170.4 0.0 copy-done
  170.4 2.1 convert_bitcast_fusion
  172.5 4.9 %all_gather.9 = bf16[2,1,64,224]{3,2,1,0:T(8,128)(2,1)S(1)} all-gather(bf16[1,1,64,224]{3,2,1,0:T(8,128)(2,1)S(1)} %get-tuple-element.18), channel_id=1, replica_groups=mesh['expert'=8,'shard_0'=2,'shard_1'=16,'shard_2'=2] {'shard_0'}, dimensions={0}, use_global_device_ids=true | all-gather | bytes 86016 | tf_op jit(solution)/shard_map/all_gather | solution.py:60
  177.4 27.9 %all_gather.10 = bf16[32,1,64,224]{3,2,1,0:T(8,128)(2,1)} all-gather(bf16[2,1,64,224]{3,2,1,0:T(8,128)(2,1)S(1)} %all_gather.9), channel_id=1, replica_groups=mesh['expert'=8,'shard_0'=2,'shard_1'=16,'shard_2'=2] {'shard_1'}, dimensions={0}, use_global_device_ids=true | all-gather | bytes 974848 | tf_op jit(solution)/shard_map/all_gather | solution.py:60
  205.4 0.0 all-gather.2.cloned.1.call-update
  205.4 22.6 %all-gather.2.cloned.1.call-done = bf16[64,1,64,224]{3,2,1,0:T(8,128)(2,1)} async-done(((bf16[32,1,64,224]{3,2,1,0:T(8,128)(2,1)}), bf16[64,1,64,224]{3,2,1,0:T(8,128)(2,1)}) %all-gather.2.cloned.1.call-update) | async-done | bytes 1835024 | tf_op jit(solution)/shard_map/all_gather | solution.py:60
  228.0 1.7 copy.66
  229.7 1.2 copy.67
  230.9 4.7 %broadcast_in_dim_reshape.3 = bf16[1,1,64,14336]{3,2,1,0:T(8,128)(2,1)} reshape(bf16[1,64,64,224]{3,2,1,0:T(8,128)(2,1)S(1)} %copy.67) | data formatting | bytes 3670016 | tf_op jit(solution)/shard_map/broadcast_in_dim;reshape | solution.py:85
  (1 shorter events, 0.0 us)
Async XLA Ops:
  7.2 46.9 %reduce-scatter.4.cloned.1.call-start = ((), (), s32[]{:S(2)}) async-start(), calls=%async_computation.5 | async-start | bytes 6291456 | tf_op jit(solution)/shard_map/reduce_scatter | solution.py:36
  24.7 145.7 %copy-start = (f32[1,1,64,224]{3,2,1,0:T(8,128)S(1)}, f32[1,1,64,224]{3,2,1,0:T(8,128)}, u32[]{:S(2)}) copy-start(f32[1,1,64,224]{3,2,1,0:T(8,128)} %param.5) | copy-start | bytes 172036
  24.7 95.4 %reduce-scatter.6.cloned.1.call-start = ((), (), s32[]{:S(2)}) async-start(), calls=%async_computation.6 | async-start | bytes 2228224 | tf_op jit(solution)/shard_map/reduce_scatter | solution.py:36
  54.1 116.3 %reduce-scatter.8.cloned.1.call-start = ((), (), s32[]{:S(2)}) async-start(), calls=%async_computation.7 | async-start | bytes 196608 | tf_op jit(solution)/shard_map/reduce_scatter | solution.py:36
  159.4 9.0 %all-to-all-start.1 = ((f32[8,1,1]{2,1,0:T(1,128)}), f32[8,1,1]{2,1,0:T(1,128)S(1)}, u32[]{:S(2)}, u32[]{:S(2)}) async-start(f32[8,1,1]{2,1,0:T(1,128)} %broadcast_in_dim.9), calls=%async_computation.1 | async-start | bytes 8192 | tf_op jit(solution)/shard_map/all_to_all | solution.py:15
  163.5 64.5 %all-gather.2.cloned.1.call-start = ((), (), s32[]{:S(2)}) async-start(), calls=%async_computation.8 | async-start | bytes 3145728 | tf_op jit(solution)/shard_map/all_gather | solution.py:60
Sparse Core Ops, SparseCore 0:
  24.8 29.1 reduce-scatter.3
  57.1 63.0 reduce-scatter.5
  123.1 30.0 reduce-scatter.7
  205.5 22.4 all-gather.1
where the time goes:
time: 243 us; the launch traced here: 242 us
  waiting for transfers between devices  122 us (50%)
  blocking collectives  70 us (29%)
  local copies, waits for them, and re-layouts  22.1 us (9%)
  between operations  17.1 us (7%)
  other arithmetic  6.46 us (3%)
  starting transfers between devices  4.21 us (2%)
    reduce_scatter x3, waiting for transfers between devices, own_block(): pieces = lax.psum_scatter(pieces, axes[k], scatter_dimension=0, tiled=True)  95.3 us
    all_to_all x1, blocking collectives, copy_for_each(): return lax.all_to_all(copies, axis, split_axis=0, concat_axis=0, tiled=True)  37.2 us
    all_gather x2, blocking collectives, stacked_from(): pieces = lax.all_gather(pieces, axes[k], axis=0, tiled=True)  32.8 us
    all_gather x1, waiting for transfers between devices, stacked_from(): pieces = lax.all_gather(pieces, axes[k], axis=0, tiled=True)  22.6 us
    mul x1, local copies, waits for them, and re-layouts, shards(): weighted = share * fast_weights[0, 0].astype(jnp.float32)  5.72 us
  transfers between devices with their start and end apart: 5, of which 4 were waited for; matrix products, arithmetic and copies ran while one was open for 1% of the time, Pallas kernels for 0%

commit v1 on v0

v1 whole, which is shorter than its diff:
```python
import jax
import jax.numpy as jnp
from jax import lax
from jax.experimental import pallas as pl
from jax.experimental.pallas import tpu as pltpu
from jax.sharding import Mesh
from jax.sharding import PartitionSpec as P

F32 = jnp.float32
BF16 = jnp.bfloat16

SHARD = ("x", "zh", "zl", "c")
NEAR = ("x", "zl", "c")

outer_rate = 0.7

ROWS = 64
OWN = 224
LANES = 128
REST = OWN - LANES
PIECE = ROWS * OWN // LANES
TOP = PIECE - ROWS
SLIVER = LANES - REST


def packed(block):
    rest = block[:, LANES:]
    tail = rest[TOP:]
    side = jnp.concatenate([tail[:, k * SLIVER : (k + 1) * SLIVER] for k in range(REST // SLIVER)], axis=0)
    return jnp.concatenate([block[:, :LANES], jnp.concatenate([rest[:TOP], side], axis=1)], axis=0)


def unpacked(piece):
    low = piece[ROWS:]
    side = low[:, REST:]
    n = ROWS - TOP
    tail = jnp.concatenate([side[k * n : (k + 1) * n] for k in range(REST // SLIVER)], axis=1)
    return jnp.concatenate([piece[:ROWS], jnp.concatenate([low[:, :REST], tail], axis=0)], axis=1)


NEAR_NOTES = 16
FAR_NOTES = 8


def as_bytes(count):
    high = count // 256
    return high.astype(F32), (count - 256 * high).astype(F32)


def sort_kernel(tokens, steps, group, fast, out):
    for k in range(out.shape[1]):
        for zh in range(fast.shape[1] // OWN // out.shape[1]):
            at = (zh * out.shape[1] + k) * OWN
            out[0, k, zh * PIECE : (zh + 1) * PIECE] = packed(fast[:, at : at + OWN])
    row = lax.broadcasted_iota(jnp.int32, (NEAR_NOTES, LANES), 0)
    notes = jnp.zeros((NEAR_NOTES, LANES), F32)
    for k, value in enumerate((*as_bytes(tokens[0, 0]), *as_bytes(steps[0, 0]), *as_bytes(group[0, 0]))):
        notes = jnp.where(row == k, value, notes)
    for k in range(out.shape[1]):
        out[0, k, out.shape[2] - NEAR_NOTES :] = notes.astype(BF16)


def near_sum_kernel(got, out):
    n, rows = got.shape[0], got.shape[1] - NEAR_NOTES
    notes = [got[s, rows:].astype(F32) for s in range(n)]
    counts = [[256 * v[2 * k : 2 * k + 1] + v[2 * k + 1 : 2 * k + 2] for k in range(3)] for v in notes]
    shares = [tokens / steps for tokens, steps, _ in counts]
    for zh in range(out.shape[0]):
        piece = slice(zh * PIECE, (zh + 1) * PIECE)
        total = shares[0] * got[0, piece].astype(F32)
        for s in range(1, n):
            total = total + shares[s] * got[s, piece].astype(F32)
        out[zh, :PIECE] = total
    row = lax.broadcasted_iota(jnp.int32, (FAR_NOTES, LANES), 0)
    sums = (
        sum(tokens for tokens, _, _ in counts),
        sum(tokens * steps for tokens, steps, _ in counts),
        sum(shares),
        sum(group for _, _, group in counts),
    )
    far = jnp.zeros((FAR_NOTES, LANES), F32)
    for k, value in enumerate(sums):
        far = jnp.where(row == k, value, far)
    for zh in range(out.shape[0]):
        out[zh, PIECE:] = far


def refresh_kernel(groups, got, slow, new_slow, copies):
    total = got[0]
    for s in range(1, got.shape[0]):
        total = total + got[s]
    notes = total[PIECE:]
    tok, work, qsum, everywhere = (notes[k : k + 1] for k in range(4))
    rate = outer_rate * groups * work / (tok * everywhere)
    mine = packed(slow[0, 0])
    fresh = mine + rate * (total[:PIECE] - qsum * mine)
    new_slow[0, 0] = unpacked(fresh)
    for k in range(copies.shape[0]):
        copies[k] = fresh.astype(BF16)


def lay_out_kernel(core, own, other, out):
    first = core[0, 0] == 0
    for zh in range(own.shape[2]):
        for zl in range(own.shape[1]):
            a, b = own[0, zl, zh].astype(F32), other[0, zl, zh].astype(F32)
            at = (zh * own.shape[1] + zl) * 2 * OWN
            out[:, at : at + OWN] = unpacked(jnp.where(first, a, b)).astype(BF16)
            out[:, at + OWN : at + 2 * OWN] = unpacked(jnp.where(first, b, a)).astype(BF16)


def call(kernel, out_shape, **more):
    return pl.pallas_call(
        kernel,
        out_shape=out_shape,
        compiler_params=pltpu.CompilerParams(vmem_limit_bytes=48 * 2**20),
        **more,
    )


def struct(shape, dtype):
    return jax.ShapeDtypeStruct(shape, dtype)


def swap(pieces, axis):
    return lax.all_to_all(pieces, axis, split_axis=0, concat_axis=0, tiled=True)


def shards(fast_weights, slow_weights, step_counts, token_counts):
    size = {a: lax.axis_size(a) for a in SHARD}
    groups = lax.axis_size("expert")
    near = size["x"] * size["zl"] * size["c"]
    quad = size["zl"] * size["c"]
    scalar = pl.BlockSpec(memory_space=pltpu.SMEM)

    spread = jnp.broadcast_to(token_counts[None], (groups, 1, 1))
    group = swap(spread, "expert").sum(axis=0)

    fast = fast_weights[0, 0, 0]
    rows = size["zh"] * PIECE + NEAR_NOTES
    half = fast.shape[1] // size["x"]
    sorted_pieces = call(
        sort_kernel,
        struct((size["x"], quad, rows, LANES), BF16),
        grid=(size["x"],),
        in_specs=[scalar, scalar, scalar, pl.BlockSpec((ROWS, half), lambda x: (0, x))],
        out_specs=pl.BlockSpec((1, quad, rows, LANES), lambda x: (x, 0, 0, 0)),
    )(token_counts, step_counts, group, fast)
    got = swap(sorted_pieces.reshape(near, rows, LANES), NEAR)
    partial = call(near_sum_kernel, struct((size["zh"], PIECE + FAR_NOTES, LANES), F32))(got)
    got = swap(partial, "zh")
    new_slow, copies = call(
        lambda *refs: refresh_kernel(groups, *refs),
        (struct(slow_weights.shape, F32), struct((size["zh"], PIECE, LANES), BF16)),
    )(got, slow_weights)
    column = swap(copies, "zh")
    plane = size["x"] * size["zl"]
    own = swap(jnp.broadcast_to(column[None], (plane, *column.shape)), ("x", "zl"))
    other = lax.ppermute(own, "c", [(0, 1), (1, 0)])
    shape = (size["x"], size["zl"], size["zh"], PIECE, LANES)
    block = pl.BlockSpec((1, *shape[1:]), lambda x: (x, 0, 0, 0, 0))
    reset = call(
        lay_out_kernel,
        struct(fast.shape, BF16),
        grid=(size["x"],),
        in_specs=[scalar, block, block],
        out_specs=pl.BlockSpec((ROWS, half), lambda x: (0, x)),
    )(lax.axis_index("c").astype(jnp.int32).reshape(1, 1), own.reshape(shape), other.reshape(shape))
    return new_slow, reset[None, None]


def solution(mesh):
    torus = Mesh(
        mesh.devices.reshape(mesh.shape["expert"], 2, 8, 2, 2),
        ("expert", *SHARD),
    )
    placed = (
        P("expert", SHARD, None, None, None),
        P("expert", None, None, SHARD),
        P("expert", SHARD),
        P("expert", SHARD),
    )
    return jax.shard_map(
        shards,
        mesh=torus,
        in_specs=placed,
        out_specs=(P("expert", None, None, SHARD), P("expert", None, None, None)),
        check_vma=False,
    )
```

time: 243 us -> 147 us (0.60)
  waiting for transfers between devices: 122 us -> 6.35 us
  blocking collectives: 70 us -> 110 us
  local copies, waits for them, and re-layouts: 22.1 us -> 2.22 us
  between operations: 17.1 us -> 1.96 us
  Pallas kernels: 0 us -> 12.9 us
  starting transfers between devices: 4.21 us -> 12.2 us
  other arithmetic: 6.46 us -> 0.64 us
    reduce_scatter x3 -> x0, waiting for transfers between devices: 95.3 us -> none  [own_block(): pieces = lax.psum_scatter(pieces, axes[k], scatter_dimension=0, tiled=True)]
    all_to_all x1 -> x4, blocking collectives: 37.2 us -> 110 us  [swap(): return lax.all_to_all(pieces, axis, split_axis=0, concat_axis=0, tiled=True)]
    all_gather x2 -> x0, blocking collectives: 32.8 us -> none  [stacked_from(): pieces = lax.all_gather(pieces, axes[k], axis=0, tiled=True)]
    all_gather x1 -> x0, waiting for transfers between devices: 22.6 us -> none  [stacked_from(): pieces = lax.all_gather(pieces, axes[k], axis=0, tiled=True)]
    pallas_call x0 -> x4, Pallas kernels: none -> 12.9 us  [the longest x1 8.23 us: shards(): call(sort_kernel, struct((size['x'], quad, rows, LANES), BF16), grid=(siz...]
    transpose x4 -> x0, local copies, waits for them, and re-layouts: 9.76 us -> none  [the longest x1 4.62 us: cut_along(): return jnp.moveaxis(pieces, dim, 0)]
    ppermute x0 -> x1, starting transfers between devices: none -> 6.27 us  [shards(): other = lax.ppermute(own, 'c', [(0, 1), (1, 0)])]
    mul x1 -> x0, local copies, waits for them, and re-layouts: 5.72 us -> none  [shards(): weighted = share * fast_weights[0, 0].astype(jnp.float32)]
  transfers between devices with their start and end apart: 5 -> 2, of which waited for: 4 -> 2; matrix products, arithmetic and copies ran while one was open for 1% -> 0% of each run, Pallas kernels for 0% -> 0%
where the time goes in v1:
time: 147 us; the launch traced here: 146 us
  blocking collectives  110 us (75%)
  Pallas kernels  12.9 us (9%)
  starting transfers between devices  12.2 us (8%)
  waiting for transfers between devices  6.35 us (4%)
  local copies, waits for them, and re-layouts  2.22 us (2%)
  between operations  1.96 us (1%)
    all_to_all x4, blocking collectives, swap(): return lax.all_to_all(pieces, axis, split_axis=0, concat_axis=0, tiled=True)  110 us
    pallas_call x1, Pallas kernels, shards(): call(sort_kernel, struct((size['x'], quad, rows, LANES), BF16), grid=(siz...  8.23 us
    ppermute x1, starting transfers between devices, shards(): other = lax.ppermute(own, 'c', [(0, 1), (1, 0)])  6.27 us
    all_to_all x1, starting transfers between devices, swap(): return lax.all_to_all(pieces, axis, split_axis=0, concat_axis=0, tiled=True)  5.95 us
    all_to_all x1, waiting for transfers between devices, swap(): return lax.all_to_all(pieces, axis, split_axis=0, concat_axis=0, tiled=True)  4.28 us
    pallas_call x1, Pallas kernels, shards(): call(lay_out_kernel, struct(fast.shape, BF16), grid=(size['x'],), in_spec...  3.51 us
  transfers between devices with their start and end apart: 2, of which 2 were waited for; matrix products, arithmetic and copies ran while one was open for 0% of the time, Pallas kernels for 0%

profile of v1, /device:TPU:1, one launch (start us, length us, event | category | flops | bytes accessed | tf_op | source)
XLA Modules:
  0.0 146.4 jit_solution(17912014050515639345)
XLA Ops:
  1.3 0.6 broadcast_in_dim.18
  1.9 5.9 %all-to-all-start = ((s32[8,1,1]{2,1,0:T(1,128)}), s32[8,1,1]{2,1,0:T(1,128)S(1)}, u32[]{:S(2)}, u32[]{:S(2)}) async-start(s32[8,1,1]{2,1,0:T(1,128)} %broadcast_in_dim.18), calls=%async_computation | async-start | bytes 8192 | tf_op jit(solution)/shard_map/all_to_all | solution.py:126
  8.5 4.3 %all-to-all-done = s32[8,1,1]{2,1,0:T(1,128)S(1)} async-done(((s32[8,1,1]{2,1,0:T(1,128)}), s32[8,1,1]{2,1,0:T(1,128)S(1)}, u32[]{:S(2)}, u32[]{:S(2)}) %all-to-all-start) | async-done | bytes 64 | tf_op jit(solution)/shard_map/all_to_all | solution.py:126
  12.7 0.6 reduce_sum.11
  13.4 0.0 copy-start
  13.4 1.5 %copy-done = bf16[1,1,1,64,14336]{4,3,2,1,0:T(8,128)(2,1)S(1)} copy-done((bf16[1,1,1,64,14336]{4,3,2,1,0:T(8,128)(2,1)S(1)}, bf16[1,1,1,64,14336]{4,3,2,1,0:T(8,128)(2,1)}, u32[]{:S(2)}) %copy-start) | copy-done | bytes 1835032
  14.9 8.2 %shard_map.59 = bf16[2,4,912,128]{3,2,1,0:T(8,128)(2,1)S(1)} custom-call(s32[1,1]{1,0:T(1,128)} %copy.9.tokens, s32[1,1]{1,0:T(1,128)S(6)} %copy.8.steps, s32[1,1]{1,0:T(1,128)} %bitcast.1.group, bf16[64,14336]{1,0:T(8,128)(2,1)S(1)} %bitcast.11), custom_call_target="tpu_custom_call" | custom-call | tf_op jit(solution)/shard_map/pallas_call | solution.py:142
  23.1 32.8 %all_to_all.25.got = bf16[8,912,128]{2,1,0:T(8,128)(2,1)S(1)} all-to-all(bf16[8,912,128]{2,1,0:T(8,128)(2,1)S(1)} %bitcast.9), channel_id=1, replica_groups=mesh['expert'=8,'x'=2,'zh'=8,'zl'=2,'c'=2] {'x','zl','c'}, dimensions={0} | all-to-all | bytes 3735552 | tf_op jit(solution)/shard_map/all_to_all | solution.py:126
  55.9 0.0 copy-start.1
  55.9 0.4 shard_map.60
  56.3 40.6 %all_to_all.26.refs_0_ = f32[8,120,128]{2,1,0:T(8,128)S(1)} all-to-all(f32[8,120,128]{2,1,0:T(8,128)S(1)} %shard_map.60), channel_id=1, replica_groups=mesh['expert'=8,'x'=2,'zh'=8,'zl'=2,'c'=2] {'zh'}, dimensions={0} | all-to-all | bytes 983040 | tf_op jit(solution)/shard_map/all_to_all | solution.py:126
  96.9 0.0 copy-done.1
  96.9 0.8 shard_map.61
  97.8 23.3 %all_to_all.27 = bf16[8,112,128]{2,1,0:T(8,128)(2,1)S(1)} all-to-all(bf16[8,112,128]{2,1,0:T(8,128)(2,1)S(1)} %get-tuple-element.5), channel_id=1, replica_groups=mesh['expert'=8,'x'=2,'zh'=8,'zl'=2,'c'=2] {'zh'}, dimensions={0} | all-to-all | bytes 458752 | tf_op jit(solution)/shard_map/all_to_all | solution.py:126
  121.1 0.1 broadcast_in_dim.19
  121.3 13.3 %all_to_all.28 = bf16[4,8,112,128]{3,2,1,0:T(8,128)(2,1)S(1)} all-to-all(bf16[4,8,112,128]{3,2,1,0:T(8,128)(2,1)S(1)} %broadcast_in_dim.19), channel_id=1, replica_groups=mesh['expert'=8,'x'=2,'zh'=8,'zl'=2,'c'=2] {'x','zl'}, dimensions={0} | all-to-all | bytes 1835008 | tf_op jit(solution)/shard_map/all_to_all | solution.py:126
  134.5 6.3 %collective-permute-start = (bf16[4,8,112,128]{3,2,1,0:T(8,128)(2,1)S(1)}, bf16[4,8,112,128]{3,2,1,0:T(8,128)(2,1)S(1)}, u32[]{:S(2)}, u32[]{:S(2)}) collective-permute-start(bf16[4,8,112,128]{3,2,1,0:T(8,128)(2,1)S(1)} %all_to_all.28), channel_id=1, source_target_pairs={{0,1},{1,0},{2,3},{3,2},{4,5},{5,4},{6,7},{7,6},{8,9},{9,8},{10,11... | collective-permute-start | bytes 2752520 | tf_op jit(solution)/shard_map/ppermute | solution.py:159
  140.8 2.1 %collective-permute-done = bf16[4,8,112,128]{3,2,1,0:T(8,128)(2,1)S(1)} collective-permute-done((bf16[4,8,112,128]{3,2,1,0:T(8,128)(2,1)S(1)}, bf16[4,8,112,128]{3,2,1,0:T(8,128)(2,1)S(1)}, u32[]{:S(2)}, u32[]{:S(2)}) %collective-permute-start) | collective-permute-done | bytes 917536 | tf_op jit(solution)/shard_map/ppermute | solution.py:159
  142.9 3.5 %shard_map.62 = bf16[64,14336]{1,0:T(8,128)(2,1)} custom-call(s32[1,1]{1,0:T(1,128)} %bitcast.4.core, bf16[2,2,8,112,128]{4,3,2,1,0:T(8,128)(2,1)S(1)} %bitcast.10, bf16[2,2,8,112,128]{4,3,2,1,0:T(8,128)(2,1)S(1)} %bitcast.12), custom_call_target="tpu_custom_call" | custom-call | tf_op jit(solution)/shard_map/pallas_call | solution.py:162
Async XLA Ops:
  1.9 10.9 %all-to-all-start = ((s32[8,1,1]{2,1,0:T(1,128)}), s32[8,1,1]{2,1,0:T(1,128)S(1)}, u32[]{:S(2)}, u32[]{:S(2)}) async-start(s32[8,1,1]{2,1,0:T(1,128)} %broadcast_in_dim.18), calls=%async_computation | async-start | bytes 8192 | tf_op jit(solution)/shard_map/all_to_all | solution.py:126
  13.4 1.5 %copy-start = (bf16[1,1,1,64,14336]{4,3,2,1,0:T(8,128)(2,1)S(1)}, bf16[1,1,1,64,14336]{4,3,2,1,0:T(8,128)(2,1)}, u32[]{:S(2)}) copy-start(bf16[1,1,1,64,14336]{4,3,2,1,0:T(8,128)(2,1)} %param.4) | copy-start | bytes 5505028
  55.9 41.0 %copy-start.1 = (f32[1,1,64,224]{3,2,1,0:T(8,128)S(1)}, f32[1,1,64,224]{3,2,1,0:T(8,128)}, u32[]{:S(2)}) copy-start(f32[1,1,64,224]{3,2,1,0:T(8,128)} %refs_1_.1) | copy-start | bytes 172036
  134.5 8.4 %collective-permute-start = (bf16[4,8,112,128]{3,2,1,0:T(8,128)(2,1)S(1)}, bf16[4,8,112,128]{3,2,1,0:T(8,128)(2,1)S(1)}, u32[]{:S(2)}, u32[]{:S(2)}) collective-permute-start(bf16[4,8,112,128]{3,2,1,0:T(8,128)(2,1)S(1)} %all_to_all.28), channel_id=1, source_target_pairs={{0,1},{1,0},{2,3},{3,2},{4,5},{5,4},{6,7},{7,6},{8,9},{9,8},{10,11... | collective-permute-start | bytes 2752520 | tf_op jit(solution)/shard_map/ppermute | solution.py:159

commit v2 on v1

v2 whole, which is shorter than its diff:
```python
import jax
import jax.numpy as jnp
from jax import lax
from jax.experimental import pallas as pl
from jax.experimental.pallas import tpu as pltpu
from jax.sharding import Mesh
from jax.sharding import PartitionSpec as P

F32 = jnp.float32
BF16 = jnp.bfloat16

SHARD = ("x", "zh", "zl", "c")
NEAR = ("x", "zl", "c")

outer_rate = 0.7

ROWS = 64
OWN = 224
LANES = 128
QUAD = 4
WIDE = QUAD * OWN
STEP = 32
TAIL = 16
REST = ROWS - TAIL

PIECE = ROWS + REST

NEAR_NOTES = 16
FAR_NOTES = 8


def lane_group(shape):
    return lax.broadcasted_iota(jnp.int32, shape, 1) // STEP


def rolled(v, by):
    by %= LANES
    return jnp.concatenate([v[:, LANES - by :], v[:, : LANES - by]], axis=1) if by else v


def folded(res, k):
    free = QUAD - 1 - k
    tail = res[REST:]
    group = lane_group((TAIL, LANES))
    return jnp.concatenate(
        [jnp.where(group == free, rolled(tail, STEP * (m + 1)), res[m * TAIL : (m + 1) * TAIL]) for m in range(QUAD - 1)],
        axis=0,
    )


def unfolded(piece, k):
    free = QUAD - 1 - k
    group = lane_group((TAIL, LANES))
    tail = rolled(piece[:TAIL], -STEP)
    for m in range(1, QUAD - 1):
        moved = rolled(piece[m * TAIL : (m + 1) * TAIL], -STEP * (m + 1))
        tail = jnp.where(group == (free - m - 1) % QUAD, moved, tail)
    return jnp.concatenate([piece, tail], axis=0)


def own_parts(block, k):
    at = STEP * k
    res = [block[:, at + LANES :], jnp.zeros((ROWS, STEP), block.dtype), block[:, :at]]
    return block[:, at : at + LANES], folded(jnp.concatenate([r for r in res if r.shape[1]], axis=1), k)


def own_block(tile, piece, k):
    at = STEP * k
    res = unfolded(piece, k)
    parts = [res[:, LANES - at :] if k else res[:, :0], tile, res[:, : LANES - STEP - at]]
    return jnp.concatenate([p for p in parts if p.shape[1]], axis=1)


def as_bytes(count):
    high = count // 256
    return high.astype(F32), (count - 256 * high).astype(F32)


def sort_kernel(fast, out):
    group = lane_group((ROWS, LANES))
    for zh in range(fast.shape[1] // WIDE):
        lanes = [slice(zh * WIDE + i * LANES, zh * WIDE + (i + 1) * LANES) for i in range(2 * QUAD - 1)]
        odd = [fast[:, at].astype(F32) for at in lanes[1::2]]
        for k in range(QUAD):
            if k == 0:
                res = odd[0]
            elif k == QUAD - 1:
                res = odd[-1]
            else:
                res = jnp.where(group >= QUAD - k, odd[k - 1], odd[k])
            at = zh * PIECE
            out[0, k, at : at + ROWS] = fast[:, lanes[2 * k]]
            out[0, k, at + ROWS : at + PIECE] = folded(res, k).astype(BF16)


def notes_kernel(tokens, steps, experts, _, out):
    row = lax.broadcasted_iota(jnp.int32, (NEAR_NOTES, LANES), 0)
    notes = jnp.zeros((NEAR_NOTES, LANES), F32)
    for i, count in enumerate((tokens[0, 0], steps[0, 0], sum(experts[e, 0] for e in range(experts.shape[0])))):
        for j, value in enumerate(as_bytes(count)):
            notes = jnp.where(row == 2 * i + j, value, notes)
    for k in range(out.shape[1]):
        out[0, k] = notes.astype(BF16)


def near_sum_kernel(got, out):
    n, rows = got.shape[0], got.shape[1] - NEAR_NOTES
    notes = [got[s, rows:].astype(F32) for s in range(n)]
    counts = [[256 * v[2 * i : 2 * i + 1] + v[2 * i + 1 : 2 * i + 2] for i in range(3)] for v in notes]
    shares = [tokens / steps for tokens, steps, _ in counts]
    tok = sum(tokens for tokens, _, _ in counts)
    work = sum(tokens * steps for tokens, steps, _ in counts)
    everywhere = sum(group for _, _, group in counts)
    row = lax.broadcasted_iota(jnp.int32, (FAR_NOTES, LANES), 0)
    far = jnp.zeros((FAR_NOTES, LANES), F32)
    for i, value in enumerate((tok, work, sum(shares), everywhere)):
        far = jnp.where(row == i, value, far)
    for zh in range(out.shape[0]):
        piece = slice(zh * PIECE, (zh + 1) * PIECE)
        total = shares[0] * got[0, piece].astype(F32)
        for s in range(1, n):
            total = total + shares[s] * got[s, piece].astype(F32)
        out[zh, :PIECE] = total
        out[zh, PIECE:] = far


def refresh_kernel(groups, place, got, slow, new_slow, copies):
    total = got[0]
    for s in range(1, got.shape[0]):
        total = total + got[s]
    tok, work, qsum, everywhere = (total[PIECE + i : PIECE + i + 1] for i in range(4))
    rate = outer_rate * groups * work / (tok * everywhere)
    for k in range(QUAD):

        @pl.when(place[0, 0] == k)
        def _(k=k):
            mine = own_parts(slow[0, 0], k)
            tile = mine[0] + rate * (total[:ROWS] - qsum * mine[0])
            rest = mine[1] + rate * (total[ROWS:PIECE] - qsum * mine[1])
            new_slow[0, 0] = own_block(tile, rest, k)
            for i in range(copies.shape[0]):
                copies[i, :ROWS] = tile.astype(BF16)
                copies[i, ROWS:] = rest.astype(BF16)


def lay_out_kernel(core, own, other, out):
    def body(pieces):
        group = lane_group((ROWS, LANES))
        for zh in range(own.shape[2]):
            at = zh * WIDE
            for k in range(QUAD):
                out[:, at + 2 * k * LANES : at + (2 * k + 1) * LANES] = pieces[k % 2][0, k // 2, zh, :ROWS]
            res = [unfolded(pieces[k % 2][0, k // 2, zh, ROWS:].astype(F32), k) for k in range(QUAD)]
            for k in range(QUAD - 1):
                odd = jnp.where(group < QUAD - 1 - k, res[k], res[k + 1])
                out[:, at + (2 * k + 1) * LANES : at + (2 * k + 2) * LANES] = odd.astype(BF16)

    @pl.when(core[0, 0] == 0)
    def _():
        body((own, other))

    @pl.when(core[0, 0] != 0)
    def _():
        body((other, own))


def call(kernel, out_shape, **more):
    return pl.pallas_call(
        kernel,
        out_shape=out_shape,
        compiler_params=pltpu.CompilerParams(vmem_limit_bytes=48 * 2**20),
        **more,
    )


def struct(shape, dtype):
    return jax.ShapeDtypeStruct(shape, dtype)


def swap(pieces, axis):
    return lax.all_to_all(pieces, axis, split_axis=0, concat_axis=0, tiled=True)


SCALAR = pl.BlockSpec(memory_space=pltpu.SMEM)
WHOLE = pl.BlockSpec(memory_space=pltpu.VMEM)


def scalar(value):
    return value.astype(jnp.int32).reshape(1, 1)


def shards(fast_weights, slow_weights, step_counts, token_counts):
    size = {a: lax.axis_size(a) for a in SHARD}
    groups = lax.axis_size("expert")
    nx, nzh, near = size["x"], size["zh"], size["x"] * size["zl"] * size["c"]
    core = lax.axis_index("c")
    place = scalar(lax.axis_index("zl") * size["c"] + core)
    core = scalar(core)

    fast = fast_weights[0, 0, 0]
    half = fast.shape[1] // nx
    halves = pl.BlockSpec((ROWS, half), lambda x: (0, x))

    def by_x(*shape):
        return pl.BlockSpec((1, *shape[1:]), lambda x: (x, *(0 for _ in shape[1:])))

    experts = swap(jnp.broadcast_to(token_counts, (groups, 1)), "expert")
    shape = (nx, QUAD, nzh * PIECE + NEAR_NOTES, LANES)
    pieces = call(sort_kernel, struct(shape, BF16), grid=(nx,), in_specs=[halves], out_specs=by_x(*shape))(fast)
    pieces = call(
        notes_kernel,
        struct(shape, BF16),
        grid=(nx,),
        in_specs=[SCALAR, SCALAR, SCALAR, pl.BlockSpec(memory_space=pl.ANY)],
        out_specs=pl.BlockSpec((1, QUAD, NEAR_NOTES, LANES), lambda x: (x, 0, shape[2] // NEAR_NOTES - 1, 0)),
        input_output_aliases={3: 0},
    )(token_counts, step_counts, experts, pieces)
    got = swap(pieces.reshape(near, *shape[2:]), NEAR)
    coded = call(near_sum_kernel, struct((nzh, PIECE + FAR_NOTES, LANES), F32))(got)
    got = swap(coded, "zh")
    new_slow, copies = call(
        lambda *refs: refresh_kernel(groups, *refs),
        (struct(slow_weights.shape, F32), struct((nzh, PIECE, LANES), BF16)),
        in_specs=[SCALAR, WHOLE, WHOLE],
    )(place, got, slow_weights)

    column = swap(copies, "zh")
    plane = nx * size["zl"]
    own = swap(jnp.broadcast_to(column[None], (plane, *column.shape)), ("x", "zl"))
    other = lax.ppermute(own, "c", [(0, 1), (1, 0)])
    shape = (nx, size["zl"], *column.shape)
    reset = call(
        lay_out_kernel,
        struct(fast.shape, BF16),
        grid=(nx,),
        in_specs=[SCALAR, by_x(*shape), by_x(*shape)],
        out_specs=halves,
    )(core, own.reshape(shape), other.reshape(shape))
    return new_slow, reset[None, None]


def solution(mesh):
    torus = Mesh(
        mesh.devices.reshape(mesh.shape["expert"], 2, 8, 2, 2),
        ("expert", *SHARD),
    )
    placed = (
        P("expert", SHARD, None, None, None),
        P("expert", None, None, SHARD),
        P("expert", SHARD),
        P("expert", SHARD),
    )
    return jax.shard_map(
        shards,
        mesh=torus,
        in_specs=placed,
        out_specs=(P("expert", None, None, SHARD), P("expert", None, None, None)),
        check_vma=False,
    )
```

time: 147 us -> 136 us (0.925)
  blocking collectives: 110 us -> 68.4 us
  waiting for transfers between devices: 6.35 us -> 32.1 us
  starting transfers between devices: 12.2 us -> 26.3 us
  Pallas kernels: 12.9 us -> 4.82 us
    all_to_all x4 -> x3, blocking collectives: 110 us -> 68.4 us  [swap(): return lax.all_to_all(pieces, axis, split_axis=0, concat_axis=0, tiled=True)]
    all_to_all x1 -> x2, waiting for transfers between devices: 4.28 us -> 30.1 us  [swap(): return lax.all_to_all(pieces, axis, split_axis=0, concat_axis=0, tiled=True)]
    all_to_all x1 -> x2, starting transfers between devices: 5.95 us -> 19.4 us  [swap(): return lax.all_to_all(pieces, axis, split_axis=0, concat_axis=0, tiled=True)]
    pallas_call x3 -> x4, Pallas kernels: 12.1 us -> 3.88 us  [the longest x1 1.43 us: shards(): call(lay_out_kernel, struct(fast.shape, BF16), grid=(nx,), in_specs=[SCAL...]
  transfers between devices with their start and end apart: 2 -> 3, of which waited for: 2 -> 3; matrix products, arithmetic and copies ran while one was open for 0% -> 0% of each run, Pallas kernels for 0% -> 0%
where the time goes in v2:
time: 136 us
  blocking collectives  68.4 us (50%)
  waiting for transfers between devices  32.1 us (24%)
  starting transfers between devices  26.3 us (19%)
  Pallas kernels  4.82 us (4%)
  local copies, waits for them, and re-layouts  2.21 us (2%)
  between operations  1.97 us (1%)
    all_to_all x3, blocking collectives, swap(): return lax.all_to_all(pieces, axis, split_axis=0, concat_axis=0, tiled=True)  68.4 us
    all_to_all x2, waiting for transfers between devices, swap(): return lax.all_to_all(pieces, axis, split_axis=0, concat_axis=0, tiled=True)  30.1 us
    all_to_all x2, starting transfers between devices, swap(): return lax.all_to_all(pieces, axis, split_axis=0, concat_axis=0, tiled=True)  19.4 us
    ppermute x1, starting transfers between devices, shards(): other = lax.ppermute(own, 'c', [(0, 1), (1, 0)])  6.91 us
  transfers between devices with their start and end apart: 3, of which 3 were waited for; matrix products, arithmetic and copies ran while one was open for 0% of the time, Pallas kernels for 0%

profile of v2, /device:TPU:1, one launch (start us, length us, event | category | flops | bytes accessed | tf_op | source)
XLA Modules:
  0.0 135.8 jit_solution(960914442041575145)
XLA Ops:
  1.3 0.6 broadcast_in_dim.17
  1.9 5.9 %all-to-all-start = ((s32[8,1,1]{2,1,0:T(1,128)}), s32[8,1,1]{2,1,0:T(1,128)S(1)}, u32[]{:S(2)}, u32[]{:S(2)}) async-start(s32[8,1,1]{2,1,0:T(1,128)} %broadcast_in_dim.17), calls=%async_computation | async-start | bytes 8192 | tf_op jit(solution)/shard_map/all_to_all | solution.py:181
  8.5 0.0 copy-start
  8.5 1.5 %copy-done = bf16[1,1,1,64,14336]{4,3,2,1,0:T(8,128)(2,1)S(1)} copy-done((bf16[1,1,1,64,14336]{4,3,2,1,0:T(8,128)(2,1)S(1)}, bf16[1,1,1,64,14336]{4,3,2,1,0:T(8,128)(2,1)}, u32[]{:S(2)}) %copy-start) | copy-done | bytes 1835032
  10.0 0.6 shard_map.59._
  10.6 2.2 %all-to-all-done = s32[8,1,1]{2,1,0:T(1,128)S(1)} async-done(((s32[8,1,1]{2,1,0:T(1,128)}), s32[8,1,1]{2,1,0:T(1,128)S(1)}, u32[]{:S(2)}, u32[]{:S(2)}) %all-to-all-start) | async-done | bytes 64 | tf_op jit(solution)/shard_map/all_to_all | solution.py:181
  12.7 0.7 shard_map.60
  13.5 32.8 %all_to_all.28.got = bf16[8,912,128]{2,1,0:T(8,128)(2,1)S(1)} all-to-all(bf16[8,912,128]{2,1,0:T(8,128)(2,1)S(1)} %bitcast.10), channel_id=1, replica_groups=mesh['expert'=8,'x'=2,'zh'=8,'zl'=2,'c'=2] {'x','zl','c'}, dimensions={0} | all-to-all | bytes 3735552 | tf_op jit(solution)/shard_map/all_to_all | solution.py:181
  46.3 0.0 copy-start.1
  46.3 1.1 shard_map.61
  47.4 13.4 %all-to-all-start.2 = ((f32[8,120,128]{2,1,0:T(8,128)}), f32[8,120,128]{2,1,0:T(8,128)S(1)}, u32[]{:S(2)}, u32[]{:S(2)}) async-start(f32[8,120,128]{2,1,0:T(8,128)} %shard_map.61), calls=%async_computation.2 | async-start | bytes 983040 | tf_op jit(solution)/shard_map/all_to_all | solution.py:181
  60.9 27.9 %all-to-all-done.2.refs_1_ = f32[8,120,128]{2,1,0:T(8,128)S(1)} async-done(((f32[8,120,128]{2,1,0:T(8,128)}), f32[8,120,128]{2,1,0:T(8,128)S(1)}, u32[]{:S(2)}, u32[]{:S(2)}) %all-to-all-start.2) | async-done | bytes 491552 | tf_op jit(solution)/shard_map/all_to_all | solution.py:181
  88.7 0.0 copy-done.1
  88.8 0.9 shard_map.62
  89.7 23.0 %all_to_all.29 = bf16[8,112,128]{2,1,0:T(8,128)(2,1)S(1)} all-to-all(bf16[8,112,128]{2,1,0:T(8,128)(2,1)S(1)} %get-tuple-element.5), channel_id=1, replica_groups=mesh['expert'=8,'x'=2,'zh'=8,'zl'=2,'c'=2] {'zh'}, dimensions={0} | all-to-all | bytes 458752 | tf_op jit(solution)/shard_map/all_to_all | solution.py:181
  112.7 0.1 broadcast_in_dim.18
  112.8 12.6 %all_to_all.30 = bf16[4,8,112,128]{3,2,1,0:T(8,128)(2,1)S(1)} all-to-all(bf16[4,8,112,128]{3,2,1,0:T(8,128)(2,1)S(1)} %broadcast_in_dim.18), channel_id=1, replica_groups=mesh['expert'=8,'x'=2,'zh'=8,'zl'=2,'c'=2] {'x','zl'}, dimensions={0} | all-to-all | bytes 1835008 | tf_op jit(solution)/shard_map/all_to_all | solution.py:181
  125.4 6.9 %collective-permute-start = (bf16[4,8,112,128]{3,2,1,0:T(8,128)(2,1)S(1)}, bf16[4,8,112,128]{3,2,1,0:T(8,128)(2,1)S(1)}, u32[]{:S(2)}, u32[]{:S(2)}) collective-permute-start(bf16[4,8,112,128]{3,2,1,0:T(8,128)(2,1)S(1)} %all_to_all.30), channel_id=1, source_target_pairs={{0,1},{1,0},{2,3},{3,2},{4,5},{5,4},{6,7},{7,6},{8,9},{9,8},{10,11... | collective-permute-start | bytes 2752520 | tf_op jit(solution)/shard_map/ppermute | solution.py:230
  132.3 2.1 %collective-permute-done = bf16[4,8,112,128]{3,2,1,0:T(8,128)(2,1)S(1)} collective-permute-done((bf16[4,8,112,128]{3,2,1,0:T(8,128)(2,1)S(1)}, bf16[4,8,112,128]{3,2,1,0:T(8,128)(2,1)S(1)}, u32[]{:S(2)}, u32[]{:S(2)}) %collective-permute-start) | collective-permute-done | bytes 917536 | tf_op jit(solution)/shard_map/ppermute | solution.py:230
  134.4 1.4 %shard_map.63 = bf16[64,14336]{1,0:T(8,128)(2,1)} custom-call(s32[1,1]{1,0:T(1,128)} %bitcast.5.core, bf16[2,2,8,112,128]{4,3,2,1,0:T(8,128)(2,1)S(1)} %bitcast.11, bf16[2,2,8,112,128]{4,3,2,1,0:T(8,128)(2,1)S(1)} %bitcast.13), custom_call_target="tpu_custom_call" | custom-call | tf_op jit(solution)/shard_map/pallas_call | solution.py:232
Async XLA Ops:
  1.9 10.9 %all-to-all-start = ((s32[8,1,1]{2,1,0:T(1,128)}), s32[8,1,1]{2,1,0:T(1,128)S(1)}, u32[]{:S(2)}, u32[]{:S(2)}) async-start(s32[8,1,1]{2,1,0:T(1,128)} %broadcast_in_dim.17), calls=%async_computation | async-start | bytes 8192 | tf_op jit(solution)/shard_map/all_to_all | solution.py:181
  8.5 1.5 %copy-start = (bf16[1,1,1,64,14336]{4,3,2,1,0:T(8,128)(2,1)S(1)}, bf16[1,1,1,64,14336]{4,3,2,1,0:T(8,128)(2,1)}, u32[]{:S(2)}) copy-start(bf16[1,1,1,64,14336]{4,3,2,1,0:T(8,128)(2,1)} %param.4) | copy-start | bytes 5505028
  46.3 42.5 %copy-start.1 = (f32[1,1,64,224]{3,2,1,0:T(8,128)S(1)}, f32[1,1,64,224]{3,2,1,0:T(8,128)}, u32[]{:S(2)}) copy-start(f32[1,1,64,224]{3,2,1,0:T(8,128)} %refs_2_.1) | copy-start | bytes 172036
  47.4 41.3 %all-to-all-start.2 = ((f32[8,120,128]{2,1,0:T(8,128)}), f32[8,120,128]{2,1,0:T(8,128)S(1)}, u32[]{:S(2)}, u32[]{:S(2)}) async-start(f32[8,120,128]{2,1,0:T(8,128)} %shard_map.61), calls=%async_computation.2 | async-start | bytes 983040 | tf_op jit(solution)/shard_map/all_to_all | solution.py:181
  125.4 9.0 %collective-permute-start = (bf16[4,8,112,128]{3,2,1,0:T(8,128)(2,1)S(1)}, bf16[4,8,112,128]{3,2,1,0:T(8,128)(2,1)S(1)}, u32[]{:S(2)}, u32[]{:S(2)}) collective-permute-start(bf16[4,8,112,128]{3,2,1,0:T(8,128)(2,1)S(1)} %all_to_all.30), channel_id=1, source_target_pairs={{0,1},{1,0},{2,3},{3,2},{4,5},{5,4},{6,7},{7,6},{8,9},{9,8},{10,11... | collective-permute-start | bytes 2752520 | tf_op jit(solution)/shard_map/ppermute | solution.py:230

commit v3 on v2

--- a/solution.py
+++ b/solution.py
@@ -27,6 +27,10 @@
 
 NEAR_NOTES = 16
 FAR_NOTES = 8
+TOP = 32767.0
+DIGIT = 4096.0
+MIDDLE = 32768.0
+FINE = 8.0
 
 
 def lane_group(shape):
@@ -111,24 +115,39 @@
     tok = sum(tokens for tokens, _, _ in counts)
     work = sum(tokens * steps for tokens, steps, _ in counts)
     everywhere = sum(group for _, _, group in counts)
+    qsum = sum(shares)
+    whole = jnp.floor(qsum)
+    part = (qsum - whole) * DIGIT
+    digit = jnp.floor(part)
+    high = jnp.floor(work / DIGIT)
+    fixed = (tok, high, work - DIGIT * high, everywhere - MIDDLE, whole, digit, jnp.floor((part - digit) * DIGIT))
     row = lax.broadcasted_iota(jnp.int32, (FAR_NOTES, LANES), 0)
     far = jnp.zeros((FAR_NOTES, LANES), F32)
-    for i, value in enumerate((tok, work, sum(shares), everywhere)):
-        far = jnp.where(row == i, value, far)
+    for i, value in enumerate(fixed):
+        far = jnp.where(row == i + 1, value, far)
     for zh in range(out.shape[0]):
         piece = slice(zh * PIECE, (zh + 1) * PIECE)
         total = shares[0] * got[0, piece].astype(F32)
         for s in range(1, n):
             total = total + shares[s] * got[s, piece].astype(F32)
-        out[zh, :PIECE] = total
-        out[zh, PIECE:] = far
+        largest = jnp.maximum(jnp.max(jnp.abs(total), axis=0, keepdims=True), 1e-30)
+        level = jnp.ceil(FINE * jnp.log2(largest))
+        coded = jnp.clip(jnp.round(total * (TOP * jnp.exp2(level * (-1 / FINE)))), -TOP, TOP)
+        out[zh, :PIECE] = coded.astype(jnp.int32).astype(jnp.int16)
+        out[zh, PIECE:] = jnp.where(row == 0, level, far).astype(jnp.int32).astype(jnp.int16)
 
 
 def refresh_kernel(groups, place, got, slow, new_slow, copies):
-    total = got[0]
-    for s in range(1, got.shape[0]):
-        total = total + got[s]
-    tok, work, qsum, everywhere = (total[PIECE + i : PIECE + i + 1] for i in range(4))
+    total = sums = None
+    for s in range(got.shape[0]):
+        notes = got[s, PIECE:].astype(jnp.int32).astype(F32)
+        unit = jnp.exp2(notes[0:1] * (1 / FINE)) * (1 / TOP)
+        part = unit * got[s, :PIECE].astype(jnp.int32).astype(F32)
+        total, sums = (part, notes) if s == 0 else (total + part, sums + notes)
+    tok = sums[1:2]
+    work = DIGIT * sums[2:3] + sums[3:4]
+    everywhere = sums[4:5] + MIDDLE * got.shape[0]
+    qsum = sums[5:6] + (sums[6:7] + sums[7:8] * (1 / DIGIT)) * (1 / DIGIT)
     rate = outer_rate * groups * work / (tok * everywhere)
     for k in range(QUAD):
 
@@ -136,7 +155,7 @@
         def _(k=k):
             mine = own_parts(slow[0, 0], k)
             tile = mine[0] + rate * (total[:ROWS] - qsum * mine[0])
-            rest = mine[1] + rate * (total[ROWS:PIECE] - qsum * mine[1])
+            rest = mine[1] + rate * (total[ROWS:] - qsum * mine[1])
             new_slow[0, 0] = own_block(tile, rest, k)
             for i in range(copies.shape[0]):
                 copies[i, :ROWS] = tile.astype(BF16)
@@ -216,7 +235,7 @@
         input_output_aliases={3: 0},
     )(token_counts, step_counts, experts, pieces)
     got = swap(pieces.reshape(near, *shape[2:]), NEAR)
-    coded = call(near_sum_kernel, struct((nzh, PIECE + FAR_NOTES, LANES), F32))(got)
+    coded = call(near_sum_kernel, struct((nzh, PIECE + FAR_NOTES, LANES), jnp.int16))(got)
     got = swap(coded, "zh")
     new_slow, copies = call(
         lambda *refs: refresh_kernel(groups, *refs),

time: 136 us -> 126 us (0.926)
  waiting for transfers between devices: 32.1 us -> 21.5 us
    all_to_all x2, waiting for transfers between devices: 30.1 us -> 19.5 us  [swap(): return lax.all_to_all(pieces, axis, split_axis=0, concat_axis=0, tiled=True)]
where the time goes in v3:
time: 126 us; the launch traced here: 125 us
  blocking collectives  68.9 us (55%)
  starting transfers between devices  25.6 us (20%)
  waiting for transfers between devices  21.5 us (17%)
  Pallas kernels  4.88 us (4%)
  local copies, waits for them, and re-layouts  2.21 us (2%)
  between operations  1.97 us (2%)
    all_to_all x3, blocking collectives, swap(): return lax.all_to_all(pieces, axis, split_axis=0, concat_axis=0, tiled=True)  68.9 us
    all_to_all x2, waiting for transfers between devices, swap(): return lax.all_to_all(pieces, axis, split_axis=0, concat_axis=0, tiled=True)  19.5 us
    all_to_all x2, starting transfers between devices, swap(): return lax.all_to_all(pieces, axis, split_axis=0, concat_axis=0, tiled=True)  19.4 us
    ppermute x1, starting transfers between devices, shards(): other = lax.ppermute(own, 'c', [(0, 1), (1, 0)])  6.23 us
  transfers between devices with their start and end apart: 3, of which 3 were waited for; matrix products, arithmetic and copies ran while one was open for 0% of the time, Pallas kernels for 0%

profile of v3, /device:TPU:1, one launch (start us, length us, event | category | flops | bytes accessed | tf_op | source)
XLA Modules:
  0.0 125.1 jit_solution(5677686976112291006)
XLA Ops:
  1.3 0.6 broadcast_in_dim.17
  1.9 5.9 %all-to-all-start = ((s32[8,1,1]{2,1,0:T(1,128)}), s32[8,1,1]{2,1,0:T(1,128)S(1)}, u32[]{:S(2)}, u32[]{:S(2)}) async-start(s32[8,1,1]{2,1,0:T(1,128)} %broadcast_in_dim.17), calls=%async_computation | async-start | bytes 8192 | tf_op jit(solution)/shard_map/all_to_all | solution.py:200
  8.5 0.0 copy-start
  8.5 1.5 %copy-done = bf16[1,1,1,64,14336]{4,3,2,1,0:T(8,128)(2,1)S(1)} copy-done((bf16[1,1,1,64,14336]{4,3,2,1,0:T(8,128)(2,1)S(1)}, bf16[1,1,1,64,14336]{4,3,2,1,0:T(8,128)(2,1)}, u32[]{:S(2)}) %copy-start) | copy-done | bytes 1835032
  10.0 0.6 shard_map.59._
  10.6 2.2 %all-to-all-done = s32[8,1,1]{2,1,0:T(1,128)S(1)} async-done(((s32[8,1,1]{2,1,0:T(1,128)}), s32[8,1,1]{2,1,0:T(1,128)S(1)}, u32[]{:S(2)}, u32[]{:S(2)}) %all-to-all-start) | async-done | bytes 64 | tf_op jit(solution)/shard_map/all_to_all | solution.py:200
  12.7 0.7 shard_map.60
  13.5 32.8 %all_to_all.28.got = bf16[8,912,128]{2,1,0:T(8,128)(2,1)S(1)} all-to-all(bf16[8,912,128]{2,1,0:T(8,128)(2,1)S(1)} %bitcast.10), channel_id=1, replica_groups=mesh['expert'=8,'x'=2,'zh'=8,'zl'=2,'c'=2] {'x','zl','c'}, dimensions={0} | all-to-all | bytes 3735552 | tf_op jit(solution)/shard_map/all_to_all | solution.py:200
  46.3 0.0 copy-start.1
  46.3 1.2 shard_map.61
  47.4 13.4 %all-to-all-start.2 = ((s16[8,120,128]{2,1,0:T(8,128)(2,1)}), s16[8,120,128]{2,1,0:T(8,128)(2,1)S(1)}, u32[]{:S(2)}, u32[]{:S(2)}) async-start(s16[8,120,128]{2,1,0:T(8,128)(2,1)} %shard_map.61), calls=%async_computation.2 | async-start | bytes 491520 | tf_op jit(solution)/shard_map/all_to_all | solution.py:200
  60.9 17.3 %all-to-all-done.2.refs_1_ = s16[8,120,128]{2,1,0:T(8,128)(2,1)S(1)} async-done(((s16[8,120,128]{2,1,0:T(8,128)(2,1)}), s16[8,120,128]{2,1,0:T(8,128)(2,1)S(1)}, u32[]{:S(2)}, u32[]{:S(2)}) %all-to-all-start.2) | async-done | bytes 245792 | tf_op jit(solution)/shard_map/all_to_all | solution.py:200
  78.2 0.0 copy-done.1
  78.2 1.0 shard_map.62
  79.2 22.8 %all_to_all.29 = bf16[8,112,128]{2,1,0:T(8,128)(2,1)S(1)} all-to-all(bf16[8,112,128]{2,1,0:T(8,128)(2,1)S(1)} %get-tuple-element.5), channel_id=1, replica_groups=mesh['expert'=8,'x'=2,'zh'=8,'zl'=2,'c'=2] {'zh'}, dimensions={0} | all-to-all | bytes 458752 | tf_op jit(solution)/shard_map/all_to_all | solution.py:200
  101.9 0.1 broadcast_in_dim.18
  102.1 13.3 %all_to_all.30 = bf16[4,8,112,128]{3,2,1,0:T(8,128)(2,1)S(1)} all-to-all(bf16[4,8,112,128]{3,2,1,0:T(8,128)(2,1)S(1)} %broadcast_in_dim.18), channel_id=1, replica_groups=mesh['expert'=8,'x'=2,'zh'=8,'zl'=2,'c'=2] {'x','zl'}, dimensions={0} | all-to-all | bytes 1835008 | tf_op jit(solution)/shard_map/all_to_all | solution.py:200
  115.3 6.2 %collective-permute-start = (bf16[4,8,112,128]{3,2,1,0:T(8,128)(2,1)S(1)}, bf16[4,8,112,128]{3,2,1,0:T(8,128)(2,1)S(1)}, u32[]{:S(2)}, u32[]{:S(2)}) collective-permute-start(bf16[4,8,112,128]{3,2,1,0:T(8,128)(2,1)S(1)} %all_to_all.30), channel_id=1, source_target_pairs={{0,1},{1,0},{2,3},{3,2},{4,5},{5,4},{6,7},{7,6},{8,9},{9,8},{10,11... | collective-permute-start | bytes 2752520 | tf_op jit(solution)/shard_map/ppermute | solution.py:249
  121.6 2.1 %collective-permute-done = bf16[4,8,112,128]{3,2,1,0:T(8,128)(2,1)S(1)} collective-permute-done((bf16[4,8,112,128]{3,2,1,0:T(8,128)(2,1)S(1)}, bf16[4,8,112,128]{3,2,1,0:T(8,128)(2,1)S(1)}, u32[]{:S(2)}, u32[]{:S(2)}) %collective-permute-start) | collective-permute-done | bytes 917536 | tf_op jit(solution)/shard_map/ppermute | solution.py:249
  123.7 1.4 %shard_map.63 = bf16[64,14336]{1,0:T(8,128)(2,1)} custom-call(s32[1,1]{1,0:T(1,128)} %bitcast.5.core, bf16[2,2,8,112,128]{4,3,2,1,0:T(8,128)(2,1)S(1)} %bitcast.11, bf16[2,2,8,112,128]{4,3,2,1,0:T(8,128)(2,1)S(1)} %bitcast.13), custom_call_target="tpu_custom_call" | custom-call | tf_op jit(solution)/shard_map/pallas_call | solution.py:251
Async XLA Ops:
  1.9 10.9 %all-to-all-start = ((s32[8,1,1]{2,1,0:T(1,128)}), s32[8,1,1]{2,1,0:T(1,128)S(1)}, u32[]{:S(2)}, u32[]{:S(2)}) async-start(s32[8,1,1]{2,1,0:T(1,128)} %broadcast_in_dim.17), calls=%async_computation | async-start | bytes 8192 | tf_op jit(solution)/shard_map/all_to_all | solution.py:200
  8.5 1.5 %copy-start = (bf16[1,1,1,64,14336]{4,3,2,1,0:T(8,128)(2,1)S(1)}, bf16[1,1,1,64,14336]{4,3,2,1,0:T(8,128)(2,1)}, u32[]{:S(2)}) copy-start(bf16[1,1,1,64,14336]{4,3,2,1,0:T(8,128)(2,1)} %param.4) | copy-start | bytes 5505028
  46.3 31.9 %copy-start.1 = (f32[1,1,64,224]{3,2,1,0:T(8,128)S(1)}, f32[1,1,64,224]{3,2,1,0:T(8,128)}, u32[]{:S(2)}) copy-start(f32[1,1,64,224]{3,2,1,0:T(8,128)} %refs_2_.1) | copy-start | bytes 172036
  47.4 30.7 %all-to-all-start.2 = ((s16[8,120,128]{2,1,0:T(8,128)(2,1)}), s16[8,120,128]{2,1,0:T(8,128)(2,1)S(1)}, u32[]{:S(2)}, u32[]{:S(2)}) async-start(s16[8,120,128]{2,1,0:T(8,128)(2,1)} %shard_map.61), calls=%async_computation.2 | async-start | bytes 491520 | tf_op jit(solution)/shard_map/all_to_all | solution.py:200
  115.3 8.3 %collective-permute-start = (bf16[4,8,112,128]{3,2,1,0:T(8,128)(2,1)S(1)}, bf16[4,8,112,128]{3,2,1,0:T(8,128)(2,1)S(1)}, u32[]{:S(2)}, u32[]{:S(2)}) collective-permute-start(bf16[4,8,112,128]{3,2,1,0:T(8,128)(2,1)S(1)} %all_to_all.30), channel_id=1, source_target_pairs={{0,1},{1,0},{2,3},{3,2},{4,5},{5,4},{6,7},{7,6},{8,9},{9,8},{10,11... | collective-permute-start | bytes 2752520 | tf_op jit(solution)/shard_map/ppermute | solution.py:249

commit v4 on v3

--- a/solution.py
+++ b/solution.py
@@ -10,7 +10,6 @@
 BF16 = jnp.bfloat16
 
 SHARD = ("x", "zh", "zl", "c")
-NEAR = ("x", "zl", "c")
 
 outer_rate = 0.7
 
@@ -25,7 +24,7 @@
 
 PIECE = ROWS + REST
 
-NEAR_NOTES = 16
+NOTES = 16
 FAR_NOTES = 8
 TOP = 32767.0
 DIGIT = 4096.0
@@ -80,74 +79,128 @@
     return high.astype(F32), (count - 256 * high).astype(F32)
 
 
-def sort_kernel(fast, out):
+def in_rows(values, rows):
+    row = lax.broadcasted_iota(jnp.int32, (rows, LANES), 0)
+    out = jnp.zeros((rows, LANES), F32)
+    for i, value in enumerate(values):
+        out = jnp.where(row == i, value, out)
+    return out
+
+
+def digits(value):
+    whole = jnp.floor(value)
+    part = (value - whole) * DIGIT
+    digit = jnp.floor(part)
+    return whole, digit, jnp.floor((part - digit) * DIGIT)
+
+
+def from_digits(whole, first, second):
+    return whole + (first + second * (1 / DIGIT)) * (1 / DIGIT)
+
+
+def coded(total):
+    largest = jnp.maximum(jnp.max(jnp.abs(total), axis=0, keepdims=True), 1e-30)
+    level = jnp.ceil(FINE * jnp.log2(largest))
+    units = jnp.clip(jnp.round(total * (TOP * jnp.exp2(level * (-1 / FINE)))), -TOP, TOP)
+    return short(units), level
+
+
+def short(values):
+    return values.astype(jnp.int32).astype(jnp.int16)
+
+
+def wide(values):
+    return values.astype(jnp.int32).astype(F32)
+
+
+def decoded(units, level):
+    return (jnp.exp2(level * (1 / FINE)) * (1 / TOP)) * wide(units)
+
+
+def sort_kernel(core, tokens, steps, fast, keep, give):
+    n_zl = keep.shape[1]
     group = lane_group((ROWS, LANES))
-    for zh in range(fast.shape[1] // WIDE):
-        lanes = [slice(zh * WIDE + i * LANES, zh * WIDE + (i + 1) * LANES) for i in range(2 * QUAD - 1)]
-        odd = [fast[:, at].astype(F32) for at in lanes[1::2]]
-        for k in range(QUAD):
-            if k == 0:
-                res = odd[0]
-            elif k == QUAD - 1:
-                res = odd[-1]
-            else:
-                res = jnp.where(group >= QUAD - k, odd[k - 1], odd[k])
-            at = zh * PIECE
-            out[0, k, at : at + ROWS] = fast[:, lanes[2 * k]]
-            out[0, k, at + ROWS : at + PIECE] = folded(res, k).astype(BF16)
-
-
-def notes_kernel(tokens, steps, experts, _, out):
-    row = lax.broadcasted_iota(jnp.int32, (NEAR_NOTES, LANES), 0)
-    notes = jnp.zeros((NEAR_NOTES, LANES), F32)
-    for i, count in enumerate((tokens[0, 0], steps[0, 0], sum(experts[e, 0] for e in range(experts.shape[0])))):
-        for j, value in enumerate(as_bytes(count)):
-            notes = jnp.where(row == 2 * i + j, value, notes)
-    for k in range(out.shape[1]):
-        out[0, k] = notes.astype(BF16)
+
+    def body(sides):
+        for g in range(fast.shape[1] // WIDE):
+            x, zh = divmod(g, keep.shape[2])
+            lanes = [slice(g * WIDE + i * LANES, g * WIDE + (i + 1) * LANES) for i in range(2 * QUAD - 1)]
+            odd = [fast[:, at].astype(F32) for at in lanes[1::2]]
+            for k in range(QUAD):
+                if k == 0:
+                    res = odd[0]
+                elif k == QUAD - 1:
+                    res = odd[-1]
+                else:
+                    res = jnp.where(group >= QUAD - k, odd[k - 1], odd[k])
+                zl, c = divmod(k, QUAD // n_zl)
+                sides[c](x, zl, zh, fast[:, lanes[2 * k]], folded(res, k).astype(BF16))
+
+    def kept(x, zl, zh, tile, rest):
+        keep[x, zl, zh, :ROWS] = tile
+        keep[x, zl, zh, ROWS:] = rest
+
+    def given(x, zl, zh, tile, rest):
+        at = ((x * n_zl + zl) * keep.shape[2] + zh) * PIECE
+        give[at : at + ROWS] = tile
+        give[at + ROWS : at + PIECE] = rest
+
+    @pl.when(core[0, 0] == 0)
+    def _():
+        body((kept, given))
+
+    @pl.when(core[0, 0] != 0)
+    def _():
+        body((given, kept))
+
+    notes = in_rows((*as_bytes(tokens[0, 0]), *as_bytes(steps[0, 0])), NOTES)
+    give[give.shape[0] - NOTES :] = notes.astype(BF16)
+
+
+def pair_sum_kernel(tokens, steps, experts, keep, got, out):
+    at = got.shape[0] - NOTES
+    notes = got[at:].astype(F32)
+    theirs = [256 * notes[2 * i : 2 * i + 1] + notes[2 * i + 1 : 2 * i + 2] for i in range(2)]
+    mine = [jnp.full((1, LANES), count[0, 0].astype(F32)) for count in (tokens, steps)]
+    share, other = mine[0] / mine[1], theirs[0] / theirs[1]
+    everywhere = sum(experts[e, 0] for e in range(experts.shape[0])).astype(F32)
+    counts = (mine[0] + theirs[0], mine[0] * mine[1] + theirs[0] * theirs[1], *digits(share + other), everywhere)
+    n_zl, n_zh = keep.shape[1:3]
+    for d in range(out.shape[0]):
+        levels = []
+        for zh in range(n_zh):
+            at = (d * n_zh + zh) * PIECE
+            mix = share * keep[d // n_zl, d % n_zl, zh].astype(F32) + other * got[at : at + PIECE].astype(F32)
+            out[d, zh * PIECE : (zh + 1) * PIECE], level = coded(mix)
+            levels.append(level)
+        out[d, n_zh * PIECE :] = short(in_rows((*levels, *counts), NOTES))
 
 
 def near_sum_kernel(got, out):
-    n, rows = got.shape[0], got.shape[1] - NEAR_NOTES
-    notes = [got[s, rows:].astype(F32) for s in range(n)]
-    counts = [[256 * v[2 * i : 2 * i + 1] + v[2 * i + 1 : 2 * i + 2] for i in range(3)] for v in notes]
-    shares = [tokens / steps for tokens, steps, _ in counts]
-    tok = sum(tokens for tokens, _, _ in counts)
-    work = sum(tokens * steps for tokens, steps, _ in counts)
-    everywhere = sum(group for _, _, group in counts)
-    qsum = sum(shares)
-    whole = jnp.floor(qsum)
-    part = (qsum - whole) * DIGIT
-    digit = jnp.floor(part)
+    n, n_zh = got.shape[0], out.shape[0]
+    notes = [wide(got[s, n_zh * PIECE :]) for s in range(n)]
+    tok, work, *qsum, everywhere = (sum(v[n_zh + i : n_zh + i + 1] for v in notes) for i in range(6))
     high = jnp.floor(work / DIGIT)
-    fixed = (tok, high, work - DIGIT * high, everywhere - MIDDLE, whole, digit, jnp.floor((part - digit) * DIGIT))
-    row = lax.broadcasted_iota(jnp.int32, (FAR_NOTES, LANES), 0)
-    far = jnp.zeros((FAR_NOTES, LANES), F32)
-    for i, value in enumerate(fixed):
-        far = jnp.where(row == i + 1, value, far)
-    for zh in range(out.shape[0]):
+    far = (tok, high, work - DIGIT * high, everywhere - MIDDLE, *digits(from_digits(*qsum)))
+    for zh in range(n_zh):
         piece = slice(zh * PIECE, (zh + 1) * PIECE)
-        total = shares[0] * got[0, piece].astype(F32)
+        total = decoded(got[0, piece], notes[0][zh : zh + 1])
         for s in range(1, n):
-            total = total + shares[s] * got[s, piece].astype(F32)
-        largest = jnp.maximum(jnp.max(jnp.abs(total), axis=0, keepdims=True), 1e-30)
-        level = jnp.ceil(FINE * jnp.log2(largest))
-        coded = jnp.clip(jnp.round(total * (TOP * jnp.exp2(level * (-1 / FINE)))), -TOP, TOP)
-        out[zh, :PIECE] = coded.astype(jnp.int32).astype(jnp.int16)
-        out[zh, PIECE:] = jnp.where(row == 0, level, far).astype(jnp.int32).astype(jnp.int16)
+            total = total + decoded(got[s, piece], notes[s][zh : zh + 1])
+        out[zh, :PIECE], level = coded(total)
+        out[zh, PIECE:] = short(in_rows((level, *far), FAR_NOTES))
 
 
 def refresh_kernel(groups, place, got, slow, new_slow, copies):
     total = sums = None
     for s in range(got.shape[0]):
-        notes = got[s, PIECE:].astype(jnp.int32).astype(F32)
-        unit = jnp.exp2(notes[0:1] * (1 / FINE)) * (1 / TOP)
-        part = unit * got[s, :PIECE].astype(jnp.int32).astype(F32)
+        notes = wide(got[s, PIECE:])
+        part = decoded(got[s, :PIECE], notes[0:1])
         total, sums = (part, notes) if s == 0 else (total + part, sums + notes)
     tok = sums[1:2]
     work = DIGIT * sums[2:3] + sums[3:4]
     everywhere = sums[4:5] + MIDDLE * got.shape[0]
-    qsum = sums[5:6] + (sums[6:7] + sums[7:8] * (1 / DIGIT)) * (1 / DIGIT)
+    qsum = from_digits(sums[5:6], sums[6:7], sums[7:8])
     rate = outer_rate * groups * work / (tok * everywhere)
     for k in range(QUAD):
 
@@ -211,7 +264,7 @@
 def shards(fast_weights, slow_weights, step_counts, token_counts):
     size = {a: lax.axis_size(a) for a in SHARD}
     groups = lax.axis_size("expert")
-    nx, nzh, near = size["x"], size["zh"], size["x"] * size["zl"] * size["c"]
+    nx, nzh = size["x"], size["zh"]
     core = lax.axis_index("c")
     place = scalar(lax.axis_index("zl") * size["c"] + core)
     core = scalar(core)
@@ -223,20 +276,26 @@
     def by_x(*shape):
         return pl.BlockSpec((1, *shape[1:]), lambda x: (x, *(0 for _ in shape[1:])))
 
-    experts = swap(jnp.broadcast_to(token_counts, (groups, 1)), "expert")
-    shape = (nx, QUAD, nzh * PIECE + NEAR_NOTES, LANES)
-    pieces = call(sort_kernel, struct(shape, BF16), grid=(nx,), in_specs=[halves], out_specs=by_x(*shape))(fast)
-    pieces = call(
-        notes_kernel,
-        struct(shape, BF16),
-        grid=(nx,),
-        in_specs=[SCALAR, SCALAR, SCALAR, pl.BlockSpec(memory_space=pl.ANY)],
-        out_specs=pl.BlockSpec((1, QUAD, NEAR_NOTES, LANES), lambda x: (x, 0, shape[2] // NEAR_NOTES - 1, 0)),
-        input_output_aliases={3: 0},
-    )(token_counts, step_counts, experts, pieces)
-    got = swap(pieces.reshape(near, *shape[2:]), NEAR)
-    coded = call(near_sum_kernel, struct((nzh, PIECE + FAR_NOTES, LANES), jnp.int16))(got)
-    got = swap(coded, "zh")
+    plane = nx * size["zl"]
+    spread = jnp.broadcast_to(token_counts, (groups * size["c"], 1))
+    experts = swap(spread, ("expert", "c"))
+    keep, give = call(
+        sort_kernel,
+        (
+            struct((nx, size["zl"], nzh, PIECE, LANES), BF16),
+            struct((plane * nzh * PIECE + NOTES, LANES), BF16),
+        ),
+        in_specs=[SCALAR, SCALAR, SCALAR, WHOLE],
+    )(core, token_counts, step_counts, fast)
+    got = lax.ppermute(give, "c", [(0, 1), (1, 0)])
+    pairs = call(
+        pair_sum_kernel,
+        struct((plane, nzh * PIECE + NOTES, LANES), jnp.int16),
+        in_specs=[SCALAR, SCALAR, SCALAR, WHOLE, WHOLE],
+    )(token_counts, step_counts, experts, keep, got)
+    got = swap(pairs, ("x", "zl"))
+    sums = call(near_sum_kernel, struct((nzh, PIECE + FAR_NOTES, LANES), jnp.int16))(got)
+    got = swap(sums, "zh")
     new_slow, copies = call(
         lambda *refs: refresh_kernel(groups, *refs),
         (struct(slow_weights.shape, F32), struct((nzh, PIECE, LANES), BF16)),
@@ -244,7 +303,6 @@
     )(place, got, slow_weights)
 
     column = swap(copies, "zh")
-    plane = nx * size["zl"]
     own = swap(jnp.broadcast_to(column[None], (plane, *column.shape)), ("x", "zl"))
     other = lax.ppermute(own, "c", [(0, 1), (1, 0)])
     shape = (nx, size["zl"], *column.shape)

time: 126 us -> 117 us (0.929)
  blocking collectives: 68.9 us -> 59.9 us
  starting transfers between devices: 25.6 us -> 28 us
  waiting for transfers between devices: 21.5 us -> 19.4 us
    all_to_all x3 -> x4, blocking collectives: 68.9 us -> 59.9 us  [swap(): return lax.all_to_all(pieces, axis, split_axis=0, concat_axis=0, tiled=True)]
    ppermute x0 -> x1, starting transfers between devices: none -> 8.79 us  [shards(): got = lax.ppermute(give, 'c', [(0, 1), (1, 0)])]
    all_to_all x2 -> x1, starting transfers between devices: 19.4 us -> 13.5 us  [swap(): return lax.all_to_all(pieces, axis, split_axis=0, concat_axis=0, tiled=True)]
    all_to_all x2 -> x1, waiting for transfers between devices: 19.5 us -> 17.3 us  [swap(): return lax.all_to_all(pieces, axis, split_axis=0, concat_axis=0, tiled=True)]
  transfers between devices with their start and end apart: 3 -> 3, of which waited for: 3 -> 2; matrix products, arithmetic and copies ran while one was open for 0% -> 0% of each run, Pallas kernels for 0% -> 0%
where the time goes in v4:
time: 117 us; the launch traced here: 116 us
  blocking collectives  59.9 us (51%)
  starting transfers between devices  28 us (24%)
  waiting for transfers between devices  19.4 us (17%)
  Pallas kernels  5.25 us (4%)
  between operations  1.99 us (2%)
  local copies, waits for them, and re-layouts  1.62 us (1%)
    all_to_all x4, blocking collectives, swap(): return lax.all_to_all(pieces, axis, split_axis=0, concat_axis=0, tiled=True)  59.9 us
    all_to_all x1, waiting for transfers between devices, swap(): return lax.all_to_all(pieces, axis, split_axis=0, concat_axis=0, tiled=True)  17.3 us
    all_to_all x1, starting transfers between devices, swap(): return lax.all_to_all(pieces, axis, split_axis=0, concat_axis=0, tiled=True)  13.5 us
    ppermute x1, starting transfers between devices, shards(): got = lax.ppermute(give, 'c', [(0, 1), (1, 0)])  8.79 us
    ppermute x1, starting transfers between devices, shards(): other = lax.ppermute(own, 'c', [(0, 1), (1, 0)])  5.66 us
  transfers between devices with their start and end apart: 3, of which 2 were waited for; matrix products, arithmetic and copies ran while one was open for 0% of the time, Pallas kernels for 0%

profile of v4, /device:TPU:1, one launch (start us, length us, event | category | flops | bytes accessed | tf_op | source)
XLA Modules:
  0.0 116.2 jit_solution(7738189124511705653)
XLA Ops:
  1.9 0.0 copy-start
  1.9 1.5 %copy-done = bf16[1,1,1,64,14336]{4,3,2,1,0:T(8,128)(2,1)S(1)} copy-done((bf16[1,1,1,64,14336]{4,3,2,1,0:T(8,128)(2,1)S(1)}, bf16[1,1,1,64,14336]{4,3,2,1,0:T(8,128)(2,1)}, u32[]{:S(2)}) %copy-start) | copy-done | bytes 1835032
  3.4 0.4 shard_map.59
  3.9 8.8 %collective-permute-start = (bf16[3600,128]{1,0:T(8,128)(2,1)S(1)}, bf16[3600,128]{1,0:T(8,128)(2,1)S(1)}, u32[]{:S(2)}, u32[]{:S(2)}) collective-permute-start(bf16[3600,128]{1,0:T(8,128)(2,1)S(1)} %get-tuple-element.7), channel_id=1, source_target_pairs={{0,1},{1,0},{2,3},{3,2},{4,5},{5,4},{6,7},{7,6},{8,9},{9,8},{10,11... | collective-permute-start | bytes 2764808 | tf_op jit(solution)/shard_map/ppermute | solution.py:290
  12.7 8.0 %all_to_all.28 = s32[16,1,1]{2,1,0:T(1,128)S(1)} all-to-all(s32[16,1,1]{2,1,0:T(1,128)S(1)} %broadcast_in_dim.17), channel_id=1, replica_groups=mesh['expert'=8,'x'=2,'zh'=8,'zl'=2,'c'=2] {'expert','c'}, dimensions={0} | all-to-all | bytes 128 | tf_op jit(solution)/shard_map/all_to_all | solution.py:253
  20.6 0.0 collective-permute-done.got
  20.7 1.3 %shard_map.60 = s16[4,912,128]{2,1,0:T(8,128)(2,1)S(1)} custom-call(s32[1,1]{1,0:T(1,128)} %copy.10.tokens, s32[1,1]{1,0:T(1,128)S(6)} %copy.9.steps, s32[16,1]{1,0:T(8,128)S(1)} %bitcast.12, bf16[2,2,8,112,128]{4,3,2,1,0:T(8,128)(2,1)S(1)} %get-tuple-element.6.keep, bf16[3600,128]{1,0:T(8,128)(2,1)S(1)} %collective-permute-done.got), custom_call_target="tpu_custom_call" | custom-call | tf_op jit(solution)/shard_map/pallas_call | solution.py:291
  22.0 0.0 copy-start.1
  22.0 16.3 %all_to_all.29.got = s16[4,912,128]{2,1,0:T(8,128)(2,1)S(1)} all-to-all(s16[4,912,128]{2,1,0:T(8,128)(2,1)S(1)} %shard_map.60), channel_id=1, replica_groups=mesh['expert'=8,'x'=2,'zh'=8,'zl'=2,'c'=2] {'x','zl'}, dimensions={0} | all-to-all | bytes 1867776 | tf_op jit(solution)/shard_map/all_to_all | solution.py:253
  38.3 1.0 shard_map.61
  39.4 13.5 %all-to-all-start.2 = ((s16[8,120,128]{2,1,0:T(8,128)(2,1)}), s16[8,120,128]{2,1,0:T(8,128)(2,1)S(1)}, u32[]{:S(2)}, u32[]{:S(2)}) async-start(s16[8,120,128]{2,1,0:T(8,128)(2,1)} %shard_map.61), calls=%async_computation.2 | async-start | bytes 491520 | tf_op jit(solution)/shard_map/all_to_all | solution.py:253
  52.9 17.3 %all-to-all-done.2.refs_1_ = s16[8,120,128]{2,1,0:T(8,128)(2,1)S(1)} async-done(((s16[8,120,128]{2,1,0:T(8,128)(2,1)}), s16[8,120,128]{2,1,0:T(8,128)(2,1)S(1)}, u32[]{:S(2)}, u32[]{:S(2)}) %all-to-all-start.2) | async-done | bytes 245792 | tf_op jit(solution)/shard_map/all_to_all | solution.py:253
  70.2 0.0 copy-done.1
  70.2 1.0 shard_map.62
  71.2 20.6 %all_to_all.30 = bf16[8,112,128]{2,1,0:T(8,128)(2,1)S(1)} all-to-all(bf16[8,112,128]{2,1,0:T(8,128)(2,1)S(1)} %get-tuple-element.9), channel_id=1, replica_groups=mesh['expert'=8,'x'=2,'zh'=8,'zl'=2,'c'=2] {'zh'}, dimensions={0} | all-to-all | bytes 458752 | tf_op jit(solution)/shard_map/all_to_all | solution.py:253
  91.8 0.1 broadcast_in_dim.18
  91.9 15.1 %all_to_all.31 = bf16[4,8,112,128]{3,2,1,0:T(8,128)(2,1)S(1)} all-to-all(bf16[4,8,112,128]{3,2,1,0:T(8,128)(2,1)S(1)} %broadcast_in_dim.18), channel_id=1, replica_groups=mesh['expert'=8,'x'=2,'zh'=8,'zl'=2,'c'=2] {'x','zl'}, dimensions={0} | all-to-all | bytes 1835008 | tf_op jit(solution)/shard_map/all_to_all | solution.py:253
  107.0 5.7 %collective-permute-start.1 = (bf16[4,8,112,128]{3,2,1,0:T(8,128)(2,1)S(1)}, bf16[4,8,112,128]{3,2,1,0:T(8,128)(2,1)S(1)}, u32[]{:S(2)}, u32[]{:S(2)}) collective-permute-start(bf16[4,8,112,128]{3,2,1,0:T(8,128)(2,1)S(1)} %all_to_all.31), channel_id=1, source_target_pairs={{0,1},{1,0},{2,3},{3,2},{4,5},{5,4},{6,7},{7,6},{8,9},{9,8},{10,11... | collective-permute-start | bytes 2752520 | tf_op jit(solution)/shard_map/ppermute | solution.py:307
  112.6 2.1 %collective-permute-done.1 = bf16[4,8,112,128]{3,2,1,0:T(8,128)(2,1)S(1)} collective-permute-done((bf16[4,8,112,128]{3,2,1,0:T(8,128)(2,1)S(1)}, bf16[4,8,112,128]{3,2,1,0:T(8,128)(2,1)S(1)}, u32[]{:S(2)}, u32[]{:S(2)}) %collective-permute-start.1) | collective-permute-done | bytes 917536 | tf_op jit(solution)/shard_map/ppermute | solution.py:307
  114.7 1.4 %shard_map.63 = bf16[64,14336]{1,0:T(8,128)(2,1)} custom-call(s32[1,1]{1,0:T(1,128)} %bitcast.3.core, bf16[2,2,8,112,128]{4,3,2,1,0:T(8,128)(2,1)S(1)} %bitcast.9, bf16[2,2,8,112,128]{4,3,2,1,0:T(8,128)(2,1)S(1)} %bitcast.11), custom_call_target="tpu_custom_call" | custom-call | tf_op jit(solution)/shard_map/pallas_call | solution.py:309
  (1 shorter events, 0.0 us)
Async XLA Ops:
  1.9 1.5 %copy-start = (bf16[1,1,1,64,14336]{4,3,2,1,0:T(8,128)(2,1)S(1)}, bf16[1,1,1,64,14336]{4,3,2,1,0:T(8,128)(2,1)}, u32[]{:S(2)}) copy-start(bf16[1,1,1,64,14336]{4,3,2,1,0:T(8,128)(2,1)} %param.4) | copy-start | bytes 5505028
  3.9 16.8 %collective-permute-start = (bf16[3600,128]{1,0:T(8,128)(2,1)S(1)}, bf16[3600,128]{1,0:T(8,128)(2,1)S(1)}, u32[]{:S(2)}, u32[]{:S(2)}) collective-permute-start(bf16[3600,128]{1,0:T(8,128)(2,1)S(1)} %get-tuple-element.7), channel_id=1, source_target_pairs={{0,1},{1,0},{2,3},{3,2},{4,5},{5,4},{6,7},{7,6},{8,9},{9,8},{10,11... | collective-permute-start | bytes 2764808 | tf_op jit(solution)/shard_map/ppermute | solution.py:290
  22.0 48.2 %copy-start.1 = (f32[1,1,64,224]{3,2,1,0:T(8,128)S(1)}, f32[1,1,64,224]{3,2,1,0:T(8,128)}, u32[]{:S(2)}) copy-start(f32[1,1,64,224]{3,2,1,0:T(8,128)} %refs_2_.1) | copy-start | bytes 172036
  39.4 30.8 %all-to-all-start.2 = ((s16[8,120,128]{2,1,0:T(8,128)(2,1)}), s16[8,120,128]{2,1,0:T(8,128)(2,1)S(1)}, u32[]{:S(2)}, u32[]{:S(2)}) async-start(s16[8,120,128]{2,1,0:T(8,128)(2,1)} %shard_map.61), calls=%async_computation.2 | async-start | bytes 491520 | tf_op jit(solution)/shard_map/all_to_all | solution.py:253
  107.0 7.7 %collective-permute-start.1 = (bf16[4,8,112,128]{3,2,1,0:T(8,128)(2,1)S(1)}, bf16[4,8,112,128]{3,2,1,0:T(8,128)(2,1)S(1)}, u32[]{:S(2)}, u32[]{:S(2)}) collective-permute-start(bf16[4,8,112,128]{3,2,1,0:T(8,128)(2,1)S(1)} %all_to_all.31), channel_id=1, source_target_pairs={{0,1},{1,0},{2,3},{3,2},{4,5},{5,4},{6,7},{7,6},{8,9},{9,8},{10,11... | collective-permute-start | bytes 2752520 | tf_op jit(solution)/shard_map/ppermute | solution.py:307

commit v5 on v4

--- a/solution.py
+++ b/solution.py
@@ -10,6 +10,8 @@
 BF16 = jnp.bfloat16
 
 SHARD = ("x", "zh", "zl", "c")
+
+FAR = ("zh", "zl", "c")
 
 outer_rate = 0.7
 
@@ -32,6 +34,22 @@
 FINE = 8.0
 
 
+SPREAD = (0, 4, 2, 6, 1, 5, 3, 7)
+
+
+def member(at, k):
+    return SPREAD[(at + 2 * k) % len(SPREAD)]
+
+
+def position(zh, k):
+    return (SPREAD[zh] - 2 * k) % len(SPREAD)
+
+
+def swap_far(pieces):
+    groups = [[member(at, k) * QUAD + k for at in range(len(SPREAD))] for k in range(QUAD)]
+    return lax.all_to_all(pieces, FAR, split_axis=0, concat_axis=0, tiled=True, axis_index_groups=groups)
+
+
 def lane_group(shape):
     return lax.broadcasted_iota(jnp.int32, shape, 1) // STEP
 
@@ -74,9 +92,8 @@
     return jnp.concatenate([p for p in parts if p.shape[1]], axis=1)
 
 
-def as_bytes(count):
-    high = count // 256
-    return high.astype(F32), (count - 256 * high).astype(F32)
+def own_place():
+    return lax.axis_index("zl") * 2 + lax.axis_index("c")
 
 
 def in_rows(values, rows):
@@ -117,7 +134,7 @@
     return (jnp.exp2(level * (1 / FINE)) * (1 / TOP)) * wide(units)
 
 
-def sort_kernel(core, tokens, steps, fast, keep, give):
+def sort_kernel(fast, keep, give):
     n_zl = keep.shape[1]
     group = lane_group((ROWS, LANES))
 
@@ -134,49 +151,41 @@
                 else:
                     res = jnp.where(group >= QUAD - k, odd[k - 1], odd[k])
                 zl, c = divmod(k, QUAD // n_zl)
-                sides[c](x, zl, zh, fast[:, lanes[2 * k]], folded(res, k).astype(BF16))
-
-    def kept(x, zl, zh, tile, rest):
-        keep[x, zl, zh, :ROWS] = tile
-        keep[x, zl, zh, ROWS:] = rest
-
-    def given(x, zl, zh, tile, rest):
-        at = ((x * n_zl + zl) * keep.shape[2] + zh) * PIECE
-        give[at : at + ROWS] = tile
-        give[at + ROWS : at + PIECE] = rest
-
-    @pl.when(core[0, 0] == 0)
+                sides[c][x, zl, zh, :ROWS] = fast[:, lanes[2 * k]]
+                sides[c][x, zl, zh, ROWS:] = folded(res, k).astype(BF16)
+
+    core = lax.axis_index("c")
+
+    @pl.when(core == 0)
     def _():
-        body((kept, given))
-
-    @pl.when(core[0, 0] != 0)
+        body((keep, give))
+
+    @pl.when(core != 0)
     def _():
-        body((given, kept))
-
-    notes = in_rows((*as_bytes(tokens[0, 0]), *as_bytes(steps[0, 0])), NOTES)
-    give[give.shape[0] - NOTES :] = notes.astype(BF16)
-
-
-def pair_sum_kernel(tokens, steps, experts, keep, got, out):
-    at = got.shape[0] - NOTES
-    notes = got[at:].astype(F32)
-    theirs = [256 * notes[2 * i : 2 * i + 1] + notes[2 * i + 1 : 2 * i + 2] for i in range(2)]
-    mine = [jnp.full((1, LANES), count[0, 0].astype(F32)) for count in (tokens, steps)]
-    share, other = mine[0] / mine[1], theirs[0] / theirs[1]
-    everywhere = sum(experts[e, 0] for e in range(experts.shape[0])).astype(F32)
-    counts = (mine[0] + theirs[0], mine[0] * mine[1] + theirs[0] * theirs[1], *digits(share + other), everywhere)
+        body((give, keep))
+
+
+def pair_sum_kernel(counts, keep, got, out):
+    core = lax.axis_index("c")
+    pair = lax.axis_index("expert") * 2
+    of_core = [[counts[pair + c, i].astype(F32) for i in range(2)] for c in (core, 1 - core)]
+    (tokens, steps), (tokens_2, steps_2) = ([jnp.full((1, LANES), v) for v in values] for values in of_core)
+    share, other = tokens / steps, tokens_2 / steps_2
+    everywhere = sum(counts[i, 0] for i in range(counts.shape[0])).astype(F32)
+    sums = (tokens + tokens_2, tokens * steps + tokens_2 * steps_2, *digits(share + other), everywhere)
     n_zl, n_zh = keep.shape[1:3]
     for d in range(out.shape[0]):
         levels = []
+        at = divmod(d, n_zl)
         for zh in range(n_zh):
-            at = (d * n_zh + zh) * PIECE
-            mix = share * keep[d // n_zl, d % n_zl, zh].astype(F32) + other * got[at : at + PIECE].astype(F32)
+            mix = share * keep[*at, zh].astype(F32) + other * got[*at, zh].astype(F32)
             out[d, zh * PIECE : (zh + 1) * PIECE], level = coded(mix)
             levels.append(level)
-        out[d, n_zh * PIECE :] = short(in_rows((*levels, *counts), NOTES))
+        out[d, n_zh * PIECE :] = short(in_rows((*levels, *sums), NOTES))
 
 
 def near_sum_kernel(got, out):
+    place = own_place()
     n, n_zh = got.shape[0], out.shape[0]
     notes = [wide(got[s, n_zh * PIECE :]) for s in range(n)]
     tok, work, *qsum, everywhere = (sum(v[n_zh + i : n_zh + i + 1] for v in notes) for i in range(6))
@@ -187,11 +196,12 @@
         total = decoded(got[0, piece], notes[0][zh : zh + 1])
         for s in range(1, n):
             total = total + decoded(got[s, piece], notes[s][zh : zh + 1])
-        out[zh, :PIECE], level = coded(total)
-        out[zh, PIECE:] = short(in_rows((level, *far), FAR_NOTES))
-
-
-def refresh_kernel(groups, place, got, slow, new_slow, copies):
+        to = (SPREAD[zh] + (n_zh - 2) * place) % n_zh
+        out[to, :PIECE], level = coded(total)
+        out[to, PIECE:] = short(in_rows((level, *far), FAR_NOTES))
+
+
+def refresh_kernel(groups, got, slow, new_slow, copies):
     total = sums = None
     for s in range(got.shape[0]):
         notes = wide(got[s, PIECE:])
@@ -202,9 +212,10 @@
     everywhere = sums[4:5] + MIDDLE * got.shape[0]
     qsum = from_digits(sums[5:6], sums[6:7], sums[7:8])
     rate = outer_rate * groups * work / (tok * everywhere)
+    place = own_place()
     for k in range(QUAD):
 
-        @pl.when(place[0, 0] == k)
+        @pl.when(place == k)
         def _(k=k):
             mine = own_parts(slow[0, 0], k)
             tile = mine[0] + rate * (total[:ROWS] - qsum * mine[0])
@@ -215,25 +226,20 @@
                 copies[i, ROWS:] = rest.astype(BF16)
 
 
-def lay_out_kernel(core, own, other, out):
-    def body(pieces):
-        group = lane_group((ROWS, LANES))
-        for zh in range(own.shape[2]):
-            at = zh * WIDE
-            for k in range(QUAD):
-                out[:, at + 2 * k * LANES : at + (2 * k + 1) * LANES] = pieces[k % 2][0, k // 2, zh, :ROWS]
-            res = [unfolded(pieces[k % 2][0, k // 2, zh, ROWS:].astype(F32), k) for k in range(QUAD)]
-            for k in range(QUAD - 1):
-                odd = jnp.where(group < QUAD - 1 - k, res[k], res[k + 1])
-                out[:, at + (2 * k + 1) * LANES : at + (2 * k + 2) * LANES] = odd.astype(BF16)
-
-    @pl.when(core[0, 0] == 0)
-    def _():
-        body((own, other))
-
-    @pl.when(core[0, 0] != 0)
-    def _():
-        body((other, own))
+def lay_out_kernel(pieces, out):
+    n_c, n_zl, n_zh = pieces.shape[0], pieces.shape[2], pieces.shape[3]
+    group = lane_group((ROWS, LANES))
+    for zh in range(n_zh):
+        at = zh * WIDE
+        res = []
+        for k in range(QUAD):
+            zl, c = divmod(k, n_c)
+            piece = pieces.at[c, 0, zl, position(zh, k)]
+            out[:, at + 2 * k * LANES : at + (2 * k + 1) * LANES] = piece[:ROWS]
+            res.append(unfolded(piece[ROWS:].astype(F32), k))
+        for k in range(QUAD - 1):
+            odd = jnp.where(group < QUAD - 1 - k, res[k], res[k + 1])
+            out[:, at + (2 * k + 1) * LANES : at + (2 * k + 2) * LANES] = odd.astype(BF16)
 
 
 def call(kernel, out_shape, **more):
@@ -257,62 +263,43 @@
 WHOLE = pl.BlockSpec(memory_space=pltpu.VMEM)
 
 
-def scalar(value):
-    return value.astype(jnp.int32).reshape(1, 1)
-
-
 def shards(fast_weights, slow_weights, step_counts, token_counts):
     size = {a: lax.axis_size(a) for a in SHARD}
     groups = lax.axis_size("expert")
     nx, nzh = size["x"], size["zh"]
-    core = lax.axis_index("c")
-    place = scalar(lax.axis_index("zl") * size["c"] + core)
-    core = scalar(core)
-
     fast = fast_weights[0, 0, 0]
     half = fast.shape[1] // nx
     halves = pl.BlockSpec((ROWS, half), lambda x: (0, x))
 
-    def by_x(*shape):
-        return pl.BlockSpec((1, *shape[1:]), lambda x: (x, *(0 for _ in shape[1:])))
-
     plane = nx * size["zl"]
-    spread = jnp.broadcast_to(token_counts, (groups * size["c"], 1))
-    experts = swap(spread, ("expert", "c"))
-    keep, give = call(
-        sort_kernel,
-        (
-            struct((nx, size["zl"], nzh, PIECE, LANES), BF16),
-            struct((plane * nzh * PIECE + NOTES, LANES), BF16),
-        ),
-        in_specs=[SCALAR, SCALAR, SCALAR, WHOLE],
-    )(core, token_counts, step_counts, fast)
+    pair = jnp.concatenate([token_counts, step_counts], axis=1)
+    counts = swap(jnp.broadcast_to(pair, (groups * size["c"], 2)), ("expert", "c"))
+    shape = (nx, size["zl"], nzh, PIECE, LANES)
+    keep, give = call(sort_kernel, (struct(shape, BF16), struct(shape, BF16)))(fast)
     got = lax.ppermute(give, "c", [(0, 1), (1, 0)])
     pairs = call(
         pair_sum_kernel,
         struct((plane, nzh * PIECE + NOTES, LANES), jnp.int16),
-        in_specs=[SCALAR, SCALAR, SCALAR, WHOLE, WHOLE],
-    )(token_counts, step_counts, experts, keep, got)
+        in_specs=[SCALAR, WHOLE, WHOLE],
+    )(counts, keep, got)
     got = swap(pairs, ("x", "zl"))
     sums = call(near_sum_kernel, struct((nzh, PIECE + FAR_NOTES, LANES), jnp.int16))(got)
-    got = swap(sums, "zh")
+    got = swap_far(sums)
     new_slow, copies = call(
         lambda *refs: refresh_kernel(groups, *refs),
         (struct(slow_weights.shape, F32), struct((nzh, PIECE, LANES), BF16)),
-        in_specs=[SCALAR, WHOLE, WHOLE],
-    )(place, got, slow_weights)
-
-    column = swap(copies, "zh")
+    )(got, slow_weights)
+
+    column = swap_far(copies)
     own = swap(jnp.broadcast_to(column[None], (plane, *column.shape)), ("x", "zl"))
-    other = lax.ppermute(own, "c", [(0, 1), (1, 0)])
-    shape = (nx, size["zl"], *column.shape)
+    both = swap(jnp.broadcast_to(own[None], (size["c"], *own.shape)), "c").reshape(size["c"], *shape)
     reset = call(
         lay_out_kernel,
         struct(fast.shape, BF16),
         grid=(nx,),
-        in_specs=[SCALAR, by_x(*shape), by_x(*shape)],
+        in_specs=[pl.BlockSpec((size["c"], 1, *shape[1:]), lambda x: (0, x, 0, 0, 0, 0))],
         out_specs=halves,
-    )(core, own.reshape(shape), other.reshape(shape))
+    )(both)
     return new_slow, reset[None, None]
 
 

time: 117 us -> 117 us (level)
  blocking collectives: 59.9 us -> 98.7 us
  waiting for transfers between devices: 19.4 us -> 0.01 us
  starting transfers between devices: 28 us -> 8.79 us
    all_to_all x0 -> x2, blocking collectives: none -> 52 us  [swap_far(): lax.all_to_all(pieces, FAR, split_axis=0, concat_axis=0, tiled=True, axis...]
    all_to_all x1 -> x0, waiting for transfers between devices: 17.3 us -> none  [swap(): return lax.all_to_all(pieces, axis, split_axis=0, concat_axis=0, tiled=True)]
    all_to_all x1 -> x0, starting transfers between devices: 13.5 us -> none  [swap(): return lax.all_to_all(pieces, axis, split_axis=0, concat_axis=0, tiled=True)]
    all_to_all x4, blocking collectives: 59.9 us -> 46.7 us  [swap(): return lax.all_to_all(pieces, axis, split_axis=0, concat_axis=0, tiled=True)]
    ppermute x1 -> x0, starting transfers between devices: 5.66 us -> none  [shards(): other = lax.ppermute(own, 'c', [(0, 1), (1, 0)])]
    ppermute x1 -> x0, waiting for transfers between devices: 2.08 us -> none  [shards(): other = lax.ppermute(own, 'c', [(0, 1), (1, 0)])]
  transfers between devices with their start and end apart: 3 -> 1, of which waited for: 2 -> 0; matrix products, arithmetic and copies ran while one was open for 0% -> 0% of each run, Pallas kernels for 0% -> 0%
where the time goes in v5:
time: 117 us; the launch traced here: 116 us
  blocking collectives  98.7 us (84%)
  starting transfers between devices  8.79 us (8%)
  Pallas kernels  4.68 us (4%)
  between operations  1.98 us (2%)
  local copies, waits for them, and re-layouts  1.86 us (2%)
    all_to_all x2, blocking collectives, swap_far(): lax.all_to_all(pieces, FAR, split_axis=0, concat_axis=0, tiled=True, axis...  52 us
    all_to_all x4, blocking collectives, swap(): return lax.all_to_all(pieces, axis, split_axis=0, concat_axis=0, tiled=True)  46.7 us
    ppermute x1, starting transfers between devices, shards(): got = lax.ppermute(give, 'c', [(0, 1), (1, 0)])  8.79 us
  transfers between devices with their start and end apart: 1, of which 0 were waited for; matrix products, arithmetic and copies ran while one was open for 0% of the time, Pallas kernels for 0%

profile of v5, /device:TPU:1, one launch (start us, length us, event | category | flops | bytes accessed | tf_op | source)
XLA Modules:
  0.0 116.1 jit_solution(15375617126955737813)
XLA Ops:
  0.6 0.0 copy-start
  0.6 1.5 %copy-done = bf16[1,1,1,64,14336]{4,3,2,1,0:T(8,128)(2,1)S(1)} copy-done((bf16[1,1,1,64,14336]{4,3,2,1,0:T(8,128)(2,1)S(1)}, bf16[1,1,1,64,14336]{4,3,2,1,0:T(8,128)(2,1)}, u32[]{:S(2)}) %copy-start) | copy-done | bytes 1835032
  2.1 0.4 shard_map.59
  2.6 8.8 %collective-permute-start = (bf16[2,2,8,112,128]{4,3,2,1,0:T(8,128)(2,1)S(1)}, bf16[2,2,8,112,128]{4,3,2,1,0:T(8,128)(2,1)S(1)}, u32[]{:S(2)}, u32[]{:S(2)}) collective-permute-start(bf16[2,2,8,112,128]{4,3,2,1,0:T(8,128)(2,1)S(1)} %get-tuple-element.7), channel_id=1, source_target_pairs={{0,1},{1,0},{2,3},{3,2},{4,5},{5,4},{6,7},{7,6},{8,9},{9,8},{10,11... | collective-permute-start | bytes 2752520 | tf_op jit(solution)/shard_map/ppermute | solution.py:279
  12.6 0.1 add_bitcast_fusion
  12.7 7.9 %all_to_all.33 = s32[16,1,2]{2,1,0:T(1,128)S(1)} all-to-all(s32[16,1,2]{2,1,0:T(1,128)S(1)} %broadcast_in_dim.8), channel_id=1, replica_groups=mesh['expert'=8,'x'=2,'zh'=8,'zl'=2,'c'=2] {'expert','c'}, dimensions={0} | all-to-all | bytes 256 | tf_op jit(solution)/shard_map/all_to_all | solution.py:259
  20.7 0.0 collective-permute-done.got
  20.7 1.3 %shard_map.60 = s16[4,912,128]{2,1,0:T(8,128)(2,1)S(1)} custom-call(s32[16,2]{1,0:T(8,128)S(1)} %bitcast.8, bf16[2,2,8,112,128]{4,3,2,1,0:T(8,128)(2,1)S(1)} %get-tuple-element.6.keep, bf16[2,2,8,112,128]{4,3,2,1,0:T(8,128)(2,1)S(1)} %collective-permute-done.got), custom_call_target="tpu_custom_call" | custom-call | tf_op jit(solution)/shard_map/pallas_call | solution.py:280
  22.0 0.0 copy-start.1
  22.0 16.3 %all_to_all.34.got = s16[4,912,128]{2,1,0:T(8,128)(2,1)S(1)} all-to-all(s16[4,912,128]{2,1,0:T(8,128)(2,1)S(1)} %shard_map.60), channel_id=1, replica_groups=mesh['expert'=8,'x'=2,'zh'=8,'zl'=2,'c'=2] {'x','zl'}, dimensions={0} | all-to-all | bytes 1867776 | tf_op jit(solution)/shard_map/all_to_all | solution.py:259
  38.4 0.4 shard_map.61
  38.7 29.7 %all_to_all.35.refs_0_ = s16[8,120,128]{2,1,0:T(8,128)(2,1)S(1)} all-to-all(s16[8,120,128]{2,1,0:T(8,128)(2,1)S(1)} %shard_map.61), channel_id=1, replica_groups={{0,16,8,24,4,20,12,28},{9,25,5,21,13,29,1,17},{6,22,14,30,2,18,10,26},{..., dimensions={0} | all-to-all | bytes 491520 | tf_op jit(solution)/shard_map/all_to_all | solution.py:50
  68.4 0.0 copy-done.1
  68.4 1.0 shard_map.62
  69.4 22.3 %all_to_all.36 = bf16[8,112,128]{2,1,0:T(8,128)(2,1)S(1)} all-to-all(bf16[8,112,128]{2,1,0:T(8,128)(2,1)S(1)} %get-tuple-element.9), channel_id=1, replica_groups={{0,16,8,24,4,20,12,28},{9,25,5,21,13,29,1,17},{6,22,14,30,2,18,10,26},{..., dimensions={0} | all-to-all | bytes 458752 | tf_op jit(solution)/shard_map/all_to_all | solution.py:50
  91.7 0.1 broadcast_in_dim.9
  91.8 14.7 %all_to_all.37 = bf16[4,8,112,128]{3,2,1,0:T(8,128)(2,1)S(1)} all-to-all(bf16[4,8,112,128]{3,2,1,0:T(8,128)(2,1)S(1)} %broadcast_in_dim.9), channel_id=1, replica_groups=mesh['expert'=8,'x'=2,'zh'=8,'zl'=2,'c'=2] {'x','zl'}, dimensions={0} | all-to-all | bytes 1835008 | tf_op jit(solution)/shard_map/all_to_all | solution.py:259
  106.5 0.2 broadcast_in_dim.10
  106.8 7.7 %all_to_all.38 = bf16[2,4,8,112,128]{4,3,2,1,0:T(8,128)(2,1)S(1)} all-to-all(bf16[2,4,8,112,128]{4,3,2,1,0:T(8,128)(2,1)S(1)} %broadcast_in_dim.10), channel_id=1, replica_groups=mesh['expert'=8,'x'=2,'zh'=8,'zl'=2,'c'=2] {'c'}, dimensions={0} | all-to-all | bytes 3670016 | tf_op jit(solution)/shard_map/all_to_all | solution.py:259
  114.5 1.6 %shard_map.63 = bf16[64,14336]{1,0:T(8,128)(2,1)} custom-call(bf16[2,2,2,8,112,128]{5,4,3,2,1,0:T(8,128)(2,1)S(1)} %bitcast.6), custom_call_target="tpu_custom_call" | custom-call | tf_op jit(solution)/shard_map/pallas_call | solution.py:296
  (1 shorter events, 0.0 us)
Async XLA Ops:
  0.6 1.5 %copy-start = (bf16[1,1,1,64,14336]{4,3,2,1,0:T(8,128)(2,1)S(1)}, bf16[1,1,1,64,14336]{4,3,2,1,0:T(8,128)(2,1)}, u32[]{:S(2)}) copy-start(bf16[1,1,1,64,14336]{4,3,2,1,0:T(8,128)(2,1)} %param.4) | copy-start | bytes 5505028
  2.6 18.1 %collective-permute-start = (bf16[2,2,8,112,128]{4,3,2,1,0:T(8,128)(2,1)S(1)}, bf16[2,2,8,112,128]{4,3,2,1,0:T(8,128)(2,1)S(1)}, u32[]{:S(2)}, u32[]{:S(2)}) collective-permute-start(bf16[2,2,8,112,128]{4,3,2,1,0:T(8,128)(2,1)S(1)} %get-tuple-element.7), channel_id=1, source_target_pairs={{0,1},{1,0},{2,3},{3,2},{4,5},{5,4},{6,7},{7,6},{8,9},{9,8},{10,11... | collective-permute-start | bytes 2752520 | tf_op jit(solution)/shard_map/ppermute | solution.py:279
  22.0 46.4 %copy-start.1 = (f32[1,1,64,224]{3,2,1,0:T(8,128)S(1)}, f32[1,1,64,224]{3,2,1,0:T(8,128)}, u32[]{:S(2)}) copy-start(f32[1,1,64,224]{3,2,1,0:T(8,128)} %refs_1_.1) | copy-start | bytes 172036

commit v6 on v5

--- a/solution.py
+++ b/solution.py
@@ -30,7 +30,6 @@
 FAR_NOTES = 8
 TOP = 32767.0
 DIGIT = 4096.0
-MIDDLE = 32768.0
 FINE = 8.0
 
 
@@ -92,6 +91,11 @@
     return jnp.concatenate([p for p in parts if p.shape[1]], axis=1)
 
 
+def as_bytes(count):
+    high = jnp.floor(count * (1 / 256))
+    return high, count - 256 * high
+
+
 def own_place():
     return lax.axis_index("zl") * 2 + lax.axis_index("c")
 
@@ -134,51 +138,45 @@
     return (jnp.exp2(level * (1 / FINE)) * (1 / TOP)) * wide(units)
 
 
-def sort_kernel(fast, keep, give):
-    n_zl = keep.shape[1]
+def sort_kernel(tokens, steps, fast, out):
+    n_c = out.shape[0]
+    n_zl = QUAD // n_c
+    n_zh = len(SPREAD)
     group = lane_group((ROWS, LANES))
-
-    def body(sides):
-        for g in range(fast.shape[1] // WIDE):
-            x, zh = divmod(g, keep.shape[2])
-            lanes = [slice(g * WIDE + i * LANES, g * WIDE + (i + 1) * LANES) for i in range(2 * QUAD - 1)]
-            odd = [fast[:, at].astype(F32) for at in lanes[1::2]]
-            for k in range(QUAD):
-                if k == 0:
-                    res = odd[0]
-                elif k == QUAD - 1:
-                    res = odd[-1]
-                else:
-                    res = jnp.where(group >= QUAD - k, odd[k - 1], odd[k])
-                zl, c = divmod(k, QUAD // n_zl)
-                sides[c][x, zl, zh, :ROWS] = fast[:, lanes[2 * k]]
-                sides[c][x, zl, zh, ROWS:] = folded(res, k).astype(BF16)
-
-    core = lax.axis_index("c")
-
-    @pl.when(core == 0)
-    def _():
-        body((keep, give))
-
-    @pl.when(core != 0)
-    def _():
-        body((give, keep))
-
-
-def pair_sum_kernel(counts, keep, got, out):
-    core = lax.axis_index("c")
-    pair = lax.axis_index("expert") * 2
-    of_core = [[counts[pair + c, i].astype(F32) for i in range(2)] for c in (core, 1 - core)]
-    (tokens, steps), (tokens_2, steps_2) = ([jnp.full((1, LANES), v) for v in values] for values in of_core)
-    share, other = tokens / steps, tokens_2 / steps_2
-    everywhere = sum(counts[i, 0] for i in range(counts.shape[0])).astype(F32)
-    sums = (tokens + tokens_2, tokens * steps + tokens_2 * steps_2, *digits(share + other), everywhere)
-    n_zl, n_zh = keep.shape[1:3]
+    for g in range(fast.shape[1] // WIDE):
+        x, zh = divmod(g, n_zh)
+        lanes = [slice(g * WIDE + i * LANES, g * WIDE + (i + 1) * LANES) for i in range(2 * QUAD - 1)]
+        odd = [fast[:, at].astype(F32) for at in lanes[1::2]]
+        for k in range(QUAD):
+            if k == 0:
+                res = odd[0]
+            elif k == QUAD - 1:
+                res = odd[-1]
+            else:
+                res = jnp.where(group >= QUAD - k, odd[k - 1], odd[k])
+            zl, c = divmod(k, n_c)
+            at = ((x * n_zl + zl) * n_zh + zh) * PIECE
+            out[c, at : at + ROWS] = fast[:, lanes[2 * k]]
+            out[c, at + ROWS : at + PIECE] = folded(res, k).astype(BF16)
+    counts = [jnp.broadcast_to(v[...].astype(F32), (1, LANES)) for v in (tokens, steps)]
+    notes = in_rows([v for count in counts for v in as_bytes(count)], NOTES).astype(BF16)
+    for c in range(n_c):
+        out[c, out.shape[1] - NOTES :] = notes
+
+
+def pair_sum_kernel(got, out):
+    rows = got.shape[1] - NOTES
+    notes = [got[c, rows:].astype(F32) for c in range(got.shape[0])]
+    counts = [[256 * v[2 * i : 2 * i + 1] + v[2 * i + 1 : 2 * i + 2] for i in range(2)] for v in notes]
+    shares = [tokens / steps for tokens, steps in counts]
+    tok = sum(tokens for tokens, _ in counts)
+    sums = (tok, sum(tokens * steps for tokens, steps in counts), *digits(sum(shares)))
+    n_zh = len(SPREAD)
     for d in range(out.shape[0]):
         levels = []
-        at = divmod(d, n_zl)
         for zh in range(n_zh):
-            mix = share * keep[*at, zh].astype(F32) + other * got[*at, zh].astype(F32)
+            at = (d * n_zh + zh) * PIECE
+            mix = sum(share * got[c, at : at + PIECE].astype(F32) for c, share in enumerate(shares))
             out[d, zh * PIECE : (zh + 1) * PIECE], level = coded(mix)
             levels.append(level)
         out[d, n_zh * PIECE :] = short(in_rows((*levels, *sums), NOTES))
@@ -188,9 +186,9 @@
     place = own_place()
     n, n_zh = got.shape[0], out.shape[0]
     notes = [wide(got[s, n_zh * PIECE :]) for s in range(n)]
-    tok, work, *qsum, everywhere = (sum(v[n_zh + i : n_zh + i + 1] for v in notes) for i in range(6))
+    tok, work, *qsum = (sum(v[n_zh + i : n_zh + i + 1] for v in notes) for i in range(5))
     high = jnp.floor(work / DIGIT)
-    far = (tok, high, work - DIGIT * high, everywhere - MIDDLE, *digits(from_digits(*qsum)))
+    far = (tok, high, work - DIGIT * high, *digits(from_digits(*qsum)))
     for zh in range(n_zh):
         piece = slice(zh * PIECE, (zh + 1) * PIECE)
         total = decoded(got[0, piece], notes[0][zh : zh + 1])
@@ -201,29 +199,52 @@
         out[to, PIECE:] = short(in_rows((level, *far), FAR_NOTES))
 
 
-def refresh_kernel(groups, got, slow, new_slow, copies):
+def tokens_kernel(got, out):
+    tok = sum(wide(got[s, PIECE:])[1:2] for s in range(got.shape[0]))
+    for e in range(out.shape[0]):
+        out[e] = tok
+
+
+def for_own_place(body):
+    place = own_place()
+    for k in range(QUAD):
+
+        @pl.when(place == k)
+        def _(k=k):
+            body(k)
+
+
+def far_sum_kernel(got, slow, mine, step, pace):
     total = sums = None
     for s in range(got.shape[0]):
         notes = wide(got[s, PIECE:])
         part = decoded(got[s, :PIECE], notes[0:1])
         total, sums = (part, notes) if s == 0 else (total + part, sums + notes)
-    tok = sums[1:2]
     work = DIGIT * sums[2:3] + sums[3:4]
-    everywhere = sums[4:5] + MIDDLE * got.shape[0]
-    qsum = from_digits(sums[5:6], sums[6:7], sums[7:8])
-    rate = outer_rate * groups * work / (tok * everywhere)
-    place = own_place()
-    for k in range(QUAD):
-
-        @pl.when(place == k)
-        def _(k=k):
-            mine = own_parts(slow[0, 0], k)
-            tile = mine[0] + rate * (total[:ROWS] - qsum * mine[0])
-            rest = mine[1] + rate * (total[ROWS:] - qsum * mine[1])
-            new_slow[0, 0] = own_block(tile, rest, k)
-            for i in range(copies.shape[0]):
-                copies[i, :ROWS] = tile.astype(BF16)
-                copies[i, ROWS:] = rest.astype(BF16)
+    qsum = from_digits(sums[4:5], sums[5:6], sums[6:7])
+    pace[0:1] = work
+    pace[1:2] = sums[1:2]
+
+    def body(k):
+        for rows, part in zip((slice(0, ROWS), slice(ROWS, PIECE)), own_parts(slow[0, 0], k)):
+            mine[rows] = part
+            step[rows] = total[rows] - qsum * part
+
+    for_own_place(body)
+
+
+def refresh_kernel(experts, mine, step, pace, new_slow, copies):
+    groups = experts.shape[0]
+    everywhere = sum(experts[e] for e in range(groups))
+    rate = outer_rate * groups * pace[0:1] / (pace[1:2] * everywhere)
+    new = mine[...] + rate * step[...]
+    for i in range(copies.shape[0]):
+        copies[i] = new.astype(BF16)
+
+    def body(k):
+        new_slow[0, 0] = own_block(new[:ROWS], new[ROWS:], k)
+
+    for_own_place(body)
 
 
 def lay_out_kernel(pieces, out):
@@ -259,10 +280,6 @@
     return lax.all_to_all(pieces, axis, split_axis=0, concat_axis=0, tiled=True)
 
 
-SCALAR = pl.BlockSpec(memory_space=pltpu.SMEM)
-WHOLE = pl.BlockSpec(memory_space=pltpu.VMEM)
-
-
 def shards(fast_weights, slow_weights, step_counts, token_counts):
     size = {a: lax.axis_size(a) for a in SHARD}
     groups = lax.axis_size("expert")
@@ -272,23 +289,19 @@
     halves = pl.BlockSpec((ROWS, half), lambda x: (0, x))
 
     plane = nx * size["zl"]
-    pair = jnp.concatenate([token_counts, step_counts], axis=1)
-    counts = swap(jnp.broadcast_to(pair, (groups * size["c"], 2)), ("expert", "c"))
     shape = (nx, size["zl"], nzh, PIECE, LANES)
-    keep, give = call(sort_kernel, (struct(shape, BF16), struct(shape, BF16)))(fast)
-    got = lax.ppermute(give, "c", [(0, 1), (1, 0)])
-    pairs = call(
-        pair_sum_kernel,
-        struct((plane, nzh * PIECE + NOTES, LANES), jnp.int16),
-        in_specs=[SCALAR, WHOLE, WHOLE],
-    )(counts, keep, got)
-    got = swap(pairs, ("x", "zl"))
-    sums = call(near_sum_kernel, struct((nzh, PIECE + FAR_NOTES, LANES), jnp.int16))(got)
-    got = swap_far(sums)
+    raw = call(sort_kernel, struct((size["c"], plane * nzh * PIECE + NOTES, LANES), BF16))(
+        token_counts, step_counts, fast
+    )
+    got = swap(raw, "c")
+    got = swap(call(pair_sum_kernel, struct((plane, nzh * PIECE + NOTES, LANES), jnp.int16))(got), ("x", "zl"))
+    got = swap_far(call(near_sum_kernel, struct((nzh, PIECE + FAR_NOTES, LANES), jnp.int16))(got))
+    experts = swap(call(tokens_kernel, struct((groups, 1, LANES), F32))(got), "expert")
+    block = struct((PIECE, LANES), F32)
+    terms = call(far_sum_kernel, (block, block, struct((FAR_NOTES, LANES), F32)))(got, slow_weights)
     new_slow, copies = call(
-        lambda *refs: refresh_kernel(groups, *refs),
-        (struct(slow_weights.shape, F32), struct((nzh, PIECE, LANES), BF16)),
-    )(got, slow_weights)
+        refresh_kernel, (struct(slow_weights.shape, F32), struct((nzh, PIECE, LANES), BF16))
+    )(experts, *terms)
 
     column = swap_far(copies)
     own = swap(jnp.broadcast_to(column[None], (plane, *column.shape)), ("x", "zl"))

time: 117 us -> 118 us (level)
  waiting for transfers between devices: 0.01 us -> 4.71 us
  starting transfers between devices: 8.79 us -> 4.22 us
  blocking collectives: 98.7 us -> 101 us
    ppermute x1 -> x0, starting transfers between devices: 8.79 us -> none  [shards(): got = lax.ppermute(give, 'c', [(0, 1), (1, 0)])]
    all_to_all x0 -> x1, waiting for transfers between devices: none -> 4.71 us  [swap(): return lax.all_to_all(pieces, axis, split_axis=0, concat_axis=0, tiled=True)]
    all_to_all x0 -> x1, starting transfers between devices: none -> 4.22 us  [swap(): return lax.all_to_all(pieces, axis, split_axis=0, concat_axis=0, tiled=True)]
    all_to_all x4, blocking collectives: 46.7 us -> 50.8 us  [swap(): return lax.all_to_all(pieces, axis, split_axis=0, concat_axis=0, tiled=True)]
    all_to_all x2, blocking collectives: 52 us -> 49.9 us  [swap_far(): lax.all_to_all(pieces, FAR, split_axis=0, concat_axis=0, tiled=True, axis...]
  transfers between devices with their start and end apart: 1 -> 1, of which waited for: 0 -> 1; matrix products, arithmetic and copies ran while one was open for 0% -> 0% of each run, Pallas kernels for 0% -> 0%
where the time goes in v6:
time: 118 us
  blocking collectives  101 us (86%)
  waiting for transfers between devices  4.71 us (4%)
  Pallas kernels  4.63 us (4%)
  starting transfers between devices  4.22 us (4%)
  between operations  1.97 us (2%)
  local copies, waits for them, and re-layouts  1.85 us (2%)
    all_to_all x4, blocking collectives, swap(): return lax.all_to_all(pieces, axis, split_axis=0, concat_axis=0, tiled=True)  50.8 us
    all_to_all x2, blocking collectives, swap_far(): lax.all_to_all(pieces, FAR, split_axis=0, concat_axis=0, tiled=True, axis...  49.9 us
    all_to_all x1, waiting for transfers between devices, swap(): return lax.all_to_all(pieces, axis, split_axis=0, concat_axis=0, tiled=True)  4.71 us
    all_to_all x1, starting transfers between devices, swap(): return lax.all_to_all(pieces, axis, split_axis=0, concat_axis=0, tiled=True)  4.22 us
  transfers between devices with their start and end apart: 1, of which 1 were waited for; matrix products, arithmetic and copies ran while one was open for 0% of the time, Pallas kernels for 0%

profile of v6, /device:TPU:1, one launch (start us, length us, event | category | flops | bytes accessed | tf_op | source)
XLA Modules:
  0.0 118.1 jit_solution(11074553073124405116)
XLA Ops:
  1.9 0.0 copy-start
  1.9 1.5 %copy-done = bf16[1,1,1,64,14336]{4,3,2,1,0:T(8,128)(2,1)S(1)} copy-done((bf16[1,1,1,64,14336]{4,3,2,1,0:T(8,128)(2,1)S(1)}, bf16[1,1,1,64,14336]{4,3,2,1,0:T(8,128)(2,1)}, u32[]{:S(2)}) %copy-start) | copy-done | bytes 1835032
  3.4 0.4 shard_map.59
  3.8 11.7 %all_to_all.35.got = bf16[2,3600,128]{2,1,0:T(8,128)(2,1)S(1)} all-to-all(bf16[2,3600,128]{2,1,0:T(8,128)(2,1)S(1)} %shard_map.59), channel_id=1, replica_groups=mesh['expert'=8,'x'=2,'zh'=8,'zl'=2,'c'=2] {'c'}, dimensions={0} | all-to-all | bytes 3686400 | tf_op jit(solution)/shard_map/all_to_all | solution.py:280
  15.5 0.7 shard_map.60
  16.2 0.0 copy-start.1
  16.2 16.7 %all_to_all.36.got = s16[4,912,128]{2,1,0:T(8,128)(2,1)S(1)} all-to-all(s16[4,912,128]{2,1,0:T(8,128)(2,1)S(1)} %shard_map.60), channel_id=1, replica_groups=mesh['expert'=8,'x'=2,'zh'=8,'zl'=2,'c'=2] {'x','zl'}, dimensions={0} | all-to-all | bytes 1867776 | tf_op jit(solution)/shard_map/all_to_all | solution.py:280
  32.9 0.3 shard_map.61
  33.2 28.2 %all_to_all.37.got = s16[8,120,128]{2,1,0:T(8,128)(2,1)S(1)} all-to-all(s16[8,120,128]{2,1,0:T(8,128)(2,1)S(1)} %shard_map.61), channel_id=1, replica_groups={{0,16,8,24,4,20,12,28},{9,25,5,21,13,29,1,17},{6,22,14,30,2,18,10,26},{..., dimensions={0} | all-to-all | bytes 491520 | tf_op jit(solution)/shard_map/all_to_all | solution.py:49
  61.4 0.6 shard_map.62
  62.1 4.2 %all-to-all-start.3 = ((f32[8,1,128]{2,1,0:T(1,128)}), f32[8,1,128]{2,1,0:T(1,128)S(1)}, u32[]{:S(2)}, u32[]{:S(2)}) async-start(f32[8,1,128]{2,1,0:T(1,128)} %shard_map.62), calls=%async_computation.3 | async-start | bytes 8192 | tf_op jit(solution)/shard_map/all_to_all | solution.py:280
  66.3 0.0 copy-done.1
  66.3 0.2 shard_map.63
  66.5 4.7 %all-to-all-done.3.experts = f32[8,1,128]{2,1,0:T(1,128)S(1)} async-done(((f32[8,1,128]{2,1,0:T(1,128)}), f32[8,1,128]{2,1,0:T(1,128)S(1)}, u32[]{:S(2)}, u32[]{:S(2)}) %all-to-all-start.3) | async-done | bytes 4128 | tf_op jit(solution)/shard_map/all_to_all | solution.py:280
  71.2 0.8 shard_map.64
  72.0 21.7 %all_to_all.38 = bf16[8,112,128]{2,1,0:T(8,128)(2,1)S(1)} all-to-all(bf16[8,112,128]{2,1,0:T(8,128)(2,1)S(1)} %get-tuple-element.11), channel_id=1, replica_groups={{0,16,8,24,4,20,12,28},{9,25,5,21,13,29,1,17},{6,22,14,30,2,18,10,26},{..., dimensions={0} | all-to-all | bytes 458752 | tf_op jit(solution)/shard_map/all_to_all | solution.py:49
  93.7 0.1 broadcast_in_dim.6
  93.8 13.9 %all_to_all.39 = bf16[4,8,112,128]{3,2,1,0:T(8,128)(2,1)S(1)} all-to-all(bf16[4,8,112,128]{3,2,1,0:T(8,128)(2,1)S(1)} %broadcast_in_dim.6), channel_id=1, replica_groups=mesh['expert'=8,'x'=2,'zh'=8,'zl'=2,'c'=2] {'x','zl'}, dimensions={0} | all-to-all | bytes 1835008 | tf_op jit(solution)/shard_map/all_to_all | solution.py:280
  107.7 0.2 broadcast_in_dim.7
  108.0 8.5 %all_to_all.40 = bf16[2,4,8,112,128]{4,3,2,1,0:T(8,128)(2,1)S(1)} all-to-all(bf16[2,4,8,112,128]{4,3,2,1,0:T(8,128)(2,1)S(1)} %broadcast_in_dim.7), channel_id=1, replica_groups=mesh['expert'=8,'x'=2,'zh'=8,'zl'=2,'c'=2] {'c'}, dimensions={0} | all-to-all | bytes 3670016 | tf_op jit(solution)/shard_map/all_to_all | solution.py:280
  116.5 1.6 %shard_map.65 = bf16[64,14336]{1,0:T(8,128)(2,1)} custom-call(bf16[2,2,2,8,112,128]{5,4,3,2,1,0:T(8,128)(2,1)S(1)} %bitcast.3), custom_call_target="tpu_custom_call" | custom-call | tf_op jit(solution)/shard_map/pallas_call | solution.py:309
Async XLA Ops:
  1.9 1.5 %copy-start = (bf16[1,1,1,64,14336]{4,3,2,1,0:T(8,128)(2,1)S(1)}, bf16[1,1,1,64,14336]{4,3,2,1,0:T(8,128)(2,1)}, u32[]{:S(2)}) copy-start(bf16[1,1,1,64,14336]{4,3,2,1,0:T(8,128)(2,1)} %param.4) | copy-start | bytes 5505028
  16.2 50.1 %copy-start.1 = (f32[1,1,64,224]{3,2,1,0:T(8,128)S(1)}, f32[1,1,64,224]{3,2,1,0:T(8,128)}, u32[]{:S(2)}) copy-start(f32[1,1,64,224]{3,2,1,0:T(8,128)} %slow.1) | copy-start | bytes 172036
  62.1 9.1 %all-to-all-start.3 = ((f32[8,1,128]{2,1,0:T(1,128)}), f32[8,1,128]{2,1,0:T(1,128)S(1)}, u32[]{:S(2)}, u32[]{:S(2)}) async-start(f32[8,1,128]{2,1,0:T(1,128)} %shard_map.62), calls=%async_computation.3 | async-start | bytes 8192 | tf_op jit(solution)/shard_map/all_to_all | solution.py:280

commit v7 on v5

--- a/solution.py
+++ b/solution.py
@@ -10,8 +10,6 @@
 BF16 = jnp.bfloat16
 
 SHARD = ("x", "zh", "zl", "c")
-
-FAR = ("zh", "zl", "c")
 
 outer_rate = 0.7
 
@@ -34,22 +32,6 @@
 FINE = 8.0
 
 
-SPREAD = (0, 4, 2, 6, 1, 5, 3, 7)
-
-
-def member(at, k):
-    return SPREAD[(at + 2 * k) % len(SPREAD)]
-
-
-def position(zh, k):
-    return (SPREAD[zh] - 2 * k) % len(SPREAD)
-
-
-def swap_far(pieces):
-    groups = [[member(at, k) * QUAD + k for at in range(len(SPREAD))] for k in range(QUAD)]
-    return lax.all_to_all(pieces, FAR, split_axis=0, concat_axis=0, tiled=True, axis_index_groups=groups)
-
-
 def lane_group(shape):
     return lax.broadcasted_iota(jnp.int32, shape, 1) // STEP
 
@@ -96,6 +78,12 @@
     return lax.axis_index("zl") * 2 + lax.axis_index("c")
 
 
+def for_core(first, second):
+    core = lax.axis_index("c")
+    pl.when(core == 0)(first)
+    pl.when(core != 0)(second)
+
+
 def in_rows(values, rows):
     row = lax.broadcasted_iota(jnp.int32, (rows, LANES), 0)
     out = jnp.zeros((rows, LANES), F32)
@@ -134,58 +122,60 @@
     return (jnp.exp2(level * (1 / FINE)) * (1 / TOP)) * wide(units)
 
 
-def sort_kernel(fast, keep, give):
-    n_zl = keep.shape[1]
+def own_pieces(fast, g, core):
     group = lane_group((ROWS, LANES))
-
-    def body(sides):
-        for g in range(fast.shape[1] // WIDE):
-            x, zh = divmod(g, keep.shape[2])
-            lanes = [slice(g * WIDE + i * LANES, g * WIDE + (i + 1) * LANES) for i in range(2 * QUAD - 1)]
-            odd = [fast[:, at].astype(F32) for at in lanes[1::2]]
-            for k in range(QUAD):
-                if k == 0:
-                    res = odd[0]
-                elif k == QUAD - 1:
-                    res = odd[-1]
-                else:
-                    res = jnp.where(group >= QUAD - k, odd[k - 1], odd[k])
-                zl, c = divmod(k, QUAD // n_zl)
-                sides[c][x, zl, zh, :ROWS] = fast[:, lanes[2 * k]]
-                sides[c][x, zl, zh, ROWS:] = folded(res, k).astype(BF16)
-
-    core = lax.axis_index("c")
-
-    @pl.when(core == 0)
-    def _():
-        body((keep, give))
-
-    @pl.when(core != 0)
-    def _():
-        body((give, keep))
-
-
-def pair_sum_kernel(counts, keep, got, out):
-    core = lax.axis_index("c")
-    pair = lax.axis_index("expert") * 2
-    of_core = [[counts[pair + c, i].astype(F32) for i in range(2)] for c in (core, 1 - core)]
-    (tokens, steps), (tokens_2, steps_2) = ([jnp.full((1, LANES), v) for v in values] for values in of_core)
-    share, other = tokens / steps, tokens_2 / steps_2
-    everywhere = sum(counts[i, 0] for i in range(counts.shape[0])).astype(F32)
-    sums = (tokens + tokens_2, tokens * steps + tokens_2 * steps_2, *digits(share + other), everywhere)
-    n_zl, n_zh = keep.shape[1:3]
-    for d in range(out.shape[0]):
-        levels = []
-        at = divmod(d, n_zl)
-        for zh in range(n_zh):
-            mix = share * keep[*at, zh].astype(F32) + other * got[*at, zh].astype(F32)
-            out[d, zh * PIECE : (zh + 1) * PIECE], level = coded(mix)
-            levels.append(level)
-        out[d, n_zh * PIECE :] = short(in_rows((*levels, *sums), NOTES))
+    lanes = [slice(g * WIDE + i * LANES, g * WIDE + (i + 1) * LANES) for i in range(2 * QUAD - 1)]
+    odd = [fast[:, at].astype(F32) for at in lanes[1::2]]
+    pieces = []
+    for k in range(core, QUAD, 2):
+        if k == 0:
+            res = odd[0]
+        elif k == QUAD - 1:
+            res = odd[-1]
+        else:
+            res = jnp.where(group >= QUAD - k, odd[k - 1], odd[k])
+        pieces.append((fast[:, lanes[2 * k]].astype(F32), folded(res, k)))
+    return pieces
+
+
+def sort_kernel(fast, keep):
+    nx, n_zl, n_zh = keep.shape[:3]
+
+    def body(core):
+        for g in range(nx * n_zh):
+            x, zh = divmod(g, n_zh)
+            for zl, (tile, rest) in enumerate(own_pieces(fast, g, core)):
+                keep[x, zl, zh, :ROWS] = tile.astype(BF16)
+                keep[x, zl, zh, ROWS:] = rest.astype(BF16)
+
+    for_core(lambda: body(0), lambda: body(1))
+
+
+def pair_sum_kernel(counts, keep, other, out):
+    nx, n_zl, n_zh = keep.shape[:3]
+
+    def body(core):
+        pair = lax.axis_index("expert") * 2
+        tokens, steps = ([jnp.full((1, LANES), counts[pair + c, i].astype(F32)) for c in (core, 1 - core)] for i in range(2))
+        shares = [t / n for t, n in zip(tokens, steps)]
+        everywhere = sum(counts[i, 0] for i in range(counts.shape[0])).astype(F32)
+        work = sum(t * n for t, n in zip(tokens, steps))
+        sums = (sum(tokens), work, *digits(sum(shares)), everywhere)
+        levels = [[] for _ in range(out.shape[0])]
+        for g in range(nx * n_zh):
+            x, zh = divmod(g, n_zh)
+            for zl, parts in enumerate(own_pieces(other, g, core)):
+                d = x * n_zl + zl
+                mix = shares[0] * keep[x, zl, zh].astype(F32) + shares[1] * jnp.concatenate(parts, axis=0)
+                out[d, zh * PIECE : (zh + 1) * PIECE], level = coded(mix)
+                levels[d].append(level)
+        for d in range(out.shape[0]):
+            out[d, n_zh * PIECE :] = short(in_rows((*levels[d], *sums), NOTES))
+
+    for_core(lambda: body(0), lambda: body(1))
 
 
 def near_sum_kernel(got, out):
-    place = own_place()
     n, n_zh = got.shape[0], out.shape[0]
     notes = [wide(got[s, n_zh * PIECE :]) for s in range(n)]
     tok, work, *qsum, everywhere = (sum(v[n_zh + i : n_zh + i + 1] for v in notes) for i in range(6))
@@ -196,9 +186,8 @@
         total = decoded(got[0, piece], notes[0][zh : zh + 1])
         for s in range(1, n):
             total = total + decoded(got[s, piece], notes[s][zh : zh + 1])
-        to = (SPREAD[zh] + (n_zh - 2) * place) % n_zh
-        out[to, :PIECE], level = coded(total)
-        out[to, PIECE:] = short(in_rows((level, *far), FAR_NOTES))
+        out[zh, :PIECE], level = coded(total)
+        out[zh, PIECE:] = short(in_rows((level, *far), FAR_NOTES))
 
 
 def refresh_kernel(groups, got, slow, new_slow, copies):
@@ -226,20 +215,19 @@
                 copies[i, ROWS:] = rest.astype(BF16)
 
 
-def lay_out_kernel(pieces, out):
-    n_c, n_zl, n_zh = pieces.shape[0], pieces.shape[2], pieces.shape[3]
-    group = lane_group((ROWS, LANES))
-    for zh in range(n_zh):
-        at = zh * WIDE
-        res = []
-        for k in range(QUAD):
-            zl, c = divmod(k, n_c)
-            piece = pieces.at[c, 0, zl, position(zh, k)]
-            out[:, at + 2 * k * LANES : at + (2 * k + 1) * LANES] = piece[:ROWS]
-            res.append(unfolded(piece[ROWS:].astype(F32), k))
-        for k in range(QUAD - 1):
-            odd = jnp.where(group < QUAD - 1 - k, res[k], res[k + 1])
-            out[:, at + (2 * k + 1) * LANES : at + (2 * k + 2) * LANES] = odd.astype(BF16)
+def lay_out_kernel(own, other, out):
+    def body(pieces):
+        group = lane_group((ROWS, LANES))
+        for zh in range(own.shape[2]):
+            at = zh * WIDE
+            for k in range(QUAD):
+                out[:, at + 2 * k * LANES : at + (2 * k + 1) * LANES] = pieces[k % 2][0, k // 2, zh, :ROWS]
+            res = [unfolded(pieces[k % 2][0, k // 2, zh, ROWS:].astype(F32), k) for k in range(QUAD)]
+            for k in range(QUAD - 1):
+                odd = jnp.where(group < QUAD - 1 - k, res[k], res[k + 1])
+                out[:, at + (2 * k + 1) * LANES : at + (2 * k + 2) * LANES] = odd.astype(BF16)
+
+    for_core(lambda: body((own, other)), lambda: body((other, own)))
 
 
 def call(kernel, out_shape, **more):
@@ -274,32 +262,33 @@
     plane = nx * size["zl"]
     pair = jnp.concatenate([token_counts, step_counts], axis=1)
     counts = swap(jnp.broadcast_to(pair, (groups * size["c"], 2)), ("expert", "c"))
+    other = lax.ppermute(fast, "c", [(0, 1), (1, 0)])
     shape = (nx, size["zl"], nzh, PIECE, LANES)
-    keep, give = call(sort_kernel, (struct(shape, BF16), struct(shape, BF16)))(fast)
-    got = lax.ppermute(give, "c", [(0, 1), (1, 0)])
+    keep = call(sort_kernel, struct(shape, BF16))(fast)
     pairs = call(
         pair_sum_kernel,
         struct((plane, nzh * PIECE + NOTES, LANES), jnp.int16),
         in_specs=[SCALAR, WHOLE, WHOLE],
-    )(counts, keep, got)
+    )(counts, keep, other)
     got = swap(pairs, ("x", "zl"))
     sums = call(near_sum_kernel, struct((nzh, PIECE + FAR_NOTES, LANES), jnp.int16))(got)
-    got = swap_far(sums)
+    got = swap(sums, "zh")
     new_slow, copies = call(
         lambda *refs: refresh_kernel(groups, *refs),
         (struct(slow_weights.shape, F32), struct((nzh, PIECE, LANES), BF16)),
     )(got, slow_weights)
 
-    column = swap_far(copies)
+    column = swap(copies, "zh")
     own = swap(jnp.broadcast_to(column[None], (plane, *column.shape)), ("x", "zl"))
-    both = swap(jnp.broadcast_to(own[None], (size["c"], *own.shape)), "c").reshape(size["c"], *shape)
+    other = lax.ppermute(own, "c", [(0, 1), (1, 0)])
+    planes = pl.BlockSpec((1, *shape[1:]), lambda x: (x, 0, 0, 0, 0))
     reset = call(
         lay_out_kernel,
         struct(fast.shape, BF16),
         grid=(nx,),
-        in_specs=[pl.BlockSpec((size["c"], 1, *shape[1:]), lambda x: (0, x, 0, 0, 0, 0))],
+        in_specs=[planes, planes],
         out_specs=halves,
-    )(both)
+    )(own.reshape(shape), other.reshape(shape))
     return new_slow, reset[None, None]
 
 

time: 117 us -> 115 us (0.983)
  blocking collectives: 98.7 us -> 82 us
  starting transfers between devices: 8.79 us -> 17.8 us
  waiting for transfers between devices: 0.01 us -> 5.72 us
    all_to_all x2 -> x0, blocking collectives: 52 us -> none  [swap_far(): lax.all_to_all(pieces, FAR, split_axis=0, concat_axis=0, tiled=True, axis...]
    all_to_all x4, blocking collectives: 46.7 us -> 82 us  [swap(): return lax.all_to_all(pieces, axis, split_axis=0, concat_axis=0, tiled=True)]
    ppermute x1 -> x2, starting transfers between devices: 8.79 us -> 14.4 us  [the longest x1 8.79 us: shards(): other = lax.ppermute(fast, 'c', [(0, 1), (1, 0)])]
    all_to_all x0 -> x1, waiting for transfers between devices: none -> 3.64 us  [swap(): return lax.all_to_all(pieces, axis, split_axis=0, concat_axis=0, tiled=True)]
    all_to_all x0 -> x1, starting transfers between devices: none -> 3.37 us  [swap(): return lax.all_to_all(pieces, axis, split_axis=0, concat_axis=0, tiled=True)]
    ppermute x1 -> x2, waiting for transfers between devices: 0.01 us -> 2.08 us  [the longest x1 2.08 us: shards(): other = lax.ppermute(own, 'c', [(0, 1), (1, 0)])]
  transfers between devices with their start and end apart: 1 -> 3, of which waited for: 0 -> 2; matrix products, arithmetic and copies ran while one was open for 0% -> 1% of each run, Pallas kernels for 0% -> 0%
where the time goes in v7:
time: 115 us; the launch traced here: 114 us
  blocking collectives  82 us (71%)
  starting transfers between devices  17.8 us (15%)
  waiting for transfers between devices  5.72 us (5%)
  Pallas kernels  4.44 us (4%)
  local copies, waits for them, and re-layouts  2.23 us (2%)
  between operations  1.99 us (2%)
    all_to_all x4, blocking collectives, swap(): return lax.all_to_all(pieces, axis, split_axis=0, concat_axis=0, tiled=True)  82 us
    ppermute x1, starting transfers between devices, shards(): other = lax.ppermute(fast, 'c', [(0, 1), (1, 0)])  8.79 us
    ppermute x1, starting transfers between devices, shards(): other = lax.ppermute(own, 'c', [(0, 1), (1, 0)])  5.63 us
    all_to_all x1, waiting for transfers between devices, swap(): return lax.all_to_all(pieces, axis, split_axis=0, concat_axis=0, tiled=True)  3.64 us
    all_to_all x1, starting transfers between devices, swap(): return lax.all_to_all(pieces, axis, split_axis=0, concat_axis=0, tiled=True)  3.37 us
  transfers between devices with their start and end apart: 3, of which 2 were waited for; matrix products, arithmetic and copies ran while one was open for 1% of the time, Pallas kernels for 0%

profile of v7, /device:TPU:1, one launch (start us, length us, event | category | flops | bytes accessed | tf_op | source)
XLA Modules:
  0.0 114.2 jit_solution(8479009711161219131)
XLA Ops:
  0.6 8.8 %collective-permute-start = (bf16[64,14336]{1,0:T(8,128)(2,1)}, bf16[64,14336]{1,0:T(8,128)(2,1)S(1)}, u32[]{:S(2)}, u32[]{:S(2)}) collective-permute-start(bf16[64,14336]{1,0:T(8,128)(2,1)} %bitcast.8), channel_id=1, source_target_pairs={{0,1},{1,0},{2,3},{3,2},{4,5},{5,4},{6,7},{7,6},{8,9},{9,8},{10,11... | collective-permute-start | bytes 5505032 | tf_op jit(solution)/shard_map/ppermute | solution.py:265
  10.7 0.1 add_bitcast_fusion
  10.8 0.6 broadcast_in_dim.6
  11.4 3.4 %all-to-all-start = ((s32[16,1,2]{2,1,0:T(1,128)}), s32[16,1,2]{2,1,0:T(1,128)S(1)}, u32[]{:S(2)}, u32[]{:S(2)}) async-start(s32[16,1,2]{2,1,0:T(1,128)} %broadcast_in_dim.6), calls=%async_computation | async-start | bytes 16384 | tf_op jit(solution)/shard_map/all_to_all | solution.py:247
  14.8 0.0 copy-start
  14.8 1.5 %copy-done = bf16[1,1,1,64,14336]{4,3,2,1,0:T(8,128)(2,1)S(1)} copy-done((bf16[1,1,1,64,14336]{4,3,2,1,0:T(8,128)(2,1)S(1)}, bf16[1,1,1,64,14336]{4,3,2,1,0:T(8,128)(2,1)}, u32[]{:S(2)}) %copy-start) | copy-done | bytes 1835032
  16.3 0.2 shard_map.59.keep
  16.5 3.6 %all-to-all-done = s32[16,1,2]{2,1,0:T(1,128)S(1)} async-done(((s32[16,1,2]{2,1,0:T(1,128)}), s32[16,1,2]{2,1,0:T(1,128)S(1)}, u32[]{:S(2)}, u32[]{:S(2)}) %all-to-all-start) | async-done | bytes 160 | tf_op jit(solution)/shard_map/all_to_all | solution.py:247
  20.1 0.0 collective-permute-done.other
  20.2 1.4 %shard_map.60 = s16[4,912,128]{2,1,0:T(8,128)(2,1)S(1)} custom-call(s32[16,2]{1,0:T(8,128)S(1)} %bitcast.11, bf16[2,2,8,112,128]{4,3,2,1,0:T(8,128)(2,1)S(1)} %shard_map.59.keep, bf16[64,14336]{1,0:T(8,128)(2,1)S(1)} %collective-permute-done.other), custom_call_target="tpu_custom_call" | custom-call | tf_op jit(solution)/shard_map/pallas_call | solution.py:268
  21.6 0.0 copy-start.1
  21.6 16.6 %all_to_all.28.got = s16[4,912,128]{2,1,0:T(8,128)(2,1)S(1)} all-to-all(s16[4,912,128]{2,1,0:T(8,128)(2,1)S(1)} %shard_map.60), channel_id=1, replica_groups=mesh['expert'=8,'x'=2,'zh'=8,'zl'=2,'c'=2] {'x','zl'}, dimensions={0} | all-to-all | bytes 1867776 | tf_op jit(solution)/shard_map/all_to_all | solution.py:247
  38.2 0.3 shard_map.61
  38.6 29.7 %all_to_all.29.refs_0_ = s16[8,120,128]{2,1,0:T(8,128)(2,1)S(1)} all-to-all(s16[8,120,128]{2,1,0:T(8,128)(2,1)S(1)} %shard_map.61), channel_id=1, replica_groups=mesh['expert'=8,'x'=2,'zh'=8,'zl'=2,'c'=2] {'zh'}, dimensions={0} | all-to-all | bytes 491520 | tf_op jit(solution)/shard_map/all_to_all | solution.py:247
  68.3 0.0 copy-done.1
  68.3 1.0 shard_map.62
  69.3 20.6 %all_to_all.30 = bf16[8,112,128]{2,1,0:T(8,128)(2,1)S(1)} all-to-all(bf16[8,112,128]{2,1,0:T(8,128)(2,1)S(1)} %get-tuple-element.5), channel_id=1, replica_groups=mesh['expert'=8,'x'=2,'zh'=8,'zl'=2,'c'=2] {'zh'}, dimensions={0} | all-to-all | bytes 458752 | tf_op jit(solution)/shard_map/all_to_all | solution.py:247
  89.9 0.1 broadcast_in_dim.7
  90.0 15.0 %all_to_all.31 = bf16[4,8,112,128]{3,2,1,0:T(8,128)(2,1)S(1)} all-to-all(bf16[4,8,112,128]{3,2,1,0:T(8,128)(2,1)S(1)} %broadcast_in_dim.7), channel_id=1, replica_groups=mesh['expert'=8,'x'=2,'zh'=8,'zl'=2,'c'=2] {'x','zl'}, dimensions={0} | all-to-all | bytes 1835008 | tf_op jit(solution)/shard_map/all_to_all | solution.py:247
  105.0 5.6 %collective-permute-start.1 = (bf16[4,8,112,128]{3,2,1,0:T(8,128)(2,1)S(1)}, bf16[4,8,112,128]{3,2,1,0:T(8,128)(2,1)S(1)}, u32[]{:S(2)}, u32[]{:S(2)}) collective-permute-start(bf16[4,8,112,128]{3,2,1,0:T(8,128)(2,1)S(1)} %all_to_all.31), channel_id=1, source_target_pairs={{0,1},{1,0},{2,3},{3,2},{4,5},{5,4},{6,7},{7,6},{8,9},{9,8},{10,11... | collective-permute-start | bytes 2752520 | tf_op jit(solution)/shard_map/ppermute | solution.py:283
  110.7 2.1 %collective-permute-done.1 = bf16[4,8,112,128]{3,2,1,0:T(8,128)(2,1)S(1)} collective-permute-done((bf16[4,8,112,128]{3,2,1,0:T(8,128)(2,1)S(1)}, bf16[4,8,112,128]{3,2,1,0:T(8,128)(2,1)S(1)}, u32[]{:S(2)}, u32[]{:S(2)}) %collective-permute-start.1) | collective-permute-done | bytes 917536 | tf_op jit(solution)/shard_map/ppermute | solution.py:283
  112.8 1.4 %shard_map.63 = bf16[64,14336]{1,0:T(8,128)(2,1)} custom-call(bf16[2,2,8,112,128]{4,3,2,1,0:T(8,128)(2,1)S(1)} %bitcast.7, bf16[2,2,8,112,128]{4,3,2,1,0:T(8,128)(2,1)S(1)} %bitcast.10), custom_call_target="tpu_custom_call" | custom-call | tf_op jit(solution)/shard_map/pallas_call | solution.py:285
Async XLA Ops:
  0.6 19.5 %collective-permute-start = (bf16[64,14336]{1,0:T(8,128)(2,1)}, bf16[64,14336]{1,0:T(8,128)(2,1)S(1)}, u32[]{:S(2)}, u32[]{:S(2)}) collective-permute-start(bf16[64,14336]{1,0:T(8,128)(2,1)} %bitcast.8), channel_id=1, source_target_pairs={{0,1},{1,0},{2,3},{3,2},{4,5},{5,4},{6,7},{7,6},{8,9},{9,8},{10,11... | collective-permute-start | bytes 5505032 | tf_op jit(solution)/shard_map/ppermute | solution.py:265
  11.4 8.7 %all-to-all-start = ((s32[16,1,2]{2,1,0:T(1,128)}), s32[16,1,2]{2,1,0:T(1,128)S(1)}, u32[]{:S(2)}, u32[]{:S(2)}) async-start(s32[16,1,2]{2,1,0:T(1,128)} %broadcast_in_dim.6), calls=%async_computation | async-start | bytes 16384 | tf_op jit(solution)/shard_map/all_to_all | solution.py:247
  14.8 1.5 %copy-start = (bf16[1,1,1,64,14336]{4,3,2,1,0:T(8,128)(2,1)S(1)}, bf16[1,1,1,64,14336]{4,3,2,1,0:T(8,128)(2,1)}, u32[]{:S(2)}) copy-start(bf16[1,1,1,64,14336]{4,3,2,1,0:T(8,128)(2,1)} %param.4) | copy-start | bytes 5505028
  21.6 46.7 %copy-start.1 = (f32[1,1,64,224]{3,2,1,0:T(8,128)S(1)}, f32[1,1,64,224]{3,2,1,0:T(8,128)}, u32[]{:S(2)}) copy-start(f32[1,1,64,224]{3,2,1,0:T(8,128)} %refs_1_.1) | copy-start | bytes 172036
  105.0 7.7 %collective-permute-start.1 = (bf16[4,8,112,128]{3,2,1,0:T(8,128)(2,1)S(1)}, bf16[4,8,112,128]{3,2,1,0:T(8,128)(2,1)S(1)}, u32[]{:S(2)}, u32[]{:S(2)}) collective-permute-start(bf16[4,8,112,128]{3,2,1,0:T(8,128)(2,1)S(1)} %all_to_all.31), channel_id=1, source_target_pairs={{0,1},{1,0},{2,3},{3,2},{4,5},{5,4},{6,7},{7,6},{8,9},{9,8},{10,11... | collective-permute-start | bytes 2752520 | tf_op jit(solution)/shard_map/ppermute | solution.py:283

commit v8 on v7

--- a/solution.py
+++ b/solution.py
@@ -26,6 +26,7 @@
 
 NOTES = 16
 FAR_NOTES = 8
+FIELD = 2**16
 TOP = 32767.0
 DIGIT = 4096.0
 MIDDLE = 32768.0
@@ -120,6 +121,10 @@
 
 def decoded(units, level):
     return (jnp.exp2(level * (1 / FINE)) * (1 / TOP)) * wide(units)
+
+
+def fields(both):
+    return both // FIELD, both % FIELD
 
 
 def own_pieces(fast, g, core):
@@ -156,9 +161,10 @@
 
     def body(core):
         pair = lax.axis_index("expert") * 2
-        tokens, steps = ([jnp.full((1, LANES), counts[pair + c, i].astype(F32)) for c in (core, 1 - core)] for i in range(2))
+        both = [counts[pair + c, 0] for c in (core, 1 - core)]
+        tokens, steps = ([jnp.full((1, LANES), v.astype(F32)) for v in f] for f in zip(*map(fields, both)))
         shares = [t / n for t, n in zip(tokens, steps)]
-        everywhere = sum(counts[i, 0] for i in range(counts.shape[0])).astype(F32)
+        everywhere = sum(fields(counts[i, 0])[0] for i in range(counts.shape[0])).astype(F32)
         work = sum(t * n for t, n in zip(tokens, steps))
         sums = (sum(tokens), work, *digits(sum(shares)), everywhere)
         levels = [[] for _ in range(out.shape[0])]
@@ -256,12 +262,10 @@
     groups = lax.axis_size("expert")
     nx, nzh = size["x"], size["zh"]
     fast = fast_weights[0, 0, 0]
-    half = fast.shape[1] // nx
-    halves = pl.BlockSpec((ROWS, half), lambda x: (0, x))
 
     plane = nx * size["zl"]
-    pair = jnp.concatenate([token_counts, step_counts], axis=1)
-    counts = swap(jnp.broadcast_to(pair, (groups * size["c"], 2)), ("expert", "c"))
+    both = token_counts * FIELD + step_counts
+    counts = swap(jnp.broadcast_to(both, (groups * size["c"], 1)), ("expert", "c"))
     other = lax.ppermute(fast, "c", [(0, 1), (1, 0)])
     shape = (nx, size["zl"], nzh, PIECE, LANES)
     keep = call(sort_kernel, struct(shape, BF16))(fast)
@@ -281,13 +285,14 @@
     column = swap(copies, "zh")
     own = swap(jnp.broadcast_to(column[None], (plane, *column.shape)), ("x", "zl"))
     other = lax.ppermute(own, "c", [(0, 1), (1, 0)])
-    planes = pl.BlockSpec((1, *shape[1:]), lambda x: (x, 0, 0, 0, 0))
+    cuts = 2
+    planes = pl.BlockSpec((1, size["zl"], nzh // cuts, PIECE, LANES), lambda x, j: (x, 0, j, 0, 0))
     reset = call(
         lay_out_kernel,
         struct(fast.shape, BF16),
-        grid=(nx,),
+        grid=(nx, cuts),
         in_specs=[planes, planes],
-        out_specs=halves,
+        out_specs=pl.BlockSpec((ROWS, nzh // cuts * WIDE), lambda x, j: (0, cuts * x + j)),
     )(own.reshape(shape), other.reshape(shape))
     return new_slow, reset[None, None]
 

time: 115 us -> 115 us (level)
  no operation moved by 1% of the time
where the time goes in v8:
time: 115 us
  blocking collectives  82 us (71%)
  starting transfers between devices  17.8 us (15%)
  waiting for transfers between devices  5.72 us (5%)
  Pallas kernels  5.1 us (4%)
  local copies, waits for them, and re-layouts  2.22 us (2%)
  between operations  1.99 us (2%)
    all_to_all x4, blocking collectives, swap(): return lax.all_to_all(pieces, axis, split_axis=0, concat_axis=0, tiled=True)  82 us
    ppermute x1, starting transfers between devices, shards(): other = lax.ppermute(fast, 'c', [(0, 1), (1, 0)])  8.79 us
    ppermute x1, starting transfers between devices, shards(): other = lax.ppermute(own, 'c', [(0, 1), (1, 0)])  5.63 us
    all_to_all x1, waiting for transfers between devices, swap(): return lax.all_to_all(pieces, axis, split_axis=0, concat_axis=0, tiled=True)  3.64 us
    all_to_all x1, starting transfers between devices, swap(): return lax.all_to_all(pieces, axis, split_axis=0, concat_axis=0, tiled=True)  3.37 us
  transfers between devices with their start and end apart: 3, of which 2 were waited for; matrix products, arithmetic and copies ran while one was open for 1% of the time, Pallas kernels for 0%

profile of v8, /device:TPU:1, one launch (start us, length us, event | category | flops | bytes accessed | tf_op | source)
XLA Modules:
  0.0 114.8 jit_solution(8050301306329097117)
XLA Ops:
  0.6 8.8 %collective-permute-start = (bf16[64,14336]{1,0:T(8,128)(2,1)}, bf16[64,14336]{1,0:T(8,128)(2,1)S(1)}, u32[]{:S(2)}, u32[]{:S(2)}) collective-permute-start(bf16[64,14336]{1,0:T(8,128)(2,1)} %bitcast.7), channel_id=1, source_target_pairs={{0,1},{1,0},{2,3},{3,2},{4,5},{5,4},{6,7},{7,6},{8,9},{9,8},{10,11... | collective-permute-start | bytes 5505032 | tf_op jit(solution)/shard_map/ppermute | solution.py:269
  10.7 0.6 broadcast_in_dim.17
  11.3 3.4 %all-to-all-start = ((s32[16,1,1]{2,1,0:T(1,128)}), s32[16,1,1]{2,1,0:T(1,128)S(1)}, u32[]{:S(2)}, u32[]{:S(2)}) async-start(s32[16,1,1]{2,1,0:T(1,128)} %broadcast_in_dim.17), calls=%async_computation | async-start | bytes 16384 | tf_op jit(solution)/shard_map/all_to_all | solution.py:253
  14.7 0.0 copy-start
  14.7 1.5 %copy-done = bf16[1,1,1,64,14336]{4,3,2,1,0:T(8,128)(2,1)S(1)} copy-done((bf16[1,1,1,64,14336]{4,3,2,1,0:T(8,128)(2,1)S(1)}, bf16[1,1,1,64,14336]{4,3,2,1,0:T(8,128)(2,1)}, u32[]{:S(2)}) %copy-start) | copy-done | bytes 1835032
  16.2 0.2 shard_map.59.keep
  16.4 3.6 %all-to-all-done = s32[16,1,1]{2,1,0:T(1,128)S(1)} async-done(((s32[16,1,1]{2,1,0:T(1,128)}), s32[16,1,1]{2,1,0:T(1,128)S(1)}, u32[]{:S(2)}, u32[]{:S(2)}) %all-to-all-start) | async-done | bytes 96 | tf_op jit(solution)/shard_map/all_to_all | solution.py:253
  20.1 0.0 collective-permute-done.other
  20.1 1.4 %shard_map.60 = s16[4,912,128]{2,1,0:T(8,128)(2,1)S(1)} custom-call(s32[16,1]{1,0:T(8,128)S(1)} %bitcast.10, bf16[2,2,8,112,128]{4,3,2,1,0:T(8,128)(2,1)S(1)} %shard_map.59.keep, bf16[64,14336]{1,0:T(8,128)(2,1)S(1)} %collective-permute-done.other), custom_call_target="tpu_custom_call" | custom-call | tf_op jit(solution)/shard_map/pallas_call | solution.py:272
  21.5 0.0 copy-start.1
  21.5 16.6 %all_to_all.28.got = s16[4,912,128]{2,1,0:T(8,128)(2,1)S(1)} all-to-all(s16[4,912,128]{2,1,0:T(8,128)(2,1)S(1)} %shard_map.60), channel_id=1, replica_groups=mesh['expert'=8,'x'=2,'zh'=8,'zl'=2,'c'=2] {'x','zl'}, dimensions={0} | all-to-all | bytes 1867776 | tf_op jit(solution)/shard_map/all_to_all | solution.py:253
  38.1 0.3 shard_map.61
  38.5 29.7 %all_to_all.29.refs_0_ = s16[8,120,128]{2,1,0:T(8,128)(2,1)S(1)} all-to-all(s16[8,120,128]{2,1,0:T(8,128)(2,1)S(1)} %shard_map.61), channel_id=1, replica_groups=mesh['expert'=8,'x'=2,'zh'=8,'zl'=2,'c'=2] {'zh'}, dimensions={0} | all-to-all | bytes 491520 | tf_op jit(solution)/shard_map/all_to_all | solution.py:253
  68.2 0.0 copy-done.1
  68.2 1.0 shard_map.62
  69.2 20.6 %all_to_all.30 = bf16[8,112,128]{2,1,0:T(8,128)(2,1)S(1)} all-to-all(bf16[8,112,128]{2,1,0:T(8,128)(2,1)S(1)} %get-tuple-element.5), channel_id=1, replica_groups=mesh['expert'=8,'x'=2,'zh'=8,'zl'=2,'c'=2] {'zh'}, dimensions={0} | all-to-all | bytes 458752 | tf_op jit(solution)/shard_map/all_to_all | solution.py:253
  89.8 0.1 broadcast_in_dim.18
  89.9 15.0 %all_to_all.31 = bf16[4,8,112,128]{3,2,1,0:T(8,128)(2,1)S(1)} all-to-all(bf16[4,8,112,128]{3,2,1,0:T(8,128)(2,1)S(1)} %broadcast_in_dim.18), channel_id=1, replica_groups=mesh['expert'=8,'x'=2,'zh'=8,'zl'=2,'c'=2] {'x','zl'}, dimensions={0} | all-to-all | bytes 1835008 | tf_op jit(solution)/shard_map/all_to_all | solution.py:253
  105.0 5.6 %collective-permute-start.1 = (bf16[4,8,112,128]{3,2,1,0:T(8,128)(2,1)S(1)}, bf16[4,8,112,128]{3,2,1,0:T(8,128)(2,1)S(1)}, u32[]{:S(2)}, u32[]{:S(2)}) collective-permute-start(bf16[4,8,112,128]{3,2,1,0:T(8,128)(2,1)S(1)} %all_to_all.31), channel_id=1, source_target_pairs={{0,1},{1,0},{2,3},{3,2},{4,5},{5,4},{6,7},{7,6},{8,9},{9,8},{10,11... | collective-permute-start | bytes 2752520 | tf_op jit(solution)/shard_map/ppermute | solution.py:287
  110.6 2.1 %collective-permute-done.1 = bf16[4,8,112,128]{3,2,1,0:T(8,128)(2,1)S(1)} collective-permute-done((bf16[4,8,112,128]{3,2,1,0:T(8,128)(2,1)S(1)}, bf16[4,8,112,128]{3,2,1,0:T(8,128)(2,1)S(1)}, u32[]{:S(2)}, u32[]{:S(2)}) %collective-permute-start.1) | collective-permute-done | bytes 917536 | tf_op jit(solution)/shard_map/ppermute | solution.py:287
  112.7 2.1 %shard_map.63 = bf16[64,14336]{1,0:T(8,128)(2,1)} custom-call(bf16[2,2,8,112,128]{4,3,2,1,0:T(8,128)(2,1)S(1)} %bitcast.6, bf16[2,2,8,112,128]{4,3,2,1,0:T(8,128)(2,1)S(1)} %bitcast.9), custom_call_target="tpu_custom_call" | custom-call | tf_op jit(solution)/shard_map/pallas_call | solution.py:290
Async XLA Ops:
  0.6 19.4 %collective-permute-start = (bf16[64,14336]{1,0:T(8,128)(2,1)}, bf16[64,14336]{1,0:T(8,128)(2,1)S(1)}, u32[]{:S(2)}, u32[]{:S(2)}) collective-permute-start(bf16[64,14336]{1,0:T(8,128)(2,1)} %bitcast.7), channel_id=1, source_target_pairs={{0,1},{1,0},{2,3},{3,2},{4,5},{5,4},{6,7},{7,6},{8,9},{9,8},{10,11... | collective-permute-start | bytes 5505032 | tf_op jit(solution)/shard_map/ppermute | solution.py:269
  11.3 8.7 %all-to-all-start = ((s32[16,1,1]{2,1,0:T(1,128)}), s32[16,1,1]{2,1,0:T(1,128)S(1)}, u32[]{:S(2)}, u32[]{:S(2)}) async-start(s32[16,1,1]{2,1,0:T(1,128)} %broadcast_in_dim.17), calls=%async_computation | async-start | bytes 16384 | tf_op jit(solution)/shard_map/all_to_all | solution.py:253
  14.7 1.5 %copy-start = (bf16[1,1,1,64,14336]{4,3,2,1,0:T(8,128)(2,1)S(1)}, bf16[1,1,1,64,14336]{4,3,2,1,0:T(8,128)(2,1)}, u32[]{:S(2)}) copy-start(bf16[1,1,1,64,14336]{4,3,2,1,0:T(8,128)(2,1)} %param.4) | copy-start | bytes 5505028
  21.5 46.7 %copy-start.1 = (f32[1,1,64,224]{3,2,1,0:T(8,128)S(1)}, f32[1,1,64,224]{3,2,1,0:T(8,128)}, u32[]{:S(2)}) copy-start(f32[1,1,64,224]{3,2,1,0:T(8,128)} %refs_1_.1) | copy-start | bytes 172036
  105.0 7.7 %collective-permute-start.1 = (bf16[4,8,112,128]{3,2,1,0:T(8,128)(2,1)S(1)}, bf16[4,8,112,128]{3,2,1,0:T(8,128)(2,1)S(1)}, u32[]{:S(2)}, u32[]{:S(2)}) collective-permute-start(bf16[4,8,112,128]{3,2,1,0:T(8,128)(2,1)S(1)} %all_to_all.31), channel_id=1, source_target_pairs={{0,1},{1,0},{2,3},{3,2},{4,5},{5,4},{6,7},{7,6},{8,9},{9,8},{10,11... | collective-permute-start | bytes 2752520 | tf_op jit(solution)/shard_map/ppermute | solution.py:287

commit v9 on v8

--- a/solution.py
+++ b/solution.py
@@ -27,6 +27,7 @@
 NOTES = 16
 FAR_NOTES = 8
 FIELD = 2**16
+PARTS = 8
 TOP = 32767.0
 DIGIT = 4096.0
 MIDDLE = 32768.0
@@ -221,17 +222,29 @@
                 copies[i, ROWS:] = rest.astype(BF16)
 
 
-def lay_out_kernel(own, other, out):
+def lay_out_kernel(own, other, out, whole, sems):
+    n_zh = own.shape[2]
+    part = whole.shape[1] // sems.shape[0]
+
     def body(pieces):
         group = lane_group((ROWS, LANES))
-        for zh in range(own.shape[2]):
-            at = zh * WIDE
+        stores = []
+        for g in range(whole.shape[1] // WIDE):
+            x, zh = divmod(g, n_zh)
+            at = g * WIDE
             for k in range(QUAD):
-                out[:, at + 2 * k * LANES : at + (2 * k + 1) * LANES] = pieces[k % 2][0, k // 2, zh, :ROWS]
-            res = [unfolded(pieces[k % 2][0, k // 2, zh, ROWS:].astype(F32), k) for k in range(QUAD)]
+                whole[:, at + 2 * k * LANES : at + (2 * k + 1) * LANES] = pieces[k % 2][x, k // 2, zh, :ROWS]
+            res = [unfolded(pieces[k % 2][x, k // 2, zh, ROWS:].astype(F32), k) for k in range(QUAD)]
             for k in range(QUAD - 1):
                 odd = jnp.where(group < QUAD - 1 - k, res[k], res[k + 1])
-                out[:, at + (2 * k + 1) * LANES : at + (2 * k + 2) * LANES] = odd.astype(BF16)
+                whole[:, at + (2 * k + 1) * LANES : at + (2 * k + 2) * LANES] = odd.astype(BF16)
+            if (at + WIDE) % part == 0:
+                i = at // part
+                span = pl.ds(i * part, part)
+                stores.append(pltpu.make_async_copy(whole.at[:, span], out.at[:, span], sems.at[i]))
+                stores[-1].start()
+        for store in stores:
+            store.wait()
 
     for_core(lambda: body((own, other)), lambda: body((other, own)))
 
@@ -285,14 +298,11 @@
     column = swap(copies, "zh")
     own = swap(jnp.broadcast_to(column[None], (plane, *column.shape)), ("x", "zl"))
     other = lax.ppermute(own, "c", [(0, 1), (1, 0)])
-    cuts = 2
-    planes = pl.BlockSpec((1, size["zl"], nzh // cuts, PIECE, LANES), lambda x, j: (x, 0, j, 0, 0))
     reset = call(
         lay_out_kernel,
         struct(fast.shape, BF16),
-        grid=(nx, cuts),
-        in_specs=[planes, planes],
-        out_specs=pl.BlockSpec((ROWS, nzh // cuts * WIDE), lambda x, j: (0, cuts * x + j)),
+        out_specs=pl.BlockSpec(memory_space=pltpu.HBM),
+        scratch_shapes=[pltpu.VMEM(fast.shape, BF16), pltpu.SemaphoreType.DMA((PARTS,))],
     )(own.reshape(shape), other.reshape(shape))
     return new_slow, reset[None, None]
 

time: 115 us -> 115 us (level)
  no operation moved by 1% of the time
where the time goes in v9:
time: 115 us; the launch traced here: 114 us
  blocking collectives  82 us (71%)
  starting transfers between devices  17.8 us (15%)
  waiting for transfers between devices  5.72 us (5%)
  Pallas kernels  4.41 us (4%)
  local copies, waits for them, and re-layouts  2.22 us (2%)
  between operations  1.99 us (2%)
    all_to_all x4, blocking collectives, swap(): return lax.all_to_all(pieces, axis, split_axis=0, concat_axis=0, tiled=True)  82 us
    ppermute x1, starting transfers between devices, shards(): other = lax.ppermute(fast, 'c', [(0, 1), (1, 0)])  8.79 us
    ppermute x1, starting transfers between devices, shards(): other = lax.ppermute(own, 'c', [(0, 1), (1, 0)])  5.63 us
    all_to_all x1, waiting for transfers between devices, swap(): return lax.all_to_all(pieces, axis, split_axis=0, concat_axis=0, tiled=True)  3.64 us
    all_to_all x1, starting transfers between devices, swap(): return lax.all_to_all(pieces, axis, split_axis=0, concat_axis=0, tiled=True)  3.37 us
  transfers between devices with their start and end apart: 3, of which 2 were waited for; matrix products, arithmetic and copies ran while one was open for 1% of the time, Pallas kernels for 0%

profile of v9, /device:TPU:1, one launch (start us, length us, event | category | flops | bytes accessed | tf_op | source)
XLA Modules:
  0.0 114.1 jit_solution(8238574970877636621)
XLA Ops:
  0.6 8.8 %collective-permute-start = (bf16[64,14336]{1,0:T(8,128)(2,1)}, bf16[64,14336]{1,0:T(8,128)(2,1)S(1)}, u32[]{:S(2)}, u32[]{:S(2)}) collective-permute-start(bf16[64,14336]{1,0:T(8,128)(2,1)} %bitcast.7), channel_id=1, source_target_pairs={{0,1},{1,0},{2,3},{3,2},{4,5},{5,4},{6,7},{7,6},{8,9},{9,8},{10,11... | collective-permute-start | bytes 5505032 | tf_op jit(solution)/shard_map/ppermute | solution.py:282
  10.7 0.6 broadcast_in_dim.17
  11.3 3.4 %all-to-all-start = ((s32[16,1,1]{2,1,0:T(1,128)}), s32[16,1,1]{2,1,0:T(1,128)S(1)}, u32[]{:S(2)}, u32[]{:S(2)}) async-start(s32[16,1,1]{2,1,0:T(1,128)} %broadcast_in_dim.17), calls=%async_computation | async-start | bytes 16384 | tf_op jit(solution)/shard_map/all_to_all | solution.py:266
  14.7 0.0 copy-start
  14.7 1.5 %copy-done = bf16[1,1,1,64,14336]{4,3,2,1,0:T(8,128)(2,1)S(1)} copy-done((bf16[1,1,1,64,14336]{4,3,2,1,0:T(8,128)(2,1)S(1)}, bf16[1,1,1,64,14336]{4,3,2,1,0:T(8,128)(2,1)}, u32[]{:S(2)}) %copy-start) | copy-done | bytes 1835032
  16.2 0.2 shard_map.59.keep
  16.4 3.6 %all-to-all-done = s32[16,1,1]{2,1,0:T(1,128)S(1)} async-done(((s32[16,1,1]{2,1,0:T(1,128)}), s32[16,1,1]{2,1,0:T(1,128)S(1)}, u32[]{:S(2)}, u32[]{:S(2)}) %all-to-all-start) | async-done | bytes 96 | tf_op jit(solution)/shard_map/all_to_all | solution.py:266
  20.1 0.0 collective-permute-done.other
  20.1 1.4 %shard_map.60 = s16[4,912,128]{2,1,0:T(8,128)(2,1)S(1)} custom-call(s32[16,1]{1,0:T(8,128)S(1)} %bitcast.10, bf16[2,2,8,112,128]{4,3,2,1,0:T(8,128)(2,1)S(1)} %shard_map.59.keep, bf16[64,14336]{1,0:T(8,128)(2,1)S(1)} %collective-permute-done.other), custom_call_target="tpu_custom_call" | custom-call | tf_op jit(solution)/shard_map/pallas_call | solution.py:285
  21.5 0.0 copy-start.1
  21.5 16.6 %all_to_all.28.got = s16[4,912,128]{2,1,0:T(8,128)(2,1)S(1)} all-to-all(s16[4,912,128]{2,1,0:T(8,128)(2,1)S(1)} %shard_map.60), channel_id=1, replica_groups=mesh['expert'=8,'x'=2,'zh'=8,'zl'=2,'c'=2] {'x','zl'}, dimensions={0} | all-to-all | bytes 1867776 | tf_op jit(solution)/shard_map/all_to_all | solution.py:266
  38.1 0.3 shard_map.61
  38.5 29.7 %all_to_all.29.refs_0_ = s16[8,120,128]{2,1,0:T(8,128)(2,1)S(1)} all-to-all(s16[8,120,128]{2,1,0:T(8,128)(2,1)S(1)} %shard_map.61), channel_id=1, replica_groups=mesh['expert'=8,'x'=2,'zh'=8,'zl'=2,'c'=2] {'zh'}, dimensions={0} | all-to-all | bytes 491520 | tf_op jit(solution)/shard_map/all_to_all | solution.py:266
  68.2 0.0 copy-done.1
  68.2 1.0 shard_map.62
  69.2 20.6 %all_to_all.30 = bf16[8,112,128]{2,1,0:T(8,128)(2,1)S(1)} all-to-all(bf16[8,112,128]{2,1,0:T(8,128)(2,1)S(1)} %get-tuple-element.5), channel_id=1, replica_groups=mesh['expert'=8,'x'=2,'zh'=8,'zl'=2,'c'=2] {'zh'}, dimensions={0} | all-to-all | bytes 458752 | tf_op jit(solution)/shard_map/all_to_all | solution.py:266
  89.8 0.1 broadcast_in_dim.18
  89.9 15.0 %all_to_all.31 = bf16[4,8,112,128]{3,2,1,0:T(8,128)(2,1)S(1)} all-to-all(bf16[4,8,112,128]{3,2,1,0:T(8,128)(2,1)S(1)} %broadcast_in_dim.18), channel_id=1, replica_groups=mesh['expert'=8,'x'=2,'zh'=8,'zl'=2,'c'=2] {'x','zl'}, dimensions={0} | all-to-all | bytes 1835008 | tf_op jit(solution)/shard_map/all_to_all | solution.py:266
  105.0 5.6 %collective-permute-start.1 = (bf16[4,8,112,128]{3,2,1,0:T(8,128)(2,1)S(1)}, bf16[4,8,112,128]{3,2,1,0:T(8,128)(2,1)S(1)}, u32[]{:S(2)}, u32[]{:S(2)}) collective-permute-start(bf16[4,8,112,128]{3,2,1,0:T(8,128)(2,1)S(1)} %all_to_all.31), channel_id=1, source_target_pairs={{0,1},{1,0},{2,3},{3,2},{4,5},{5,4},{6,7},{7,6},{8,9},{9,8},{10,11... | collective-permute-start | bytes 2752520 | tf_op jit(solution)/shard_map/ppermute | solution.py:300
  110.6 2.1 %collective-permute-done.1 = bf16[4,8,112,128]{3,2,1,0:T(8,128)(2,1)S(1)} collective-permute-done((bf16[4,8,112,128]{3,2,1,0:T(8,128)(2,1)S(1)}, bf16[4,8,112,128]{3,2,1,0:T(8,128)(2,1)S(1)}, u32[]{:S(2)}, u32[]{:S(2)}) %collective-permute-start.1) | collective-permute-done | bytes 917536 | tf_op jit(solution)/shard_map/ppermute | solution.py:300
  112.7 1.4 %shard_map.63 = bf16[64,14336]{1,0:T(8,128)(2,1)} custom-call(bf16[2,2,8,112,128]{4,3,2,1,0:T(8,128)(2,1)S(1)} %bitcast.6, bf16[2,2,8,112,128]{4,3,2,1,0:T(8,128)(2,1)S(1)} %bitcast.9), custom_call_target="tpu_custom_call" | custom-call | tf_op jit(solution)/shard_map/pallas_call | solution.py:301
Async XLA Ops:
  0.6 19.4 %collective-permute-start = (bf16[64,14336]{1,0:T(8,128)(2,1)}, bf16[64,14336]{1,0:T(8,128)(2,1)S(1)}, u32[]{:S(2)}, u32[]{:S(2)}) collective-permute-start(bf16[64,14336]{1,0:T(8,128)(2,1)} %bitcast.7), channel_id=1, source_target_pairs={{0,1},{1,0},{2,3},{3,2},{4,5},{5,4},{6,7},{7,6},{8,9},{9,8},{10,11... | collective-permute-start | bytes 5505032 | tf_op jit(solution)/shard_map/ppermute | solution.py:282
  11.3 8.7 %all-to-all-start = ((s32[16,1,1]{2,1,0:T(1,128)}), s32[16,1,1]{2,1,0:T(1,128)S(1)}, u32[]{:S(2)}, u32[]{:S(2)}) async-start(s32[16,1,1]{2,1,0:T(1,128)} %broadcast_in_dim.17), calls=%async_computation | async-start | bytes 16384 | tf_op jit(solution)/shard_map/all_to_all | solution.py:266
  14.7 1.5 %copy-start = (bf16[1,1,1,64,14336]{4,3,2,1,0:T(8,128)(2,1)S(1)}, bf16[1,1,1,64,14336]{4,3,2,1,0:T(8,128)(2,1)}, u32[]{:S(2)}) copy-start(bf16[1,1,1,64,14336]{4,3,2,1,0:T(8,128)(2,1)} %param.4) | copy-start | bytes 5505028
  21.5 46.7 %copy-start.1 = (f32[1,1,64,224]{3,2,1,0:T(8,128)S(1)}, f32[1,1,64,224]{3,2,1,0:T(8,128)}, u32[]{:S(2)}) copy-start(f32[1,1,64,224]{3,2,1,0:T(8,128)} %refs_1_.1) | copy-start | bytes 172036
  105.0 7.7 %collective-permute-start.1 = (bf16[4,8,112,128]{3,2,1,0:T(8,128)(2,1)S(1)}, bf16[4,8,112,128]{3,2,1,0:T(8,128)(2,1)S(1)}, u32[]{:S(2)}, u32[]{:S(2)}) collective-permute-start(bf16[4,8,112,128]{3,2,1,0:T(8,128)(2,1)S(1)} %all_to_all.31), channel_id=1, source_target_pairs={{0,1},{1,0},{2,3},{3,2},{4,5},{5,4},{6,7},{7,6},{8,9},{9,8},{10,11... | collective-permute-start | bytes 2752520 | tf_op jit(solution)/shard_map/ppermute | solution.py:300

commit v10 on v9

--- a/solution.py
+++ b/solution.py
@@ -144,8 +144,19 @@
     return pieces
 
 
-def sort_kernel(fast, keep):
+def for_own_place(body):
+    place = own_place()
+    for k in range(QUAD):
+        pl.when(place == k)(lambda k=k: body(k))
+
+
+def sort_kernel(fast, slow, keep, mine):
     nx, n_zl, n_zh = keep.shape[:3]
+
+    def pack(k):
+        mine[:ROWS], mine[ROWS:] = own_parts(slow[0, 0], k)
+
+    for_own_place(pack)
 
     def body(core):
         for g in range(nx * n_zh):
@@ -197,7 +208,7 @@
         out[zh, PIECE:] = short(in_rows((level, *far), FAR_NOTES))
 
 
-def refresh_kernel(groups, got, slow, new_slow, copies):
+def refresh_kernel(groups, got, mine, fresh, copies):
     total = sums = None
     for s in range(got.shape[0]):
         notes = wide(got[s, PIECE:])
@@ -208,37 +219,56 @@
     everywhere = sums[4:5] + MIDDLE * got.shape[0]
     qsum = from_digits(sums[5:6], sums[6:7], sums[7:8])
     rate = outer_rate * groups * work / (tok * everywhere)
-    place = own_place()
-    for k in range(QUAD):
-
-        @pl.when(place == k)
-        def _(k=k):
-            mine = own_parts(slow[0, 0], k)
-            tile = mine[0] + rate * (total[:ROWS] - qsum * mine[0])
-            rest = mine[1] + rate * (total[ROWS:] - qsum * mine[1])
-            new_slow[0, 0] = own_block(tile, rest, k)
-            for i in range(copies.shape[0]):
-                copies[i, :ROWS] = tile.astype(BF16)
-                copies[i, ROWS:] = rest.astype(BF16)
-
-
-def lay_out_kernel(own, other, out, whole, sems):
-    n_zh = own.shape[2]
+    new = mine[...] + rate * (total - qsum * mine[...])
+    fresh[...] = new
+    for i in range(copies.shape[0]):
+        copies[i] = new.astype(BF16)
+
+
+def side_kernel(fresh, own, new_slow, half):
+    def unpack(k):
+        new_slow[0, 0] = own_block(fresh[:ROWS], fresh[ROWS:], k)
+
+    for_own_place(unpack)
+
+    def body(core):
+        for at, k, piece in pieces_of(own, core):
+            half[:, at + 2 * k * LANES : at + (2 * k + 1) * LANES] = piece[:ROWS]
+            res = unfolded(piece[ROWS:].astype(F32), k).astype(BF16)
+            for i in beside(k):
+                half[:, at + i * LANES : at + (i + 1) * LANES] = res
+
+    for_core(lambda: body(0), lambda: body(1))
+
+
+def pieces_of(pieces, core):
+    for g in range(pieces.shape[0] * pieces.shape[2]):
+        x, zh = divmod(g, pieces.shape[2])
+        for zl in range(pieces.shape[1]):
+            yield g * WIDE, 2 * zl + core, pieces[x, zl, zh]
+
+
+def beside(k):
+    return [i for i in (2 * k - 1, 2 * k + 1) if 0 < i < 2 * QUAD - 1]
+
+
+def lay_out_kernel(half, other, out, whole, sems):
     part = whole.shape[1] // sems.shape[0]
-
-    def body(pieces):
-        group = lane_group((ROWS, LANES))
+    group = lane_group((ROWS, LANES))
+
+    def body(core):
         stores = []
-        for g in range(whole.shape[1] // WIDE):
-            x, zh = divmod(g, n_zh)
-            at = g * WIDE
-            for k in range(QUAD):
-                whole[:, at + 2 * k * LANES : at + (2 * k + 1) * LANES] = pieces[k % 2][x, k // 2, zh, :ROWS]
-            res = [unfolded(pieces[k % 2][x, k // 2, zh, ROWS:].astype(F32), k) for k in range(QUAD)]
-            for k in range(QUAD - 1):
-                odd = jnp.where(group < QUAD - 1 - k, res[k], res[k + 1])
-                whole[:, at + (2 * k + 1) * LANES : at + (2 * k + 2) * LANES] = odd.astype(BF16)
-            if (at + WIDE) % part == 0:
+        for at, k, piece in pieces_of(other, 1 - core):
+            mine = at + 2 * (k + 2 * core - 1) * LANES
+            whole[:, mine : mine + LANES] = half[:, mine : mine + LANES]
+            whole[:, at + 2 * k * LANES : at + (2 * k + 1) * LANES] = piece[:ROWS]
+            res = unfolded(piece[ROWS:].astype(F32), k)
+            for i in beside(k):
+                span = slice(at + i * LANES, at + (i + 1) * LANES)
+                left = group < QUAD - 1 - i // 2
+                theirs = left if i > 2 * k else jnp.logical_not(left)
+                whole[:, span] = jnp.where(theirs, res, half[:, span].astype(F32)).astype(BF16)
+            if k // 2 == 1 and (at + WIDE) % part == 0:
                 i = at // part
                 span = pl.ds(i * part, part)
                 stores.append(pltpu.make_async_copy(whole.at[:, span], out.at[:, span], sems.at[i]))
@@ -246,7 +276,7 @@
         for store in stores:
             store.wait()
 
-    for_core(lambda: body((own, other)), lambda: body((other, own)))
+    for_core(lambda: body(0), lambda: body(1))
 
 
 def call(kernel, out_shape, **more):
@@ -281,7 +311,8 @@
     counts = swap(jnp.broadcast_to(both, (groups * size["c"], 1)), ("expert", "c"))
     other = lax.ppermute(fast, "c", [(0, 1), (1, 0)])
     shape = (nx, size["zl"], nzh, PIECE, LANES)
-    keep = call(sort_kernel, struct(shape, BF16))(fast)
+    block = struct((PIECE, LANES), F32)
+    keep, mine = call(sort_kernel, (struct(shape, BF16), block))(fast, slow_weights)
     pairs = call(
         pair_sum_kernel,
         struct((plane, nzh * PIECE + NOTES, LANES), jnp.int16),
@@ -290,20 +321,22 @@
     got = swap(pairs, ("x", "zl"))
     sums = call(near_sum_kernel, struct((nzh, PIECE + FAR_NOTES, LANES), jnp.int16))(got)
     got = swap(sums, "zh")
-    new_slow, copies = call(
-        lambda *refs: refresh_kernel(groups, *refs),
-        (struct(slow_weights.shape, F32), struct((nzh, PIECE, LANES), BF16)),
-    )(got, slow_weights)
+    fresh, copies = call(
+        lambda *refs: refresh_kernel(groups, *refs), (block, struct((nzh, PIECE, LANES), BF16))
+    )(got, mine)
 
     column = swap(copies, "zh")
     own = swap(jnp.broadcast_to(column[None], (plane, *column.shape)), ("x", "zl"))
     other = lax.ppermute(own, "c", [(0, 1), (1, 0)])
+    new_slow, half = call(side_kernel, (struct(slow_weights.shape, F32), struct(fast.shape, BF16)))(
+        fresh, own.reshape(shape)
+    )
     reset = call(
         lay_out_kernel,
         struct(fast.shape, BF16),
         out_specs=pl.BlockSpec(memory_space=pltpu.HBM),
         scratch_shapes=[pltpu.VMEM(fast.shape, BF16), pltpu.SemaphoreType.DMA((PARTS,))],
-    )(own.reshape(shape), other.reshape(shape))
+    )(half, other.reshape(shape))
     return new_slow, reset[None, None]
 
 

time: 115 us -> 113 us (0.983)
  waiting for transfers between devices: 5.72 us -> 3.71 us
  transfers between devices with their start and end apart: 3 -> 3, of which waited for: 2 -> 2; matrix products, arithmetic and copies ran while one was open for 1% -> 1% of each run, Pallas kernels for 0% -> 1%
where the time goes in v10:
time: 113 us
  blocking collectives  81.6 us (72%)
  starting transfers between devices  17.8 us (16%)
  Pallas kernels  4.7 us (4%)
  waiting for transfers between devices  3.71 us (3%)
  local copies, waits for them, and re-layouts  3.06 us (3%)
  between operations  1.98 us (2%)
    all_to_all x4, blocking collectives, swap(): return lax.all_to_all(pieces, axis, split_axis=0, concat_axis=0, tiled=True)  81.6 us
    ppermute x1, starting transfers between devices, shards(): other = lax.ppermute(fast, 'c', [(0, 1), (1, 0)])  8.79 us
    ppermute x1, starting transfers between devices, shards(): other = lax.ppermute(own, 'c', [(0, 1), (1, 0)])  5.62 us
    all_to_all x1, starting transfers between devices, swap(): return lax.all_to_all(pieces, axis, split_axis=0, concat_axis=0, tiled=True)  3.37 us
    all_to_all x1, waiting for transfers between devices, swap(): return lax.all_to_all(pieces, axis, split_axis=0, concat_axis=0, tiled=True)  2.65 us
    unnamed x4, local copies, waits for them, and re-layouts  2.33 us
  transfers between devices with their start and end apart: 3, of which 2 were waited for; matrix products, arithmetic and copies ran while one was open for 1% of the time, Pallas kernels for 1%

profile of v10, /device:TPU:1, one launch (start us, length us, event | category | flops | bytes accessed | tf_op | source)
XLA Modules:
  0.0 112.8 jit_solution(1021700851801977630)
XLA Ops:
  0.6 8.8 %collective-permute-start = (bf16[64,14336]{1,0:T(8,128)(2,1)}, bf16[64,14336]{1,0:T(8,128)(2,1)S(1)}, u32[]{:S(2)}, u32[]{:S(2)}) collective-permute-start(bf16[64,14336]{1,0:T(8,128)(2,1)} %bitcast.7), channel_id=1, source_target_pairs={{0,1},{1,0},{2,3},{3,2},{4,5},{5,4},{6,7},{7,6},{8,9},{9,8},{10,11... | collective-permute-start | bytes 5505032 | tf_op jit(solution)/shard_map/ppermute | solution.py:312
  10.7 0.6 broadcast_in_dim.17
  11.3 3.4 %all-to-all-start = ((s32[16,1,1]{2,1,0:T(1,128)}), s32[16,1,1]{2,1,0:T(1,128)S(1)}, u32[]{:S(2)}, u32[]{:S(2)}) async-start(s32[16,1,1]{2,1,0:T(1,128)} %broadcast_in_dim.17), calls=%async_computation | async-start | bytes 16384 | tf_op jit(solution)/shard_map/all_to_all | solution.py:296
  14.7 0.0 copy-start
  14.7 1.5 %copy-done = bf16[1,1,1,64,14336]{4,3,2,1,0:T(8,128)(2,1)S(1)} copy-done((bf16[1,1,1,64,14336]{4,3,2,1,0:T(8,128)(2,1)S(1)}, bf16[1,1,1,64,14336]{4,3,2,1,0:T(8,128)(2,1)}, u32[]{:S(2)}) %copy-start) | copy-done | bytes 1835032
  16.2 0.0 copy-start.1
  16.2 0.8 copy-done.1
  17.0 0.4 shard_map.59
  17.4 2.7 %all-to-all-done = s32[16,1,1]{2,1,0:T(1,128)S(1)} async-done(((s32[16,1,1]{2,1,0:T(1,128)}), s32[16,1,1]{2,1,0:T(1,128)S(1)}, u32[]{:S(2)}, u32[]{:S(2)}) %all-to-all-start) | async-done | bytes 96 | tf_op jit(solution)/shard_map/all_to_all | solution.py:296
  20.1 0.0 collective-permute-done.other
  20.1 1.4 %shard_map.60 = s16[4,912,128]{2,1,0:T(8,128)(2,1)S(1)} custom-call(s32[16,1]{1,0:T(8,128)S(1)} %bitcast.10, bf16[2,2,8,112,128]{4,3,2,1,0:T(8,128)(2,1)S(1)} %get-tuple-element.8.keep, bf16[64,14336]{1,0:T(8,128)(2,1)S(1)} %collective-permute-done.other), custom_call_target="tpu_custom_call" | custom-call | tf_op jit(solution)/shard_map/pallas_call | solution.py:316
  21.5 16.5 %all_to_all.28.got = s16[4,912,128]{2,1,0:T(8,128)(2,1)S(1)} all-to-all(s16[4,912,128]{2,1,0:T(8,128)(2,1)S(1)} %shard_map.60), channel_id=1, replica_groups=mesh['expert'=8,'x'=2,'zh'=8,'zl'=2,'c'=2] {'x','zl'}, dimensions={0} | all-to-all | bytes 1867776 | tf_op jit(solution)/shard_map/all_to_all | solution.py:296
  38.0 0.3 shard_map.61
  38.4 29.7 %all_to_all.29.refs_0_ = s16[8,120,128]{2,1,0:T(8,128)(2,1)S(1)} all-to-all(s16[8,120,128]{2,1,0:T(8,128)(2,1)S(1)} %shard_map.61), channel_id=1, replica_groups=mesh['expert'=8,'x'=2,'zh'=8,'zl'=2,'c'=2] {'zh'}, dimensions={0} | all-to-all | bytes 491520 | tf_op jit(solution)/shard_map/all_to_all | solution.py:296
  68.1 0.1 shard_map.62
  68.1 20.5 %all_to_all.30 = bf16[8,112,128]{2,1,0:T(8,128)(2,1)S(1)} all-to-all(bf16[8,112,128]{2,1,0:T(8,128)(2,1)S(1)} %get-tuple-element.11), channel_id=1, replica_groups=mesh['expert'=8,'x'=2,'zh'=8,'zl'=2,'c'=2] {'zh'}, dimensions={0} | all-to-all | bytes 458752 | tf_op jit(solution)/shard_map/all_to_all | solution.py:296
  88.7 0.1 broadcast_in_dim.18
  88.8 14.9 %all_to_all.31 = bf16[4,8,112,128]{3,2,1,0:T(8,128)(2,1)S(1)} all-to-all(bf16[4,8,112,128]{3,2,1,0:T(8,128)(2,1)S(1)} %broadcast_in_dim.18), channel_id=1, replica_groups=mesh['expert'=8,'x'=2,'zh'=8,'zl'=2,'c'=2] {'x','zl'}, dimensions={0} | all-to-all | bytes 1835008 | tf_op jit(solution)/shard_map/all_to_all | solution.py:296
  103.7 5.6 %collective-permute-start.1 = (bf16[4,8,112,128]{3,2,1,0:T(8,128)(2,1)S(1)}, bf16[4,8,112,128]{3,2,1,0:T(8,128)(2,1)S(1)}, u32[]{:S(2)}, u32[]{:S(2)}) collective-permute-start(bf16[4,8,112,128]{3,2,1,0:T(8,128)(2,1)S(1)} %all_to_all.31), channel_id=1, source_target_pairs={{0,1},{1,0},{2,3},{3,2},{4,5},{5,4},{6,7},{7,6},{8,9},{9,8},{10,11... | collective-permute-start | bytes 2752520 | tf_op jit(solution)/shard_map/ppermute | solution.py:330
  109.3 1.0 shard_map.63
  110.3 1.1 collective-permute-done.1
  111.4 1.4 %shard_map.64 = bf16[64,14336]{1,0:T(8,128)(2,1)} custom-call(bf16[64,14336]{1,0:T(8,128)(2,1)S(1)} %get-tuple-element.13.half, bf16[2,2,8,112,128]{4,3,2,1,0:T(8,128)(2,1)S(1)} %bitcast.9), custom_call_target="tpu_custom_call" | custom-call | tf_op jit(solution)/shard_map/pallas_call | solution.py:334
Async XLA Ops:
  0.6 19.4 %collective-permute-start = (bf16[64,14336]{1,0:T(8,128)(2,1)}, bf16[64,14336]{1,0:T(8,128)(2,1)S(1)}, u32[]{:S(2)}, u32[]{:S(2)}) collective-permute-start(bf16[64,14336]{1,0:T(8,128)(2,1)} %bitcast.7), channel_id=1, source_target_pairs={{0,1},{1,0},{2,3},{3,2},{4,5},{5,4},{6,7},{7,6},{8,9},{9,8},{10,11... | collective-permute-start | bytes 5505032 | tf_op jit(solution)/shard_map/ppermute | solution.py:312
  11.3 8.7 %all-to-all-start = ((s32[16,1,1]{2,1,0:T(1,128)}), s32[16,1,1]{2,1,0:T(1,128)S(1)}, u32[]{:S(2)}, u32[]{:S(2)}) async-start(s32[16,1,1]{2,1,0:T(1,128)} %broadcast_in_dim.17), calls=%async_computation | async-start | bytes 16384 | tf_op jit(solution)/shard_map/all_to_all | solution.py:296
  14.7 1.5 %copy-start = (bf16[1,1,1,64,14336]{4,3,2,1,0:T(8,128)(2,1)S(1)}, bf16[1,1,1,64,14336]{4,3,2,1,0:T(8,128)(2,1)}, u32[]{:S(2)}) copy-start(bf16[1,1,1,64,14336]{4,3,2,1,0:T(8,128)(2,1)} %param.4) | copy-start | bytes 5505028
  16.2 0.8 copy-start.1
  103.7 7.7 %collective-permute-start.1 = (bf16[4,8,112,128]{3,2,1,0:T(8,128)(2,1)S(1)}, bf16[4,8,112,128]{3,2,1,0:T(8,128)(2,1)S(1)}, u32[]{:S(2)}, u32[]{:S(2)}) collective-permute-start(bf16[4,8,112,128]{3,2,1,0:T(8,128)(2,1)S(1)} %all_to_all.31), channel_id=1, source_target_pairs={{0,1},{1,0},{2,3},{3,2},{4,5},{5,4},{6,7},{7,6},{8,9},{9,8},{10,11... | collective-permute-start | bytes 2752520 | tf_op jit(solution)/shard_map/ppermute | solution.py:330

commit v11 on v10

--- a/solution.py
+++ b/solution.py
@@ -39,8 +39,7 @@
 
 
 def rolled(v, by):
-    by %= LANES
-    return jnp.concatenate([v[:, LANES - by :], v[:, : LANES - by]], axis=1) if by else v
+    return pltpu.roll(v, by % LANES, 1)
 
 
 def folded(res, k):

time: 113 us -> 113 us (level)
  no operation moved by 1% of the time
where the time goes in v11:
time: 113 us
  blocking collectives  81.6 us (72%)
  starting transfers between devices  17.8 us (16%)
  Pallas kernels  4.7 us (4%)
  waiting for transfers between devices  3.71 us (3%)
  local copies, waits for them, and re-layouts  3.06 us (3%)
  between operations  1.98 us (2%)
    all_to_all x4, blocking collectives, swap(): return lax.all_to_all(pieces, axis, split_axis=0, concat_axis=0, tiled=True)  81.6 us
    ppermute x1, starting transfers between devices, shards(): other = lax.ppermute(fast, 'c', [(0, 1), (1, 0)])  8.79 us
    ppermute x1, starting transfers between devices, shards(): other = lax.ppermute(own, 'c', [(0, 1), (1, 0)])  5.62 us
    all_to_all x1, starting transfers between devices, swap(): return lax.all_to_all(pieces, axis, split_axis=0, concat_axis=0, tiled=True)  3.37 us
    all_to_all x1, waiting for transfers between devices, swap(): return lax.all_to_all(pieces, axis, split_axis=0, concat_axis=0, tiled=True)  2.65 us
    unnamed x4, local copies, waits for them, and re-layouts  2.33 us
  transfers between devices with their start and end apart: 3, of which 2 were waited for; matrix products, arithmetic and copies ran while one was open for 1% of the time, Pallas kernels for 1%

profile of v11, /device:TPU:1, one launch (start us, length us, event | category | flops | bytes accessed | tf_op | source)
XLA Modules:
  0.0 112.8 jit_solution(9334599214657837731)
XLA Ops:
  0.6 8.8 %collective-permute-start = (bf16[64,14336]{1,0:T(8,128)(2,1)}, bf16[64,14336]{1,0:T(8,128)(2,1)S(1)}, u32[]{:S(2)}, u32[]{:S(2)}) collective-permute-start(bf16[64,14336]{1,0:T(8,128)(2,1)} %bitcast.7), channel_id=1, source_target_pairs={{0,1},{1,0},{2,3},{3,2},{4,5},{5,4},{6,7},{7,6},{8,9},{9,8},{10,11... | collective-permute-start | bytes 5505032 | tf_op jit(solution)/shard_map/ppermute | solution.py:311
  10.7 0.6 broadcast_in_dim.17
  11.3 3.4 %all-to-all-start = ((s32[16,1,1]{2,1,0:T(1,128)}), s32[16,1,1]{2,1,0:T(1,128)S(1)}, u32[]{:S(2)}, u32[]{:S(2)}) async-start(s32[16,1,1]{2,1,0:T(1,128)} %broadcast_in_dim.17), calls=%async_computation | async-start | bytes 16384 | tf_op jit(solution)/shard_map/all_to_all | solution.py:295
  14.7 0.0 copy-start
  14.7 1.5 %copy-done = bf16[1,1,1,64,14336]{4,3,2,1,0:T(8,128)(2,1)S(1)} copy-done((bf16[1,1,1,64,14336]{4,3,2,1,0:T(8,128)(2,1)S(1)}, bf16[1,1,1,64,14336]{4,3,2,1,0:T(8,128)(2,1)}, u32[]{:S(2)}) %copy-start) | copy-done | bytes 1835032
  16.2 0.0 copy-start.1
  16.2 0.8 copy-done.1
  17.0 0.4 shard_map.59
  17.4 2.7 %all-to-all-done = s32[16,1,1]{2,1,0:T(1,128)S(1)} async-done(((s32[16,1,1]{2,1,0:T(1,128)}), s32[16,1,1]{2,1,0:T(1,128)S(1)}, u32[]{:S(2)}, u32[]{:S(2)}) %all-to-all-start) | async-done | bytes 96 | tf_op jit(solution)/shard_map/all_to_all | solution.py:295
  20.1 0.0 collective-permute-done.other
  20.1 1.4 %shard_map.60 = s16[4,912,128]{2,1,0:T(8,128)(2,1)S(1)} custom-call(s32[16,1]{1,0:T(8,128)S(1)} %bitcast.10, bf16[2,2,8,112,128]{4,3,2,1,0:T(8,128)(2,1)S(1)} %get-tuple-element.8.keep, bf16[64,14336]{1,0:T(8,128)(2,1)S(1)} %collective-permute-done.other), custom_call_target="tpu_custom_call" | custom-call | tf_op jit(solution)/shard_map/pallas_call | solution.py:315
  21.5 16.5 %all_to_all.28.got = s16[4,912,128]{2,1,0:T(8,128)(2,1)S(1)} all-to-all(s16[4,912,128]{2,1,0:T(8,128)(2,1)S(1)} %shard_map.60), channel_id=1, replica_groups=mesh['expert'=8,'x'=2,'zh'=8,'zl'=2,'c'=2] {'x','zl'}, dimensions={0} | all-to-all | bytes 1867776 | tf_op jit(solution)/shard_map/all_to_all | solution.py:295
  38.0 0.3 shard_map.61
  38.4 29.7 %all_to_all.29.refs_0_ = s16[8,120,128]{2,1,0:T(8,128)(2,1)S(1)} all-to-all(s16[8,120,128]{2,1,0:T(8,128)(2,1)S(1)} %shard_map.61), channel_id=1, replica_groups=mesh['expert'=8,'x'=2,'zh'=8,'zl'=2,'c'=2] {'zh'}, dimensions={0} | all-to-all | bytes 491520 | tf_op jit(solution)/shard_map/all_to_all | solution.py:295
  68.1 0.1 shard_map.62
  68.1 20.5 %all_to_all.30 = bf16[8,112,128]{2,1,0:T(8,128)(2,1)S(1)} all-to-all(bf16[8,112,128]{2,1,0:T(8,128)(2,1)S(1)} %get-tuple-element.11), channel_id=1, replica_groups=mesh['expert'=8,'x'=2,'zh'=8,'zl'=2,'c'=2] {'zh'}, dimensions={0} | all-to-all | bytes 458752 | tf_op jit(solution)/shard_map/all_to_all | solution.py:295
  88.7 0.1 broadcast_in_dim.18
  88.8 14.9 %all_to_all.31 = bf16[4,8,112,128]{3,2,1,0:T(8,128)(2,1)S(1)} all-to-all(bf16[4,8,112,128]{3,2,1,0:T(8,128)(2,1)S(1)} %broadcast_in_dim.18), channel_id=1, replica_groups=mesh['expert'=8,'x'=2,'zh'=8,'zl'=2,'c'=2] {'x','zl'}, dimensions={0} | all-to-all | bytes 1835008 | tf_op jit(solution)/shard_map/all_to_all | solution.py:295
  103.7 5.6 %collective-permute-start.1 = (bf16[4,8,112,128]{3,2,1,0:T(8,128)(2,1)S(1)}, bf16[4,8,112,128]{3,2,1,0:T(8,128)(2,1)S(1)}, u32[]{:S(2)}, u32[]{:S(2)}) collective-permute-start(bf16[4,8,112,128]{3,2,1,0:T(8,128)(2,1)S(1)} %all_to_all.31), channel_id=1, source_target_pairs={{0,1},{1,0},{2,3},{3,2},{4,5},{5,4},{6,7},{7,6},{8,9},{9,8},{10,11... | collective-permute-start | bytes 2752520 | tf_op jit(solution)/shard_map/ppermute | solution.py:329
  109.3 1.0 shard_map.63
  110.3 1.1 collective-permute-done.1
  111.4 1.4 %shard_map.64 = bf16[64,14336]{1,0:T(8,128)(2,1)} custom-call(bf16[64,14336]{1,0:T(8,128)(2,1)S(1)} %get-tuple-element.13.half, bf16[2,2,8,112,128]{4,3,2,1,0:T(8,128)(2,1)S(1)} %bitcast.9), custom_call_target="tpu_custom_call" | custom-call | tf_op jit(solution)/shard_map/pallas_call | solution.py:333
Async XLA Ops:
  0.6 19.4 %collective-permute-start = (bf16[64,14336]{1,0:T(8,128)(2,1)}, bf16[64,14336]{1,0:T(8,128)(2,1)S(1)}, u32[]{:S(2)}, u32[]{:S(2)}) collective-permute-start(bf16[64,14336]{1,0:T(8,128)(2,1)} %bitcast.7), channel_id=1, source_target_pairs={{0,1},{1,0},{2,3},{3,2},{4,5},{5,4},{6,7},{7,6},{8,9},{9,8},{10,11... | collective-permute-start | bytes 5505032 | tf_op jit(solution)/shard_map/ppermute | solution.py:311
  11.3 8.7 %all-to-all-start = ((s32[16,1,1]{2,1,0:T(1,128)}), s32[16,1,1]{2,1,0:T(1,128)S(1)}, u32[]{:S(2)}, u32[]{:S(2)}) async-start(s32[16,1,1]{2,1,0:T(1,128)} %broadcast_in_dim.17), calls=%async_computation | async-start | bytes 16384 | tf_op jit(solution)/shard_map/all_to_all | solution.py:295
  14.7 1.5 %copy-start = (bf16[1,1,1,64,14336]{4,3,2,1,0:T(8,128)(2,1)S(1)}, bf16[1,1,1,64,14336]{4,3,2,1,0:T(8,128)(2,1)}, u32[]{:S(2)}) copy-start(bf16[1,1,1,64,14336]{4,3,2,1,0:T(8,128)(2,1)} %param.4) | copy-start | bytes 5505028
  16.2 0.8 copy-start.1
  103.7 7.7 %collective-permute-start.1 = (bf16[4,8,112,128]{3,2,1,0:T(8,128)(2,1)S(1)}, bf16[4,8,112,128]{3,2,1,0:T(8,128)(2,1)S(1)}, u32[]{:S(2)}, u32[]{:S(2)}) collective-permute-start(bf16[4,8,112,128]{3,2,1,0:T(8,128)(2,1)S(1)} %all_to_all.31), channel_id=1, source_target_pairs={{0,1},{1,0},{2,3},{3,2},{4,5},{5,4},{6,7},{7,6},{8,9},{9,8},{10,11... | collective-permute-start | bytes 2752520 | tf_op jit(solution)/shard_map/ppermute | solution.py:329

commit v12 on v11

--- a/solution.py
+++ b/solution.py
@@ -31,6 +31,7 @@
 TOP = 32767.0
 DIGIT = 4096.0
 MIDDLE = 32768.0
+MARGIN = 0.01
 FINE = 8.0
 
 
@@ -106,8 +107,8 @@
 
 def coded(total):
     largest = jnp.maximum(jnp.max(jnp.abs(total), axis=0, keepdims=True), 1e-30)
-    level = jnp.ceil(FINE * jnp.log2(largest))
-    units = jnp.clip(jnp.round(total * (TOP * jnp.exp2(level * (-1 / FINE)))), -TOP, TOP)
+    level = jnp.ceil(FINE * jnp.log2(largest) + MARGIN)
+    units = jnp.round(total * (TOP * jnp.exp2(level * (-1 / FINE))))
     return short(units), level
 
 

time: 113 us -> 113 us (level)
  no operation moved by 1% of the time
where the time goes in v12:
time: 113 us
  blocking collectives  81.6 us (72%)
  starting transfers between devices  17.8 us (16%)
  Pallas kernels  4.63 us (4%)
  waiting for transfers between devices  3.71 us (3%)
  local copies, waits for them, and re-layouts  3.06 us (3%)
  between operations  1.98 us (2%)
    all_to_all x4, blocking collectives, swap(): return lax.all_to_all(pieces, axis, split_axis=0, concat_axis=0, tiled=True)  81.6 us
    ppermute x1, starting transfers between devices, shards(): other = lax.ppermute(fast, 'c', [(0, 1), (1, 0)])  8.79 us
    ppermute x1, starting transfers between devices, shards(): other = lax.ppermute(own, 'c', [(0, 1), (1, 0)])  5.64 us
    all_to_all x1, starting transfers between devices, swap(): return lax.all_to_all(pieces, axis, split_axis=0, concat_axis=0, tiled=True)  3.37 us
    all_to_all x1, waiting for transfers between devices, swap(): return lax.all_to_all(pieces, axis, split_axis=0, concat_axis=0, tiled=True)  2.65 us
    unnamed x4, local copies, waits for them, and re-layouts  2.33 us
  transfers between devices with their start and end apart: 3, of which 2 were waited for; matrix products, arithmetic and copies ran while one was open for 1% of the time, Pallas kernels for 1%

profile of v12, /device:TPU:1, one launch (start us, length us, event | category | flops | bytes accessed | tf_op | source)
XLA Modules:
  0.0 112.7 jit_solution(2297611632688968472)
XLA Ops:
  0.6 8.8 %collective-permute-start = (bf16[64,14336]{1,0:T(8,128)(2,1)}, bf16[64,14336]{1,0:T(8,128)(2,1)S(1)}, u32[]{:S(2)}, u32[]{:S(2)}) collective-permute-start(bf16[64,14336]{1,0:T(8,128)(2,1)} %bitcast.7), channel_id=1, source_target_pairs={{0,1},{1,0},{2,3},{3,2},{4,5},{5,4},{6,7},{7,6},{8,9},{9,8},{10,11... | collective-permute-start | bytes 5505032 | tf_op jit(solution)/shard_map/ppermute | solution.py:312
  10.7 0.6 broadcast_in_dim.17
  11.3 3.4 %all-to-all-start = ((s32[16,1,1]{2,1,0:T(1,128)}), s32[16,1,1]{2,1,0:T(1,128)S(1)}, u32[]{:S(2)}, u32[]{:S(2)}) async-start(s32[16,1,1]{2,1,0:T(1,128)} %broadcast_in_dim.17), calls=%async_computation | async-start | bytes 16384 | tf_op jit(solution)/shard_map/all_to_all | solution.py:296
  14.7 0.0 copy-start
  14.7 1.5 %copy-done = bf16[1,1,1,64,14336]{4,3,2,1,0:T(8,128)(2,1)S(1)} copy-done((bf16[1,1,1,64,14336]{4,3,2,1,0:T(8,128)(2,1)S(1)}, bf16[1,1,1,64,14336]{4,3,2,1,0:T(8,128)(2,1)}, u32[]{:S(2)}) %copy-start) | copy-done | bytes 1835032
  16.2 0.0 copy-start.1
  16.2 0.8 copy-done.1
  17.0 0.4 shard_map.59
  17.4 2.7 %all-to-all-done = s32[16,1,1]{2,1,0:T(1,128)S(1)} async-done(((s32[16,1,1]{2,1,0:T(1,128)}), s32[16,1,1]{2,1,0:T(1,128)S(1)}, u32[]{:S(2)}, u32[]{:S(2)}) %all-to-all-start) | async-done | bytes 96 | tf_op jit(solution)/shard_map/all_to_all | solution.py:296
  20.1 0.0 collective-permute-done.other
  20.1 1.4 %shard_map.60 = s16[4,912,128]{2,1,0:T(8,128)(2,1)S(1)} custom-call(s32[16,1]{1,0:T(8,128)S(1)} %bitcast.10, bf16[2,2,8,112,128]{4,3,2,1,0:T(8,128)(2,1)S(1)} %get-tuple-element.8.keep, bf16[64,14336]{1,0:T(8,128)(2,1)S(1)} %collective-permute-done.other), custom_call_target="tpu_custom_call" | custom-call | tf_op jit(solution)/shard_map/pallas_call | solution.py:316
  21.5 16.5 %all_to_all.28.got = s16[4,912,128]{2,1,0:T(8,128)(2,1)S(1)} all-to-all(s16[4,912,128]{2,1,0:T(8,128)(2,1)S(1)} %shard_map.60), channel_id=1, replica_groups=mesh['expert'=8,'x'=2,'zh'=8,'zl'=2,'c'=2] {'x','zl'}, dimensions={0} | all-to-all | bytes 1867776 | tf_op jit(solution)/shard_map/all_to_all | solution.py:296
  38.0 0.3 shard_map.61
  38.3 29.7 %all_to_all.29.refs_0_ = s16[8,120,128]{2,1,0:T(8,128)(2,1)S(1)} all-to-all(s16[8,120,128]{2,1,0:T(8,128)(2,1)S(1)} %shard_map.61), channel_id=1, replica_groups=mesh['expert'=8,'x'=2,'zh'=8,'zl'=2,'c'=2] {'zh'}, dimensions={0} | all-to-all | bytes 491520 | tf_op jit(solution)/shard_map/all_to_all | solution.py:296
  68.0 0.1 shard_map.62
  68.1 20.4 %all_to_all.30 = bf16[8,112,128]{2,1,0:T(8,128)(2,1)S(1)} all-to-all(bf16[8,112,128]{2,1,0:T(8,128)(2,1)S(1)} %get-tuple-element.11), channel_id=1, replica_groups=mesh['expert'=8,'x'=2,'zh'=8,'zl'=2,'c'=2] {'zh'}, dimensions={0} | all-to-all | bytes 458752 | tf_op jit(solution)/shard_map/all_to_all | solution.py:296
  88.5 0.1 broadcast_in_dim.18
  88.6 14.9 %all_to_all.31 = bf16[4,8,112,128]{3,2,1,0:T(8,128)(2,1)S(1)} all-to-all(bf16[4,8,112,128]{3,2,1,0:T(8,128)(2,1)S(1)} %broadcast_in_dim.18), channel_id=1, replica_groups=mesh['expert'=8,'x'=2,'zh'=8,'zl'=2,'c'=2] {'x','zl'}, dimensions={0} | all-to-all | bytes 1835008 | tf_op jit(solution)/shard_map/all_to_all | solution.py:296
  103.6 5.6 %collective-permute-start.1 = (bf16[4,8,112,128]{3,2,1,0:T(8,128)(2,1)S(1)}, bf16[4,8,112,128]{3,2,1,0:T(8,128)(2,1)S(1)}, u32[]{:S(2)}, u32[]{:S(2)}) collective-permute-start(bf16[4,8,112,128]{3,2,1,0:T(8,128)(2,1)S(1)} %all_to_all.31), channel_id=1, source_target_pairs={{0,1},{1,0},{2,3},{3,2},{4,5},{5,4},{6,7},{7,6},{8,9},{9,8},{10,11... | collective-permute-start | bytes 2752520 | tf_op jit(solution)/shard_map/ppermute | solution.py:330
  109.2 1.0 shard_map.63
  110.2 1.1 collective-permute-done.1
  111.3 1.4 %shard_map.64 = bf16[64,14336]{1,0:T(8,128)(2,1)} custom-call(bf16[64,14336]{1,0:T(8,128)(2,1)S(1)} %get-tuple-element.13.half, bf16[2,2,8,112,128]{4,3,2,1,0:T(8,128)(2,1)S(1)} %bitcast.9), custom_call_target="tpu_custom_call" | custom-call | tf_op jit(solution)/shard_map/pallas_call | solution.py:334
Async XLA Ops:
  0.6 19.4 %collective-permute-start = (bf16[64,14336]{1,0:T(8,128)(2,1)}, bf16[64,14336]{1,0:T(8,128)(2,1)S(1)}, u32[]{:S(2)}, u32[]{:S(2)}) collective-permute-start(bf16[64,14336]{1,0:T(8,128)(2,1)} %bitcast.7), channel_id=1, source_target_pairs={{0,1},{1,0},{2,3},{3,2},{4,5},{5,4},{6,7},{7,6},{8,9},{9,8},{10,11... | collective-permute-start | bytes 5505032 | tf_op jit(solution)/shard_map/ppermute | solution.py:312
  11.3 8.7 %all-to-all-start = ((s32[16,1,1]{2,1,0:T(1,128)}), s32[16,1,1]{2,1,0:T(1,128)S(1)}, u32[]{:S(2)}, u32[]{:S(2)}) async-start(s32[16,1,1]{2,1,0:T(1,128)} %broadcast_in_dim.17), calls=%async_computation | async-start | bytes 16384 | tf_op jit(solution)/shard_map/all_to_all | solution.py:296
  14.7 1.5 %copy-start = (bf16[1,1,1,64,14336]{4,3,2,1,0:T(8,128)(2,1)S(1)}, bf16[1,1,1,64,14336]{4,3,2,1,0:T(8,128)(2,1)}, u32[]{:S(2)}) copy-start(bf16[1,1,1,64,14336]{4,3,2,1,0:T(8,128)(2,1)} %param.4) | copy-start | bytes 5505028
  16.2 0.8 copy-start.1
  103.6 7.7 %collective-permute-start.1 = (bf16[4,8,112,128]{3,2,1,0:T(8,128)(2,1)S(1)}, bf16[4,8,112,128]{3,2,1,0:T(8,128)(2,1)S(1)}, u32[]{:S(2)}, u32[]{:S(2)}) collective-permute-start(bf16[4,8,112,128]{3,2,1,0:T(8,128)(2,1)S(1)} %all_to_all.31), channel_id=1, source_target_pairs={{0,1},{1,0},{2,3},{3,2},{4,5},{5,4},{6,7},{7,6},{8,9},{9,8},{10,11... | collective-permute-start | bytes 2752520 | tf_op jit(solution)/shard_map/ppermute | solution.py:330
